TPU v7x, 256 devices: a whole 4x4x8 slice. The times are simulated.
256 devices in a mesh: tm: 8 (over y, core), rows: 32 (over z, x).
Axes of the slice: x: 4, y: 4, z: 8, core: 2. Of those that a mesh axis runs over, the one named last changes fastest.
Arguments:
- features: bfloat16 [32, 64, 320, 128], P('tm', 'rows'), may hold values from -20 to 20
- gain_one: float32 [128], replicated, may hold values from 0.1 to 1.9
- shift_one: float32 [128], replicated, may hold values from -4 to 4
- weight_one: bfloat16 [3456, 128], replicated, may hold values from -0.109375 to 0.109375
- bias_one: float32 [128], replicated, may hold values from -6 to 6
- gain_two: float32 [128], replicated, may hold values from 0.1 to 1.9
- shift_two: float32 [128], replicated, may hold values from -4 to 4
- weight_two: bfloat16 [3456, 128], replicated, may hold values from -0.109375 to 0.109375
- bias_two: float32 [128], replicated, may hold values from -6 to 6
Outputs:
- block_out: bfloat16 [32, 64, 320, 128], P('tm', 'rows')
All inputs are finite; a program needn't handle non-finite values.
Results may differ from a plain program's by a relative error of at most 0.007.
Values may be sent and summed in bfloat16 or wider, within the bound.
No kernel may reach another device: no remote copies, remote signals or barrier semaphores. Data moves between devices by JAX's collectives and lax.ppermute only.
A program may use at most 64 MiB of HBM per device.

v0:
```python
import jax
import jax.numpy as jnp
from jax import lax
from jax.sharding import Mesh
from jax.sharding import PartitionSpec as P

C = 128
GROUPS = 32
ROWS = ("rows_0", "rows_1")
TM = ("tm_0", "tm_1")


EPS = 1e-06


def sent_to_all(array, axis):
    copies = jnp.broadcast_to(array, (lax.axis_size(axis), *array.shape))
    return lax.all_to_all(copies, axis, split_axis=0, concat_axis=0, tiled=True)


def over_copies(array, axis):
    return sent_to_all(array, axis).sum(axis=0)


def over_axes(array, axes):
    far, near = axes
    nearer = over_copies(array, near)
    return over_copies(nearer, far)


def packed_total(arrays, axis):
    ends = [0]
    for a in arrays:
        ends.append(ends[-1] + a.size)
    total = over_axes(jnp.concatenate([a.ravel() for a in arrays]), axis)
    return tuple((total[b:e].reshape(a.shape) for a, b, e in zip(arrays, ends, ends[1:])))


def extended_2(cells, sides, width):
    for axis, dim in sides:
        count = lax.axis_size(axis)
        ends = count - 1
        head = lax.slice_in_dim(cells, 0, width, axis=dim)
        tail = lax.slice_in_dim(cells, cells.shape[dim] - width, cells.shape[dim], axis=dim)
        cells = jnp.concatenate(
            [
                lax.ppermute(tail, axis, [(i, (i + 1) % count) for i in range(ends)]),
                cells,
                lax.ppermute(head, axis, [((i + 1) % count, i) for i in range(ends)]),
            ],
            axis=dim,
        )
    return cells


def shifted(block, axis, distance):
    devices = range(lax.axis_size(axis))
    route = [(i - distance, i) for i in devices if i - distance in devices]
    return lax.ppermute(block, axis, route)


def group_sums(values):
    per_channel = jnp.sum(values, axis=(0, 1, 2))
    return jnp.sum(per_channel.reshape(GROUPS, -1), axis=1)


def moments(values, cell_count):
    first_sum, square_sum = packed_total(
        (group_sums(values), group_sums(values * values)), ("tm_0", ("tm_1", "rows_0", "rows_1"))
    )
    average = first_sum / cell_count
    spread = square_sum / cell_count - average * average
    return (average, spread)


def activate(values, average, spread, gain, shift):
    center = jnp.repeat(average, C // GROUPS)
    factor = jnp.repeat(lax.rsqrt(spread + EPS), C // GROUPS)
    normed = (values - center) * factor * gain + shift
    return jax.nn.silu(normed).astype(jnp.bfloat16)


def border(values, depth, width):
    padded = extended_2(values, ((ROWS, 1),), width)
    carried = shifted(padded[padded.shape[0] - depth :], TM, 1)
    return jnp.concatenate([carried, padded], 0)


def repeat_first(extended, depth):
    first_span = lax.axis_index(TM) == 0
    leading = jnp.broadcast_to(extended[depth : depth + 1], extended[:depth].shape)
    replaced = jnp.concatenate([leading, extended[depth:]], 0)
    return jnp.where(first_span, replaced, extended)


def valid_conv(padded, weight, bias):
    out_frames = padded.shape[0] - 2
    out_rows = padded.shape[1] - 2
    width_cells = padded.shape[2]
    channels = padded.shape[3]
    widened = jnp.pad(padded, ((0, 0), (0, 0), (1, 1), (0, 0)))
    summed = jnp.zeros((out_frames, out_rows, width_cells, channels), jnp.float32)
    for time_tap in range(3):
        for row_tap in range(3):
            columns = jnp.concatenate(
                [
                    widened[
                        time_tap : time_tap + out_frames,
                        row_tap : row_tap + out_rows,
                        col_tap : col_tap + width_cells,
                    ]
                    for col_tap in range(3)
                ],
                -1,
            )
            first_row = (time_tap * 3 + row_tap) * 3 * channels
            taps_block = weight[first_row : first_row + 3 * channels]
            summed = summed + jnp.einsum(
                "frwk,kc->frwc", columns, taps_block, preferred_element_type=jnp.float32
            )
    return summed + bias


def body(
    features, gain_one, shift_one, weight_one, bias_one, gain_two, shift_two, weight_two, bias_two
):
    inputs = features.astype(jnp.float32)
    frames_dev, rows_dev, width_cells = (features.shape[0], features.shape[1], features.shape[2])
    cell_count = (
        frames_dev
        * rows_dev
        * width_cells
        * (C // GROUPS)
        * lax.axis_size(TM)
        * lax.axis_size(ROWS)
    )
    average, spread = moments(inputs, cell_count)
    activated = activate(inputs, average, spread, gain_one, shift_one)
    hidden = valid_conv(repeat_first(border(activated, 2, 1), 2), weight_one, bias_one).astype(
        jnp.bfloat16
    )
    hidden_wide = hidden.astype(jnp.float32)
    average_two, spread_two = moments(hidden_wide, cell_count)
    second = activate(hidden_wide, average_two, spread_two, gain_two, shift_two)
    second = repeat_first(border(second, 2, 1), 2)
    result = valid_conv(second, weight_two, bias_two) + inputs
    return result.astype(jnp.bfloat16)


def solution(mesh):
    split = Mesh(mesh.devices.reshape(4, 2, 8, 4), ("tm_0", "tm_1", "rows_0", "rows_1"))
    return jax.shard_map(
        body,
        mesh=split,
        in_specs=(P(TM, ROWS, None, None), P(), P(), P(), P(), P(), P(), P(), P()),
        out_specs=P(TM, ROWS, None, None),
        check_vma=False,
    )
```

profile of v0, /device:TPU:14, one launch (start us, length us, event | category | flops | bytes accessed | tf_op | source)
XLA Modules:
  0.0 136.0 jit_solution(17593626664098692561)
XLA Ops:
  0.0 1.4 %convert_reduce_fusion = (f32[128]{0:T(128)S(1)}, f32[128]{0:T(128)S(1)}) fusion(bf16[4,2,320,128]{3,2,1,0:T(8,128)(2,1)} %param.9), kind=kLoop, calls=%fused_computation.3 | loop fusion | flops 1310464 | bytes 656384 | tf_op jit(solution)/shard_map/reduce_sum | solution.py:63
  1.7 0.1 reduce_sum.109
  2.0 19.6 %all_to_all.24 = f32[64,1,64]{2,1,0:T(1,128)S(1)} all-to-all(f32[64,1,64]{2,1,0:T(1,128)S(1)} %broadcast_in_dim.44), channel_id=1, replica_groups=mesh['tm_0'=4,'tm_1'=2,'rows_0'=8,'rows_1'=4] {'tm_1','rows_0','rows_1'}, dimensions={0} | all-to-all | bytes 32768 | tf_op jit(solution)/shard_map/all_to_all | solution.py:18
  21.6 8.5 %all_to_all.25 = f32[4,1,64]{2,1,0:T(1,128)S(1)} all-to-all(f32[4,1,64]{2,1,0:T(1,128)S(1)} %broadcast_in_dim.45), channel_id=1, replica_groups=mesh['tm_0'=4,'tm_1'=2,'rows_0'=8,'rows_1'=4] {'tm_0'}, dimensions={0} | all-to-all | bytes 2048 | tf_op jit(solution)/shard_map/all_to_all | solution.py:18
  30.6 1.6 %fusion.189 = bf16[4,2,320,128]{3,2,1,0:T(8,128)(2,1)S(1)} fusion(bf16[4,2,320,128]{3,2,1,0:T(8,128)(2,1)} %param.9, f32[128]{0:T(128)} %param.11, f32[128]{0:T(128)} %param.10, f32[128]{0:T(128)S(1)} %mul.62, f32[128]{0:T(128)S(1)} %sub.26), kind=kLoop, calls=%fused_computation.158 | loop fusion | flops 3276800 | bytes 1312768 | tf_op jit(solution)/shard_map/convert_element_type | solution.py:80
  32.2 4.0 %collective-permute-start = (bf16[4,1,320,128]{3,2,1,0:T(8,128)(2,1)S(1)}, bf16[4,1,320,128]{3,2,1,0:T(8,128)(2,1)S(1)}, u32[]{:S(2)}, u32[]{:S(2)}) collective-permute-start(bf16[4,1,320,128]{3,2,1,0:T(8,128)(2,1)S(1)} %get-tuple-element.65), channel_id=1, source_target_pairs={{0,1},{1,2},{2,3},{3,4},{4,5},{5,6},{6,7},{7,8},{8,9},{9,10},{10,1... | collective-permute-start | bytes 983048 | tf_op jit(solution)/shard_map/ppermute | solution.py:47
  36.2 1.9 %collective-permute-start.1 = (bf16[4,1,320,128]{3,2,1,0:T(8,128)(2,1)S(1)}, bf16[4,1,320,128]{3,2,1,0:T(8,128)(2,1)S(1)}, u32[]{:S(2)}, u32[]{:S(2)}) collective-permute-start(bf16[4,1,320,128]{3,2,1,0:T(8,128)(2,1)S(1)} %get-tuple-element.66), channel_id=1, source_target_pairs={{1,0},{2,1},{3,2},{4,3},{5,4},{6,5},{7,6},{8,7},{9,8},{10,9},{11,1... | collective-permute-start | bytes 983048 | tf_op jit(solution)/shard_map/ppermute | solution.py:49
  38.1 4.2 %collective-permute-done = bf16[4,1,320,128]{3,2,1,0:T(8,128)(2,1)S(1)} collective-permute-done((bf16[4,1,320,128]{3,2,1,0:T(8,128)(2,1)S(1)}, bf16[4,1,320,128]{3,2,1,0:T(8,128)(2,1)S(1)}, u32[]{:S(2)}, u32[]{:S(2)}) %collective-permute-start) | collective-permute-done | bytes 327712 | tf_op jit(solution)/shard_map/ppermute | solution.py:47
  42.3 5.8 %collective-permute-done.1 = bf16[4,1,320,128]{3,2,1,0:T(8,128)(2,1)S(1)} collective-permute-done((bf16[4,1,320,128]{3,2,1,0:T(8,128)(2,1)S(1)}, bf16[4,1,320,128]{3,2,1,0:T(8,128)(2,1)S(1)}, u32[]{:S(2)}, u32[]{:S(2)}) %collective-permute-start.1) | collective-permute-done | bytes 327712 | tf_op jit(solution)/shard_map/ppermute | solution.py:49
  48.2 1.9 %collective-permute-start.2 = (bf16[2,4,320,128]{3,2,1,0:T(8,128)(2,1)S(1)}, bf16[2,4,320,128]{3,2,1,0:T(8,128)(2,1)S(1)}, u32[]{:S(2)}, u32[]{:S(2)}) collective-permute-start(bf16[2,4,320,128]{3,2,1,0:T(8,128)(2,1)S(1)} %pad_maximum_fusion.4), channel_id=1, source_target_pairs={{0,32},{32,64},{64,96},{96,128},{128,160},{160,192},{192,224},{1,3... | collective-permute-start | bytes 1966088 | tf_op jit(solution)/shard_map/ppermute | solution.py:59
  50.2 9.9 %collective-permute-done.2 = bf16[2,4,320,128]{3,2,1,0:T(8,128)(2,1)S(1)} collective-permute-done((bf16[2,4,320,128]{3,2,1,0:T(8,128)(2,1)S(1)}, bf16[2,4,320,128]{3,2,1,0:T(8,128)(2,1)S(1)}, u32[]{:S(2)}, u32[]{:S(2)}) %collective-permute-start.2) | collective-permute-done | bytes 655392 | tf_op jit(solution)/shard_map/ppermute | solution.py:59
  60.2 0.3 maximum_select_fusion
  60.5 1.0 fusion.247
  61.4 2.1 %fusion.246 = (bf16[4,2,320,128]{3,2,1,0:T(8,128)(2,1)S(1)}, bf16[4,2,320,128]{3,2,1,0:T(8,128)(2,1)S(1)}, bf16[4,2,320,128]{3,2,1,0:T(8,128)(2,1)S(1)}, bf16[4,...) fusion(bf16[6,4,320,128]{3,2,1,0:T(8,128)(2,1)S(1)} %maximum_se, ...), kind=kLoop, calls=%fused_computation.263 | loop fusion | bytes 9175040 | tf_op jit(solution)/shard_map/slice | solution.py:107
  63.5 1.9 %pad_slice_fusion.35 = (bf16[4,2,320,128]{3,2,1,0:T(8,128)(2,1)S(1)}, bf16[4,2,320,128]{3,2,1,0:T(8,128)(2,1)S(1)}, bf16[4,2,320,128]{3,2,1,0:T(8,128)(2,1)S(1)}...) fusion(bf16[6,4,320,128]{3,2,1,0:T(8,128)(2,1)S(1)} %maximum_se, ...), kind=kLoop, calls=%fused_computation.260 | loop fusion | bytes 9175040 | tf_op jit(solution)/shard_map/slice | solution.py:107
  65.5 0.7 fusion.30
  66.2 0.7 fusion.36
  66.8 0.7 fusion.42
  67.5 0.7 fusion.48
  68.2 0.7 fusion.24
  68.9 0.7 fusion.6
  69.5 0.7 fusion.12
  70.2 0.7 fusion.18
  71.0 1.1 convert_reduce_fusion.1
  72.1 0.1 reduce_sum.115
  72.6 14.0 %all_to_all.26 = f32[64,1,64]{2,1,0:T(1,128)S(1)} all-to-all(f32[64,1,64]{2,1,0:T(1,128)S(1)} %broadcast_in_dim.50), channel_id=1, replica_groups=mesh['tm_0'=4,'tm_1'=2,'rows_0'=8,'rows_1'=4] {'tm_1','rows_0','rows_1'}, dimensions={0} | all-to-all | bytes 32768 | tf_op jit(solution)/shard_map/all_to_all | solution.py:18
  86.6 7.5 %all_to_all.27 = f32[4,1,64]{2,1,0:T(1,128)S(1)} all-to-all(f32[4,1,64]{2,1,0:T(1,128)S(1)} %broadcast_in_dim.51), channel_id=1, replica_groups=mesh['tm_0'=4,'tm_1'=2,'rows_0'=8,'rows_1'=4] {'tm_0'}, dimensions={0} | all-to-all | bytes 2048 | tf_op jit(solution)/shard_map/all_to_all | solution.py:18
  94.6 0.5 fusion.179
  95.1 4.0 %collective-permute-start.3 = (bf16[4,1,320,128]{3,2,1,0:T(8,128)(2,1)S(1)}, bf16[4,1,320,128]{3,2,1,0:T(8,128)(2,1)S(1)}, u32[]{:S(2)}, u32[]{:S(2)}) collective-permute-start(bf16[4,1,320,128]{3,2,1,0:T(8,128)(2,1)S(1)} %get-tuple-element.63), channel_id=1, source_target_pairs={{0,1},{1,2},{2,3},{3,4},{4,5},{5,6},{6,7},{7,8},{8,9},{9,10},{10,1... | collective-permute-start | bytes 983048 | tf_op jit(solution)/shard_map/ppermute | solution.py:47
  99.1 1.9 %collective-permute-start.4 = (bf16[4,1,320,128]{3,2,1,0:T(8,128)(2,1)S(1)}, bf16[4,1,320,128]{3,2,1,0:T(8,128)(2,1)S(1)}, u32[]{:S(2)}, u32[]{:S(2)}) collective-permute-start(bf16[4,1,320,128]{3,2,1,0:T(8,128)(2,1)S(1)} %get-tuple-element.64), channel_id=1, source_target_pairs={{1,0},{2,1},{3,2},{4,3},{5,4},{6,5},{7,6},{8,7},{9,8},{10,9},{11,1... | collective-permute-start | bytes 983048 | tf_op jit(solution)/shard_map/ppermute | solution.py:49
  101.0 4.2 %collective-permute-done.3 = bf16[4,1,320,128]{3,2,1,0:T(8,128)(2,1)S(1)} collective-permute-done((bf16[4,1,320,128]{3,2,1,0:T(8,128)(2,1)S(1)}, bf16[4,1,320,128]{3,2,1,0:T(8,128)(2,1)S(1)}, u32[]{:S(2)}, u32[]{:S(2)}) %collective-permute-start.3) | collective-permute-done | bytes 327712 | tf_op jit(solution)/shard_map/ppermute | solution.py:47
  105.2 5.8 %collective-permute-done.4 = bf16[4,1,320,128]{3,2,1,0:T(8,128)(2,1)S(1)} collective-permute-done((bf16[4,1,320,128]{3,2,1,0:T(8,128)(2,1)S(1)}, bf16[4,1,320,128]{3,2,1,0:T(8,128)(2,1)S(1)}, u32[]{:S(2)}, u32[]{:S(2)}) %collective-permute-start.4) | collective-permute-done | bytes 327712 | tf_op jit(solution)/shard_map/ppermute | solution.py:49
  111.1 1.9 %collective-permute-start.5 = (bf16[2,4,320,128]{3,2,1,0:T(8,128)(2,1)S(1)}, bf16[2,4,320,128]{3,2,1,0:T(8,128)(2,1)S(1)}, u32[]{:S(2)}, u32[]{:S(2)}) collective-permute-start(bf16[2,4,320,128]{3,2,1,0:T(8,128)(2,1)S(1)} %pad_maximum_fusion.2), channel_id=1, source_target_pairs={{0,32},{32,64},{64,96},{96,128},{128,160},{160,192},{192,224},{1,3... | collective-permute-start | bytes 1966088 | tf_op jit(solution)/shard_map/ppermute | solution.py:59
  113.1 9.9 %collective-permute-done.5 = bf16[2,4,320,128]{3,2,1,0:T(8,128)(2,1)S(1)} collective-permute-done((bf16[2,4,320,128]{3,2,1,0:T(8,128)(2,1)S(1)}, bf16[2,4,320,128]{3,2,1,0:T(8,128)(2,1)S(1)}, u32[]{:S(2)}, u32[]{:S(2)}) %collective-permute-start.5) | collective-permute-done | bytes 655392 | tf_op jit(solution)/shard_map/ppermute | solution.py:59
  123.1 0.3 maximum_select_fusion.1
  123.4 1.0 fusion.245
  124.4 2.0 %fusion.244 = (bf16[4,2,320,128]{3,2,1,0:T(8,128)(2,1)S(1)}, bf16[4,2,320,128]{3,2,1,0:T(8,128)(2,1)S(1)}, bf16[4,2,320,128]{3,2,1,0:T(8,128)(2,1)S(1)}, bf16[4,...) fusion(bf16[6,4,320,128]{3,2,1,0:T(8,128)(2,1)S(1)} %maximum_se, ...), kind=kLoop, calls=%fused_computation.261 | loop fusion | bytes 9175040 | tf_op jit(solution)/shard_map/slice | solution.py:107
  126.4 1.9 %pad_slice_fusion.17 = (bf16[4,2,320,128]{3,2,1,0:T(8,128)(2,1)S(1)}, bf16[4,2,320,128]{3,2,1,0:T(8,128)(2,1)S(1)}, bf16[4,2,320,128]{3,2,1,0:T(8,128)(2,1)S(1)}...) fusion(bf16[6,4,320,128]{3,2,1,0:T(8,128)(2,1)S(1)} %maximum_se, ...), kind=kLoop, calls=%fused_computation.242 | loop fusion | bytes 9175040 | tf_op jit(solution)/shard_map/slice | solution.py:107
  128.3 0.7 fusion.84
  129.0 0.7 fusion.90
  129.7 0.7 fusion.96
  130.4 0.7 fusion.102
  131.1 0.7 fusion.78
  131.7 0.7 fusion.60
  132.4 0.7 fusion.66
  133.1 0.7 fusion.72
  133.8 0.4 copy-done
  134.2 1.8 %fusion.164 = bf16[4,2,320,128]{3,2,1,0:T(8,128)(2,1)} fusion(bf16[4,2,320,128]{3,2,1,0:T(8,128)(2,1)S(1)} %copy-done, f32[4,2,320,128]{3,2,1,0:T(8,128)S(1)} %fusion.102, f32[4,2,320,128]{3,2,1,0:T(8,128)S(1)} %fusion.96, f32[4,2,320,128]{3,2,1,0:T(8,128)S(1)} %fusion.90, f32[4,2,320,128]{3,2,1,0:T(8,128)S(1)} %fusion.84, ...), kind=kOutput, calls=%fused_computation.137 | convolution fusion | flops 261488640 | bytes 13861376 | tf_op jit(solution)/shard_map/frwk,kc->frwc/dot_general | solution.py:118
  (47 shorter events, 2.3 us)
Async XLA Ops:
  32.2 10.1 %collective-permute-start = (bf16[4,1,320,128]{3,2,1,0:T(8,128)(2,1)S(1)}, bf16[4,1,320,128]{3,2,1,0:T(8,128)(2,1)S(1)}, u32[]{:S(2)}, u32[]{:S(2)}) collective-permute-start(bf16[4,1,320,128]{3,2,1,0:T(8,128)(2,1)S(1)} %get-tuple-element.65), channel_id=1, source_target_pairs={{0,1},{1,2},{2,3},{3,4},{4,5},{5,6},{6,7},{7,8},{8,9},{9,10},{10,1... | collective-permute-start | bytes 983048 | tf_op jit(solution)/shard_map/ppermute | solution.py:47
  36.2 11.9 %collective-permute-start.1 = (bf16[4,1,320,128]{3,2,1,0:T(8,128)(2,1)S(1)}, bf16[4,1,320,128]{3,2,1,0:T(8,128)(2,1)S(1)}, u32[]{:S(2)}, u32[]{:S(2)}) collective-permute-start(bf16[4,1,320,128]{3,2,1,0:T(8,128)(2,1)S(1)} %get-tuple-element.66), channel_id=1, source_target_pairs={{1,0},{2,1},{3,2},{4,3},{5,4},{6,5},{7,6},{8,7},{9,8},{10,9},{11,1... | collective-permute-start | bytes 983048 | tf_op jit(solution)/shard_map/ppermute | solution.py:49
  48.2 11.9 %collective-permute-start.2 = (bf16[2,4,320,128]{3,2,1,0:T(8,128)(2,1)S(1)}, bf16[2,4,320,128]{3,2,1,0:T(8,128)(2,1)S(1)}, u32[]{:S(2)}, u32[]{:S(2)}) collective-permute-start(bf16[2,4,320,128]{3,2,1,0:T(8,128)(2,1)S(1)} %pad_maximum_fusion.4), channel_id=1, source_target_pairs={{0,32},{32,64},{64,96},{96,128},{128,160},{160,192},{192,224},{1,3... | collective-permute-start | bytes 1966088 | tf_op jit(solution)/shard_map/ppermute | solution.py:59
  63.5 1.9 %copy-start.1 = (bf16[3456,128]{1,0:T(8,128)(2,1)S(1)}, bf16[3456,128]{1,0:T(8,128)(2,1)}, u32[]{:S(2)}) copy-start(bf16[3456,128]{1,0:T(8,128)(2,1)} %param.12) | copy-start | bytes 2654212
  70.2 0.7 copy-start.3
  70.9 23.6 %copy-start.5 = (f32[128]{0:T(128)S(1)}, f32[128]{0:T(128)}, u32[]{:S(2)}) copy-start(f32[128]{0:T(128)} %param.15) | copy-start | bytes 1540
  71.0 23.6 %copy-start.6 = (f32[128]{0:T(128)S(1)}, f32[128]{0:T(128)}, u32[]{:S(2)}) copy-start(f32[128]{0:T(128)} %param.14) | copy-start | bytes 1540
  95.1 10.1 %collective-permute-start.3 = (bf16[4,1,320,128]{3,2,1,0:T(8,128)(2,1)S(1)}, bf16[4,1,320,128]{3,2,1,0:T(8,128)(2,1)S(1)}, u32[]{:S(2)}, u32[]{:S(2)}) collective-permute-start(bf16[4,1,320,128]{3,2,1,0:T(8,128)(2,1)S(1)} %get-tuple-element.63), channel_id=1, source_target_pairs={{0,1},{1,2},{2,3},{3,4},{4,5},{5,6},{6,7},{7,8},{8,9},{9,10},{10,1... | collective-permute-start | bytes 983048 | tf_op jit(solution)/shard_map/ppermute | solution.py:47
  99.1 11.9 %collective-permute-start.4 = (bf16[4,1,320,128]{3,2,1,0:T(8,128)(2,1)S(1)}, bf16[4,1,320,128]{3,2,1,0:T(8,128)(2,1)S(1)}, u32[]{:S(2)}, u32[]{:S(2)}) collective-permute-start(bf16[4,1,320,128]{3,2,1,0:T(8,128)(2,1)S(1)} %get-tuple-element.64), channel_id=1, source_target_pairs={{1,0},{2,1},{3,2},{4,3},{5,4},{6,5},{7,6},{8,7},{9,8},{10,9},{11,1... | collective-permute-start | bytes 983048 | tf_op jit(solution)/shard_map/ppermute | solution.py:49
  111.1 11.9 %collective-permute-start.5 = (bf16[2,4,320,128]{3,2,1,0:T(8,128)(2,1)S(1)}, bf16[2,4,320,128]{3,2,1,0:T(8,128)(2,1)S(1)}, u32[]{:S(2)}, u32[]{:S(2)}) collective-permute-start(bf16[2,4,320,128]{3,2,1,0:T(8,128)(2,1)S(1)} %pad_maximum_fusion.2), channel_id=1, source_target_pairs={{0,32},{32,64},{64,96},{96,128},{128,160},{160,192},{192,224},{1,3... | collective-permute-start | bytes 1966088 | tf_op jit(solution)/shard_map/ppermute | solution.py:59
  126.4 1.9 %copy-start.2 = (bf16[3456,128]{1,0:T(8,128)(2,1)S(1)}, bf16[3456,128]{1,0:T(8,128)(2,1)}, u32[]{:S(2)}) copy-start(bf16[3456,128]{1,0:T(8,128)(2,1)} %param.16) | copy-start | bytes 2654212
  133.1 1.1 copy-start
  133.1 1.1 copy-start.4
where the time goes:
time: 136 us
  blocking collectives  49.6 us (36%)
  waiting for transfers between devices  39.9 us (29%)
  starting transfers between devices  15.6 us (11%)
  matrix products  13.7 us (10%)
  local copies, waits for them, and re-layouts  11.7 us (9%)
  other arithmetic  5.14 us (4%)
    all_to_all x4, blocking collectives, sent_to_all(): return lax.all_to_all(copies, axis, split_axis=0, concat_axis=0, tiled=True)  49.6 us
    ppermute x2, waiting for transfers between devices, shifted(): return lax.ppermute(block, axis, route)  19.8 us
    dot_general x18, matrix products, valid_conv(): jnp.einsum('frwk,kc->frwc', columns, taps_block, preferred_element_type=j...  13.7 us
    ppermute x2, waiting for transfers between devices, extended_2(): lax.ppermute(head, axis, [((i + 1) % count, i) for i in range(ends)])  11.6 us
    slice x6, local copies, waits for them, and re-layouts, valid_conv(): widened[time_tap:time_tap + out_frames, row_tap:row_tap + out_rows, col_t...  9.84 us
    ppermute x2, waiting for transfers between devices, extended_2(): lax.ppermute(tail, axis, [(i, (i + 1) % count) for i in range(ends)])  8.37 us
    ppermute x2, starting transfers between devices, extended_2(): lax.ppermute(tail, axis, [(i, (i + 1) % count) for i in range(ends)])  7.91 us
    ppermute x2, starting transfers between devices, extended_2(): lax.ppermute(head, axis, [((i + 1) % count, i) for i in range(ends)])  3.84 us
  transfers between devices with their start and end apart: 6, of which 6 were waited for; matrix products, arithmetic and copies ran while one was open for 0% of the time, Pallas kernels for 0%

commit v1 on v0

v1 whole, which is shorter than its diff:
```python
import jax
import jax.numpy as jnp
from jax import lax
from jax.sharding import Mesh
from jax.sharding import PartitionSpec as P

C = 128
GROUPS = 32
TM = ("y", "c")
ROWS = ("z", "x")
FAR = ("y", "z", "x")
EPS = 1e-06


def total_over_mesh(array):
    swapped = lax.ppermute(array, "c", [(0, 1), (1, 0)])
    pair = array + swapped
    count = lax.axis_size(FAR)
    copies = jnp.broadcast_to(pair, (count, *pair.shape))
    return lax.all_to_all(copies, FAR, split_axis=0, concat_axis=0, tiled=True).sum(axis=0)


def moments(values, cell_count):
    per_channel = jnp.stack([jnp.sum(values, axis=(0, 1, 2)), jnp.sum(values * values, axis=(0, 1, 2))])
    total = total_over_mesh(per_channel)
    first_sum, square_sum = jnp.sum(total.reshape(2, GROUPS, -1), axis=2)
    average = first_sum / cell_count
    spread = square_sum / cell_count - average * average
    return average, spread


def activate(values, average, spread, gain, shift):
    center = jnp.repeat(average, C // GROUPS)
    factor = jnp.repeat(lax.rsqrt(spread + EPS), C // GROUPS)
    normed = (values.astype(jnp.float32) - center) * factor * gain + shift
    return jax.nn.silu(normed).astype(jnp.bfloat16)


def sent(block, tm_step, row_step):
    tms, rows = lax.axis_size(TM), lax.axis_size(ROWS)
    route = []
    for t in range(tms):
        for r in range(rows):
            if 0 <= t + tm_step < tms and 0 <= r + row_step < rows:
                route.append((t * rows + r, (t + tm_step) * rows + r + row_step))
    return lax.ppermute(block, TM + ROWS, route)


def extended(block):
    top, bottom = block[:, :1], block[:, -1:]
    above = sent(bottom, 0, 1)
    below = sent(top, 0, -1)
    back = sent(block[-2:], 1, 0)
    back_above = sent(bottom[-2:], 1, 1)
    back_below = sent(top[-2:], 1, -1)
    now = jnp.concatenate([above, block, below], 1)
    before = jnp.concatenate([back_above, back, back_below], 1)
    repeated = jnp.broadcast_to(now[:1], before.shape)
    before = jnp.where(lax.axis_index(TM) == 0, repeated, before)
    return jnp.concatenate([before, now], 0)


def zero_outside(block):
    row = lax.axis_index(ROWS)
    index = lax.broadcasted_iota(jnp.int32, block.shape, 1)
    first = jnp.where(row == 0, 1, 0)
    last = jnp.where(row == lax.axis_size(ROWS) - 1, block.shape[1] - 1, block.shape[1])
    return jnp.where((index >= first) & (index < last), block, jnp.zeros_like(block))


def valid_conv(padded, weight, bias):
    out_frames, out_rows = padded.shape[0] - 2, padded.shape[1] - 2
    width_cells, channels = padded.shape[2], padded.shape[3]
    widened = jnp.pad(padded, ((0, 0), (0, 0), (1, 1), (0, 0)))
    summed = jnp.zeros((out_frames, out_rows, width_cells, channels), jnp.float32)
    for time_tap in range(3):
        for row_tap in range(3):
            columns = jnp.concatenate(
                [
                    widened[
                        time_tap : time_tap + out_frames,
                        row_tap : row_tap + out_rows,
                        col_tap : col_tap + width_cells,
                    ]
                    for col_tap in range(3)
                ],
                -1,
            )
            first_row = (time_tap * 3 + row_tap) * 3 * channels
            taps_block = weight[first_row : first_row + 3 * channels]
            summed = summed + jnp.einsum(
                "frwk,kc->frwc", columns, taps_block, preferred_element_type=jnp.float32
            )
    return summed + bias


def body(features, gain_one, shift_one, weight_one, bias_one, gain_two, shift_two, weight_two, bias_two):
    inputs = features.astype(jnp.float32)
    cell_count = (
        features.shape[0] * features.shape[1] * features.shape[2] * (C // GROUPS)
        * lax.axis_size(TM) * lax.axis_size(ROWS)
    )
    wide = extended(features)
    average, spread = moments(inputs, cell_count)
    activated = zero_outside(activate(wide, average, spread, gain_one, shift_one))
    hidden = valid_conv(activated, weight_one, bias_one).astype(jnp.bfloat16)
    hidden_wide = extended(hidden)
    average_two, spread_two = moments(hidden.astype(jnp.float32), cell_count)
    second = zero_outside(activate(hidden_wide, average_two, spread_two, gain_two, shift_two))
    result = valid_conv(second, weight_two, bias_two) + inputs
    return result.astype(jnp.bfloat16)


def solution(mesh):
    split = Mesh(mesh.devices.reshape(4, 2, 8, 4), ("y", "c", "z", "x"))
    return jax.shard_map(
        body,
        mesh=split,
        in_specs=(P(TM, ROWS, None, None), P(), P(), P(), P(), P(), P(), P(), P()),
        out_specs=P(TM, ROWS, None, None),
        check_vma=False,
    )
```

time: 136 us -> 123 us (0.904)
  the two profiles are of different devices: /device:TPU:14 before, /device:TPU:111 now
where the time goes in v1:
time: 123 us; the launch traced here: 122 us
  starting transfers between devices  68.6 us (56%)
  waiting for transfers between devices  17.4 us (14%)
  local copies, waits for them, and re-layouts  15.6 us (13%)
  matrix products  13.7 us (11%)
  other arithmetic  6.48 us (5%)
    ppermute x10, starting transfers between devices, sent(): return lax.ppermute(block, TM + ROWS, route)  39.1 us
    all_to_all x2, starting transfers between devices, total_over_mesh(): lax.all_to_all(copies, FAR, split_axis=0, concat_axis=0, tiled=True)  26.5 us
    ppermute x10, waiting for transfers between devices, sent(): return lax.ppermute(block, TM + ROWS, route)  16.6 us
    dot_general x18, matrix products, valid_conv(): jnp.einsum('frwk,kc->frwc', columns, taps_block, preferred_element_type=j...  13.7 us
    slice x6, local copies, waits for them, and re-layouts, valid_conv(): widened[time_tap:time_tap + out_frames, row_tap:row_tap + out_rows, col_t...  9.93 us
    select_n x2, other arithmetic, zero_outside(): jnp.where((index >= first) & (index < last), block, jnp.zeros_like(block))  3.19 us
    ppermute x2, starting transfers between devices, total_over_mesh(): swapped = lax.ppermute(array, 'c', [(0, 1), (1, 0)])  3.03 us
  transfers between devices with their start and end apart: 14, of which 4 were waited for; matrix products, arithmetic and copies ran while one was open for 4% of the time, Pallas kernels for 0%

profile of v1, /device:TPU:111, one launch (start us, length us, event | category | flops | bytes accessed | tf_op | source)
XLA Modules:
  0.0 122.4 jit_solution(3557862835485475348)
XLA Ops:
  0.0 1.5 %convert_reduce_fusion = (f32[128]{0:T(128)S(1)}, f32[128]{0:T(128)S(1)}) fusion(bf16[4,2,320,128]{3,2,1,0:T(8,128)(2,1)} %param.9), kind=kLoop, calls=%fused_computation.114 | loop fusion | flops 1310464 | bytes 656384 | tf_op jit(solution)/shard_map/reduce_sum | solution.py:24
  1.5 0.8 collective-permute-start.5
  2.3 1.0 fusion.241
  3.3 5.6 %collective-permute-start.2 = (bf16[2,1,320,128]{3,2,1,0:T(8,128)(2,1)S(1)}, bf16[2,1,320,128]{3,2,1,0:T(8,128)(2,1)S(1)}, u32[]{:S(2)}, u32[]{:S(2)}) collective-permute-start(bf16[2,1,320,128]{3,2,1,0:T(8,128)(2,1)S(1)} %get-tuple-element.67), channel_id=1, source_target_pairs={{0,33},{1,34},{2,35},{3,36},{4,37},{5,38},{6,39},{7,40},{8,41},{9,... | collective-permute-start | bytes 491528 | tf_op jit(solution)/shard_map/ppermute | solution.py:46
  8.9 1.9 %collective-permute-start.4 = (bf16[2,1,320,128]{3,2,1,0:T(8,128)(2,1)S(1)}, bf16[2,1,320,128]{3,2,1,0:T(8,128)(2,1)S(1)}, u32[]{:S(2)}, u32[]{:S(2)}) collective-permute-start(bf16[2,1,320,128]{3,2,1,0:T(8,128)(2,1)S(1)} %get-tuple-element.68), channel_id=1, source_target_pairs={{1,32},{2,33},{3,34},{4,35},{5,36},{6,37},{7,38},{8,39},{9,40},{10... | collective-permute-start | bytes 491528 | tf_op jit(solution)/shard_map/ppermute | solution.py:46
  10.8 1.0 slice.278
  11.8 2.6 %collective-permute-start.3 = (bf16[2,2,320,128]{3,2,1,0:T(8,128)(2,1)S(1)}, bf16[2,2,320,128]{3,2,1,0:T(8,128)(2,1)S(1)}, u32[]{:S(2)}, u32[]{:S(2)}) collective-permute-start(bf16[2,2,320,128]{3,2,1,0:T(8,128)(2,1)S(1)} %slice.278), channel_id=1, source_target_pairs={{0,32},{1,33},{2,34},{3,35},{4,36},{5,37},{6,38},{7,39},{8,40},{9,... | collective-permute-start | bytes 983048 | tf_op jit(solution)/shard_map/ppermute | solution.py:46
  14.4 0.7 broadcast_in_dim.40
  15.1 12.5 %all-to-all-start = ((f32[128,2,128]{2,1,0:T(2,128)}), f32[128,2,128]{2,1,0:T(2,128)S(1)}, u32[]{:S(2)}, u32[]{:S(2)}) async-start(f32[128,2,128]{2,1,0:T(2,128)} %broadcast_in_dim.40), calls=%async_computation | async-start | bytes 262144 | tf_op jit(solution)/shard_map/all_to_all | solution.py:20
  27.7 2.5 %collective-permute-start.1 = (bf16[4,1,320,128]{3,2,1,0:T(8,128)(2,1)S(1)}, bf16[4,1,320,128]{3,2,1,0:T(8,128)(2,1)S(1)}, u32[]{:S(2)}, u32[]{:S(2)}) collective-permute-start(bf16[4,1,320,128]{3,2,1,0:T(8,128)(2,1)S(1)} %get-tuple-element.69), channel_id=1, source_target_pairs={{1,0},{2,1},{3,2},{4,3},{5,4},{6,5},{7,6},{8,7},{9,8},{10,9},{11,1... | collective-permute-start | bytes 983048 | tf_op jit(solution)/shard_map/ppermute | solution.py:46
  30.2 6.3 %collective-permute-start = (bf16[4,1,320,128]{3,2,1,0:T(8,128)(2,1)S(1)}, bf16[4,1,320,128]{3,2,1,0:T(8,128)(2,1)S(1)}, u32[]{:S(2)}, u32[]{:S(2)}) collective-permute-start(bf16[4,1,320,128]{3,2,1,0:T(8,128)(2,1)S(1)} %get-tuple-element.70), channel_id=1, source_target_pairs={{0,1},{1,2},{2,3},{3,4},{4,5},{5,6},{6,7},{7,8},{8,9},{9,10},{10,1... | collective-permute-start | bytes 983048 | tf_op jit(solution)/shard_map/ppermute | solution.py:46
  37.3 4.8 %collective-permute-done = bf16[4,1,320,128]{3,2,1,0:T(8,128)(2,1)S(1)} collective-permute-done((bf16[4,1,320,128]{3,2,1,0:T(8,128)(2,1)S(1)}, bf16[4,1,320,128]{3,2,1,0:T(8,128)(2,1)S(1)}, u32[]{:S(2)}, u32[]{:S(2)}) %collective-permute-start) | collective-permute-done | bytes 327712 | tf_op jit(solution)/shard_map/ppermute | solution.py:46
  42.7 1.6 %fusion = bf16[6,4,320,128]{3,2,1,0:T(8,128)(2,1)S(1)} fusion(bf16[4,4,320,128]{3,2,1,0:T(8,128)(2,1)S(1)} %constant_dynamic-update-slice_fusion, bf16[2,4,320,128]{3,2,1,0:T(8,128)(2,1)S(1)} %maximum_select_fusion, f32[128]{0:T(128)S(1)} %copy-done.5, f32[128]{0:T(128)S(1)} %copy-done.6, f32[128]{0:T(128)S(1)} %mul.67, f32[128]{0:T(128)S(1)} %sub.26, ...), kind=kLoop, calls=%fused_computation.2 | loop fusion | flops 11796480 | bytes 3934212 | tf_op jit(solution)/shard_map/jit(_where)/select_n | solution.py:68
  44.3 1.0 fusion.238
  45.3 2.1 %fusion.237 = (bf16[4,2,320,128]{3,2,1,0:T(8,128)(2,1)S(1)}, bf16[4,2,320,128]{3,2,1,0:T(8,128)(2,1)S(1)}, bf16[4,2,320,128]{3,2,1,0:T(8,128)(2,1)S(1)}, bf16[4,...) fusion(bf16[6,4,320,128]{3,2,1,0:T(8,128)(2,1)S(1)} %fusion), kind=kLoop, calls=%fused_computation.253 | loop fusion | bytes 9175040 | tf_op jit(solution)/shard_map/slice | solution.py:80
  47.4 1.9 %pad_slice_fusion.35 = (bf16[4,2,320,128]{3,2,1,0:T(8,128)(2,1)S(1)}, bf16[4,2,320,128]{3,2,1,0:T(8,128)(2,1)S(1)}, bf16[4,2,320,128]{3,2,1,0:T(8,128)(2,1)S(1)}...) fusion(bf16[6,4,320,128]{3,2,1,0:T(8,128)(2,1)S(1)} %fusion), kind=kLoop, calls=%fused_computation.250 | loop fusion | bytes 9175040 | tf_op jit(solution)/shard_map/slice | solution.py:80
  49.3 0.7 fusion.32
  50.0 0.7 fusion.38
  51.4 0.7 fusion.50
  52.1 0.7 fusion.26
  52.8 0.7 fusion.8
  53.4 0.7 fusion.14
  54.1 0.7 fusion.20
  54.8 1.1 convert_reduce_fusion.1
  55.9 2.3 %collective-permute-start.11 = (f32[2,128]{1,0:T(2,128)S(1)}, f32[2,128]{1,0:T(2,128)S(1)}, u32[]{:S(2)}, u32[]{:S(2)}) collective-permute-start(f32[2,128]{1,0:T(2,128)S(1)} %pad_maximum_fusion.3), channel_id=1, source_target_pairs={{0,32},{32,0},{1,33},{33,1},{2,34},{34,2},{3,35},{35,3},{4,36},{36... | collective-permute-start | bytes 3080 | tf_op jit(solution)/shard_map/ppermute | solution.py:16
  58.2 0.8 collective-permute-done.11
  59.0 0.7 broadcast_in_dim.45
  59.7 13.9 %all-to-all-start.1 = ((f32[128,2,128]{2,1,0:T(2,128)}), f32[128,2,128]{2,1,0:T(2,128)S(1)}, u32[]{:S(2)}, u32[]{:S(2)}) async-start(f32[128,2,128]{2,1,0:T(2,128)} %broadcast_in_dim.45), calls=%async_computation.1 | async-start | bytes 262144 | tf_op jit(solution)/shard_map/all_to_all | solution.py:20
  73.6 0.7 fusion.239
  74.4 6.2 %collective-permute-start.8 = (bf16[2,1,320,128]{3,2,1,0:T(8,128)(2,1)}, bf16[2,1,320,128]{3,2,1,0:T(8,128)(2,1)}, u32[]{:S(2)}, u32[]{:S(2)}) collective-permute-start(bf16[2,1,320,128]{3,2,1,0:T(8,128)(2,1)} %get-tuple-element.63), channel_id=1, source_target_pairs={{0,33},{1,34},{2,35},{3,36},{4,37},{5,38},{6,39},{7,40},{8,41},{9,... | collective-permute-start | bytes 491528 | tf_op jit(solution)/shard_map/ppermute | solution.py:46
  80.6 1.9 %collective-permute-start.10 = (bf16[2,1,320,128]{3,2,1,0:T(8,128)(2,1)}, bf16[2,1,320,128]{3,2,1,0:T(8,128)(2,1)}, u32[]{:S(2)}, u32[]{:S(2)}) collective-permute-start(bf16[2,1,320,128]{3,2,1,0:T(8,128)(2,1)} %get-tuple-element.64), channel_id=1, source_target_pairs={{1,32},{2,33},{3,34},{4,35},{5,36},{6,37},{7,38},{8,39},{9,40},{10... | collective-permute-start | bytes 491528 | tf_op jit(solution)/shard_map/ppermute | solution.py:46
  82.6 2.6 %collective-permute-start.9 = (bf16[2,2,320,128]{3,2,1,0:T(8,128)(2,1)S(1)}, bf16[2,2,320,128]{3,2,1,0:T(8,128)(2,1)S(1)}, u32[]{:S(2)}, u32[]{:S(2)}) collective-permute-start(bf16[2,2,320,128]{3,2,1,0:T(8,128)(2,1)S(1)} %slice.371), channel_id=1, source_target_pairs={{0,32},{1,33},{2,34},{3,35},{4,36},{5,37},{6,38},{7,39},{8,40},{9,... | collective-permute-start | bytes 983048 | tf_op jit(solution)/shard_map/ppermute | solution.py:46
  85.2 7.6 %collective-permute-start.6 = (bf16[4,1,320,128]{3,2,1,0:T(8,128)(2,1)S(1)}, bf16[4,1,320,128]{3,2,1,0:T(8,128)(2,1)S(1)}, u32[]{:S(2)}, u32[]{:S(2)}) collective-permute-start(bf16[4,1,320,128]{3,2,1,0:T(8,128)(2,1)S(1)} %get-tuple-element.65), channel_id=1, source_target_pairs={{0,1},{1,2},{2,3},{3,4},{4,5},{5,6},{6,7},{7,8},{8,9},{9,10},{10,1... | collective-permute-start | bytes 983048 | tf_op jit(solution)/shard_map/ppermute | solution.py:46
  92.9 1.9 %collective-permute-start.7 = (bf16[4,1,320,128]{3,2,1,0:T(8,128)(2,1)S(1)}, bf16[4,1,320,128]{3,2,1,0:T(8,128)(2,1)S(1)}, u32[]{:S(2)}, u32[]{:S(2)}) collective-permute-start(bf16[4,1,320,128]{3,2,1,0:T(8,128)(2,1)S(1)} %get-tuple-element.66), channel_id=1, source_target_pairs={{1,0},{2,1},{3,2},{4,3},{5,4},{6,5},{7,6},{8,7},{9,8},{10,9},{11,1... | collective-permute-start | bytes 983048 | tf_op jit(solution)/shard_map/ppermute | solution.py:46
  95.5 4.3 %collective-permute-done.6 = bf16[4,1,320,128]{3,2,1,0:T(8,128)(2,1)S(1)} collective-permute-done((bf16[4,1,320,128]{3,2,1,0:T(8,128)(2,1)S(1)}, bf16[4,1,320,128]{3,2,1,0:T(8,128)(2,1)S(1)}, u32[]{:S(2)}, u32[]{:S(2)}) %collective-permute-start.6) | collective-permute-done | bytes 327712 | tf_op jit(solution)/shard_map/ppermute | solution.py:46
  99.8 7.5 %collective-permute-done.7 = bf16[4,1,320,128]{3,2,1,0:T(8,128)(2,1)S(1)} collective-permute-done((bf16[4,1,320,128]{3,2,1,0:T(8,128)(2,1)S(1)}, bf16[4,1,320,128]{3,2,1,0:T(8,128)(2,1)S(1)}, u32[]{:S(2)}, u32[]{:S(2)}) %collective-permute-start.7) | collective-permute-done | bytes 327712 | tf_op jit(solution)/shard_map/ppermute | solution.py:46
  107.4 1.1 maximum_select_fusion.1
  108.5 1.6 %fusion.1 = bf16[6,4,320,128]{3,2,1,0:T(8,128)(2,1)S(1)} fusion(bf16[4,1,320,128]{3,2,1,0:T(8,128)(2,1)S(1)} %collective-permute-done.7, bf16[4,2,320,128]{3,2,1,0:T(8,128)(2,1)S(1)} %get-tuple-element.71, bf16[4,1,320,128]{3,2,1,0:T(8,128)(2,1)S(1)} %collective-permute-done.6, bf16[2,4,320,128]{3,2,1,0:T(8,128)(2,1)S(1)} %maximum_select_fusion.1, ...), kind=kLoop, calls=%fused_computation.3 | loop fusion | flops 13762560 | bytes 3934212 | tf_op jit(solution)/shard_map/jit(_where)/select_n | solution.py:68
  110.1 1.0 fusion.236
  111.1 2.1 %fusion.235 = (bf16[4,2,320,128]{3,2,1,0:T(8,128)(2,1)S(1)}, bf16[4,2,320,128]{3,2,1,0:T(8,128)(2,1)S(1)}, bf16[4,2,320,128]{3,2,1,0:T(8,128)(2,1)S(1)}, bf16[4,...) fusion(bf16[6,4,320,128]{3,2,1,0:T(8,128)(2,1)S(1)} %fusion.1), kind=kLoop, calls=%fused_computation.251 | loop fusion | bytes 9175040 | tf_op jit(solution)/shard_map/slice | solution.py:80
  113.2 1.9 %pad_slice_fusion.17 = (bf16[4,2,320,128]{3,2,1,0:T(8,128)(2,1)S(1)}, bf16[4,2,320,128]{3,2,1,0:T(8,128)(2,1)S(1)}, bf16[4,2,320,128]{3,2,1,0:T(8,128)(2,1)S(1)}...) fusion(bf16[6,4,320,128]{3,2,1,0:T(8,128)(2,1)S(1)} %fusion.1), kind=kLoop, calls=%fused_computation.232 | loop fusion | bytes 9175040 | tf_op jit(solution)/shard_map/slice | solution.py:80
  115.1 0.7 fusion.86
  116.5 0.7 fusion.98
  117.2 0.7 fusion.104
  117.9 0.7 fusion.80
  119.2 0.7 fusion.68
  119.9 0.7 fusion.74
  120.6 1.8 %fusion.166 = bf16[4,2,320,128]{3,2,1,0:T(8,128)(2,1)} fusion(bf16[4,2,320,128]{3,2,1,0:T(8,128)(2,1)S(1)} %copy-done, f32[4,2,320,128]{3,2,1,0:T(8,128)S(1)} %fusion.104, f32[4,2,320,128]{3,2,1,0:T(8,128)S(1)} %fusion.98, f32[4,2,320,128]{3,2,1,0:T(8,128)S(1)} %fusion.92, f32[4,2,320,128]{3,2,1,0:T(8,128)S(1)} %fusion.86, ...), kind=kOutput, calls=%fused_computation.135 | convolution fusion | flops 261488640 | bytes 13861376 | tf_op jit(solution)/shard_map/frwk,kc->frwc/dot_general | solution.py:91
  (63 shorter events, 4.3 us)
Async XLA Ops:
  0.0 27.7 %copy-start = (bf16[4,2,320,128]{3,2,1,0:T(8,128)(2,1)S(1)}, bf16[4,2,320,128]{3,2,1,0:T(8,128)(2,1)}, u32[]{:S(2)}) copy-start(bf16[4,2,320,128]{3,2,1,0:T(8,128)(2,1)} %param.9) | copy-start | bytes 1966084
  1.5 12.9 %collective-permute-start.5 = (f32[2,128]{1,0:T(2,128)S(1)}, f32[2,128]{1,0:T(2,128)S(1)}, u32[]{:S(2)}, u32[]{:S(2)}) collective-permute-start(f32[2,128]{1,0:T(2,128)S(1)} %pad_maximum_fusion.2), channel_id=1, source_target_pairs={{0,32},{32,0},{1,33},{33,1},{2,34},{34,2},{3,35},{35,3},{4,36},{36... | collective-permute-start | bytes 3080 | tf_op jit(solution)/shard_map/ppermute | solution.py:16
  3.3 39.0 %collective-permute-start.2 = (bf16[2,1,320,128]{3,2,1,0:T(8,128)(2,1)S(1)}, bf16[2,1,320,128]{3,2,1,0:T(8,128)(2,1)S(1)}, u32[]{:S(2)}, u32[]{:S(2)}) collective-permute-start(bf16[2,1,320,128]{3,2,1,0:T(8,128)(2,1)S(1)} %get-tuple-element.67), channel_id=1, source_target_pairs={{0,33},{1,34},{2,35},{3,36},{4,37},{5,38},{6,39},{7,40},{8,41},{9,... | collective-permute-start | bytes 491528 | tf_op jit(solution)/shard_map/ppermute | solution.py:46
  8.9 33.4 %collective-permute-start.4 = (bf16[2,1,320,128]{3,2,1,0:T(8,128)(2,1)S(1)}, bf16[2,1,320,128]{3,2,1,0:T(8,128)(2,1)S(1)}, u32[]{:S(2)}, u32[]{:S(2)}) collective-permute-start(bf16[2,1,320,128]{3,2,1,0:T(8,128)(2,1)S(1)} %get-tuple-element.68), channel_id=1, source_target_pairs={{1,32},{2,33},{3,34},{4,35},{5,36},{6,37},{7,38},{8,39},{9,40},{10... | collective-permute-start | bytes 491528 | tf_op jit(solution)/shard_map/ppermute | solution.py:46
  11.8 30.5 %collective-permute-start.3 = (bf16[2,2,320,128]{3,2,1,0:T(8,128)(2,1)S(1)}, bf16[2,2,320,128]{3,2,1,0:T(8,128)(2,1)S(1)}, u32[]{:S(2)}, u32[]{:S(2)}) collective-permute-start(bf16[2,2,320,128]{3,2,1,0:T(8,128)(2,1)S(1)} %slice.278), channel_id=1, source_target_pairs={{0,32},{1,33},{2,34},{3,35},{4,36},{5,37},{6,38},{7,39},{8,40},{9,... | collective-permute-start | bytes 983048 | tf_op jit(solution)/shard_map/ppermute | solution.py:46
  15.1 21.4 %all-to-all-start = ((f32[128,2,128]{2,1,0:T(2,128)}), f32[128,2,128]{2,1,0:T(2,128)S(1)}, u32[]{:S(2)}, u32[]{:S(2)}) async-start(f32[128,2,128]{2,1,0:T(2,128)} %broadcast_in_dim.40), calls=%async_computation | async-start | bytes 262144 | tf_op jit(solution)/shard_map/all_to_all | solution.py:20
  27.7 14.5 %collective-permute-start.1 = (bf16[4,1,320,128]{3,2,1,0:T(8,128)(2,1)S(1)}, bf16[4,1,320,128]{3,2,1,0:T(8,128)(2,1)S(1)}, u32[]{:S(2)}, u32[]{:S(2)}) collective-permute-start(bf16[4,1,320,128]{3,2,1,0:T(8,128)(2,1)S(1)} %get-tuple-element.69), channel_id=1, source_target_pairs={{1,0},{2,1},{3,2},{4,3},{5,4},{6,5},{7,6},{8,7},{9,8},{10,9},{11,1... | collective-permute-start | bytes 983048 | tf_op jit(solution)/shard_map/ppermute | solution.py:46
  30.2 11.8 %collective-permute-start = (bf16[4,1,320,128]{3,2,1,0:T(8,128)(2,1)S(1)}, bf16[4,1,320,128]{3,2,1,0:T(8,128)(2,1)S(1)}, u32[]{:S(2)}, u32[]{:S(2)}) collective-permute-start(bf16[4,1,320,128]{3,2,1,0:T(8,128)(2,1)S(1)} %get-tuple-element.70), channel_id=1, source_target_pairs={{0,1},{1,2},{2,3},{3,4},{4,5},{5,6},{6,7},{7,8},{8,9},{9,10},{10,1... | collective-permute-start | bytes 983048 | tf_op jit(solution)/shard_map/ppermute | solution.py:46
  42.1 0.7 copy-start.5
  42.1 0.7 copy-start.6
  47.4 1.9 %copy-start.1 = (bf16[3456,128]{1,0:T(8,128)(2,1)S(1)}, bf16[3456,128]{1,0:T(8,128)(2,1)}, u32[]{:S(2)}) copy-start(bf16[3456,128]{1,0:T(8,128)(2,1)} %param.12) | copy-start | bytes 2654212
  54.1 0.7 copy-start.3
  55.9 3.1 %collective-permute-start.11 = (f32[2,128]{1,0:T(2,128)S(1)}, f32[2,128]{1,0:T(2,128)S(1)}, u32[]{:S(2)}, u32[]{:S(2)}) collective-permute-start(f32[2,128]{1,0:T(2,128)S(1)} %pad_maximum_fusion.3), channel_id=1, source_target_pairs={{0,32},{32,0},{1,33},{33,1},{2,34},{34,2},{3,35},{35,3},{4,36},{36... | collective-permute-start | bytes 3080 | tf_op jit(solution)/shard_map/ppermute | solution.py:16
  59.7 35.1 %all-to-all-start.1 = ((f32[128,2,128]{2,1,0:T(2,128)}), f32[128,2,128]{2,1,0:T(2,128)S(1)}, u32[]{:S(2)}, u32[]{:S(2)}) async-start(f32[128,2,128]{2,1,0:T(2,128)} %broadcast_in_dim.45), calls=%async_computation.1 | async-start | bytes 262144 | tf_op jit(solution)/shard_map/all_to_all | solution.py:20
  74.4 33.0 %collective-permute-start.8 = (bf16[2,1,320,128]{3,2,1,0:T(8,128)(2,1)}, bf16[2,1,320,128]{3,2,1,0:T(8,128)(2,1)}, u32[]{:S(2)}, u32[]{:S(2)}) collective-permute-start(bf16[2,1,320,128]{3,2,1,0:T(8,128)(2,1)} %get-tuple-element.63), channel_id=1, source_target_pairs={{0,33},{1,34},{2,35},{3,36},{4,37},{5,38},{6,39},{7,40},{8,41},{9,... | collective-permute-start | bytes 491528 | tf_op jit(solution)/shard_map/ppermute | solution.py:46
  80.6 26.7 %collective-permute-start.10 = (bf16[2,1,320,128]{3,2,1,0:T(8,128)(2,1)}, bf16[2,1,320,128]{3,2,1,0:T(8,128)(2,1)}, u32[]{:S(2)}, u32[]{:S(2)}) collective-permute-start(bf16[2,1,320,128]{3,2,1,0:T(8,128)(2,1)} %get-tuple-element.64), channel_id=1, source_target_pairs={{1,32},{2,33},{3,34},{4,35},{5,36},{6,37},{7,38},{8,39},{9,40},{10... | collective-permute-start | bytes 491528 | tf_op jit(solution)/shard_map/ppermute | solution.py:46
  82.6 24.8 %collective-permute-start.9 = (bf16[2,2,320,128]{3,2,1,0:T(8,128)(2,1)S(1)}, bf16[2,2,320,128]{3,2,1,0:T(8,128)(2,1)S(1)}, u32[]{:S(2)}, u32[]{:S(2)}) collective-permute-start(bf16[2,2,320,128]{3,2,1,0:T(8,128)(2,1)S(1)} %slice.371), channel_id=1, source_target_pairs={{0,32},{1,33},{2,34},{3,35},{4,36},{5,37},{6,38},{7,39},{8,40},{9,... | collective-permute-start | bytes 983048 | tf_op jit(solution)/shard_map/ppermute | solution.py:46
  85.2 23.3 %copy-start.7 = (f32[128]{0:T(128)S(1)}, f32[128]{0:T(128)}, u32[]{:S(2)}) copy-start(f32[128]{0:T(128)} %param.15) | copy-start | bytes 1540
  85.2 23.3 %copy-start.8 = (f32[128]{0:T(128)S(1)}, f32[128]{0:T(128)}, u32[]{:S(2)}) copy-start(f32[128]{0:T(128)} %param.14) | copy-start | bytes 1540
  85.2 14.6 %collective-permute-start.6 = (bf16[4,1,320,128]{3,2,1,0:T(8,128)(2,1)S(1)}, bf16[4,1,320,128]{3,2,1,0:T(8,128)(2,1)S(1)}, u32[]{:S(2)}, u32[]{:S(2)}) collective-permute-start(bf16[4,1,320,128]{3,2,1,0:T(8,128)(2,1)S(1)} %get-tuple-element.65), channel_id=1, source_target_pairs={{0,1},{1,2},{2,3},{3,4},{4,5},{5,6},{6,7},{7,8},{8,9},{9,10},{10,1... | collective-permute-start | bytes 983048 | tf_op jit(solution)/shard_map/ppermute | solution.py:46
  92.9 14.5 %collective-permute-start.7 = (bf16[4,1,320,128]{3,2,1,0:T(8,128)(2,1)S(1)}, bf16[4,1,320,128]{3,2,1,0:T(8,128)(2,1)S(1)}, u32[]{:S(2)}, u32[]{:S(2)}) collective-permute-start(bf16[4,1,320,128]{3,2,1,0:T(8,128)(2,1)S(1)} %get-tuple-element.66), channel_id=1, source_target_pairs={{1,0},{2,1},{3,2},{4,3},{5,4},{6,5},{7,6},{8,7},{9,8},{10,9},{11,1... | collective-permute-start | bytes 983048 | tf_op jit(solution)/shard_map/ppermute | solution.py:46
  113.2 1.9 %copy-start.2 = (bf16[3456,128]{1,0:T(8,128)(2,1)S(1)}, bf16[3456,128]{1,0:T(8,128)(2,1)}, u32[]{:S(2)}) copy-start(bf16[3456,128]{1,0:T(8,128)(2,1)} %param.16) | copy-start | bytes 2654212
  119.9 0.7 copy-start.4

commit v2 on v1

v2 whole, which is shorter than its diff:
```python
import jax
import jax.numpy as jnp
from jax import lax
from jax.experimental import pallas as pl
from jax.experimental.pallas import tpu as pltpu
from jax.sharding import Mesh
from jax.sharding import PartitionSpec as P

C = 128
GROUP = 4
TM = ("y", "c")
ROWS = ("z", "x")
EVERY = TM + ROWS
EPS = 1e-06
MIB = 1 << 20
VMEM = pl.BlockSpec(memory_space=pltpu.VMEM)
SMEM = pl.BlockSpec(memory_space=pltpu.SMEM)


def group_total(v):
    lane = lax.broadcasted_iota(jnp.int32, v.shape, v.ndim - 1)
    for step in (1, 2):
        ahead = pltpu.roll(v, C - step, v.ndim - 1)
        behind = pltpu.roll(v, step, v.ndim - 1)
        v = v + jnp.where((lane & step) == 0, ahead, behind)
    return v


def local_sums(ref, frames, rows, width):
    cells = frames * rows * width

    def over(step):
        total = jnp.zeros((8, C), jnp.float32)
        for f in range(frames):
            for r in range(rows):
                part = step(ref[f, r].astype(jnp.float32))
                total = total + part.reshape(width // 8, 8, C).sum(axis=0)
        return jnp.sum(total, axis=0, keepdims=True)

    first = over(lambda v: v)
    mean = first / cells
    centered = over(lambda v: (v - mean) * (v - mean))
    return first, centered


def scale_and_offset(sums_ref, gain_ref, shift_ref, cells):
    devices = sums_ref.shape[0]
    every = sums_ref[:, 0, :]
    squares = jnp.sum(sums_ref[:, 1, :], axis=0, keepdims=True)
    whole = cells * devices * GROUP
    average = group_total(jnp.broadcast_to(jnp.sum(every, axis=0, keepdims=True), (8, C)))[:1] / whole
    apart = every / cells - average
    squares = squares + cells * jnp.sum(apart * apart, axis=0, keepdims=True)
    spread = group_total(jnp.broadcast_to(squares, (8, C)))[:1] / whole
    scale = lax.rsqrt(spread + EPS) * gain_ref[...]
    offset = shift_ref[...] - average * scale
    return 0.5 * scale, 0.5 * offset


def activated(values, scale, offset):
    half = values.astype(jnp.float32) * scale + offset
    return (half + half * jnp.tanh(half)).astype(jnp.bfloat16)


def fill(act_ref, own, back, above_ref, below_ref, flags_ref, scale, offset):
    back_frames = 2
    frames, rows, width = act_ref.shape[0], act_ref.shape[1], act_ref.shape[2]
    for f in range(frames):
        act_ref[f, 0] = activated(above_ref[f, 0], scale, offset)
        act_ref[f, rows - 1] = activated(below_ref[f, 0], scale, offset)
        for r in range(1, rows - 1):
            source = back(f, r - 1) if f < back_frames else own(f - back_frames, r - 1)
            act_ref[f, r] = activated(source, scale, offset)

    @pl.when(flags_ref[1] == 1)
    def _():
        act_ref[:, 0] = jnp.zeros((frames, width, C), jnp.bfloat16)

    @pl.when(flags_ref[2] == 1)
    def _():
        act_ref[:, rows - 1] = jnp.zeros((frames, width, C), jnp.bfloat16)

    @pl.when(flags_ref[0] == 1)
    def _():
        act_ref[0] = act_ref[back_frames]
        act_ref[1] = act_ref[back_frames]


def taps(act_ref, w_ref, start, count):
    width = act_ref.shape[2]
    cells = count * width
    pieces = [
        act_ref[start + i : start + i + count, r].reshape(cells, C) for i in range(3) for r in range(4)
    ]
    left = jnp.concatenate(pieces, axis=1)
    column = lax.broadcasted_iota(jnp.int32, (cells, 2 * C), 0) % width

    def block(i, j, k):
        if not 0 <= j < 3:
            return jnp.zeros((C, C), jnp.bfloat16)
        first = ((i * 3 + j) * 3 + k) * C
        return w_ref[first : first + C, :]

    total = None
    for k in (1, 0, 2):
        right = jnp.concatenate(
            [
                jnp.concatenate([block(i, r, k), block(i, r - 1, k)], axis=1)
                for i in range(3)
                for r in range(4)
            ],
            axis=0,
        )
        part = jnp.dot(left, right, preferred_element_type=jnp.float32)
        if k == 0:
            part = jnp.where(column == 0, 0.0, pltpu.roll(part, 1, 0))
        if k == 2:
            part = jnp.where(column == width - 1, 0.0, pltpu.roll(part, cells - 1, 0))
        total = part if total is None else total + part
    return total


def stats_kernel(x_ref, sums_ref):
    frames, rows, width, _ = x_ref.shape
    first, centered = local_sums(x_ref, frames, rows, width)
    pair = jnp.concatenate([first, centered], axis=0)
    sums_ref[...] = jnp.broadcast_to(pair[None], sums_ref.shape)


def first_conv_kernel(
    flags_ref, own_ref, back_ref, above_ref, below_ref, sums_ref, gain_ref, shift_ref, w_ref, bias_ref,
    hidden_ref, next_ref, act_ref,
):
    frames, rows, width, _ = own_ref.shape
    scale, offset = scale_and_offset(sums_ref, gain_ref, shift_ref, frames * rows * width)
    fill(
        act_ref, lambda f, r: own_ref[f, r], lambda f, r: back_ref[f, r], above_ref, below_ref,
        flags_ref, scale, offset,
    )
    for f in range(frames):
        total = taps(act_ref, w_ref, f, 1)
        for r in range(rows):
            value = total[:, r * C : (r + 1) * C] + bias_ref[...]
            hidden_ref[f, r] = value.astype(jnp.bfloat16)
    first, centered = local_sums(hidden_ref, frames, rows, width)
    pair = jnp.concatenate([first, centered], axis=0)
    next_ref[...] = jnp.broadcast_to(pair[None], next_ref.shape)


def second_conv_kernel(
    flags_ref, own_ref, back_ref, above_ref, below_ref, sums_ref, gain_ref, shift_ref, w_ref, bias_ref,
    features_ref, out_ref, act_ref,
):
    frames, rows, width, _ = own_ref.shape
    scale, offset = scale_and_offset(sums_ref, gain_ref, shift_ref, frames * rows * width)
    fill(
        act_ref, lambda f, r: own_ref[f, r], lambda f, r: back_ref[f, r], above_ref, below_ref,
        flags_ref, scale, offset,
    )
    for f in range(frames):
        total = taps(act_ref, w_ref, f, 1)
        for r in range(rows):
            value = total[:, r * C : (r + 1) * C] + bias_ref[...]
            value = value + features_ref[f, r].astype(jnp.float32)
            out_ref[f, r] = value.astype(jnp.bfloat16)


def edge_kernel(own_ref, back_ref, top_ref, bottom_ref):
    rows = own_ref.shape[1]
    top_ref[:2, 0] = back_ref[:, 0]
    top_ref[2:, 0] = own_ref[:, 0]
    bottom_ref[:2, 0] = back_ref[:, rows - 1]
    bottom_ref[2:, 0] = own_ref[:, rows - 1]


def shifted(block, axes, step):
    count = lax.axis_size(axes)
    return lax.ppermute(block, axes, [(i, i + step) for i in range(count) if 0 <= i + step < count])


def edges(own, back):
    frames, _, width, _ = own.shape
    shape = jax.ShapeDtypeStruct((frames + 2, 1, width, C), own.dtype)
    top, bottom = pl.pallas_call(
        edge_kernel, out_shape=(shape, shape), in_specs=[VMEM] * 2, out_specs=(VMEM, VMEM), name="edge_rows",
        compiler_params=pltpu.CompilerParams(vmem_limit_bytes=8 * MIB),
    )(own, back)
    above = shifted(bottom, ROWS, 1)
    below = shifted(top, ROWS, -1)
    return above, below


def everywhere(copies):
    return lax.all_to_all(copies, EVERY, split_axis=0, concat_axis=0, tiled=True)


def body(features, gain_one, shift_one, weight_one, bias_one, gain_two, shift_two, weight_two, bias_two):
    frames, rows, width, _ = features.shape
    devices = lax.axis_size(EVERY)
    copies = jax.ShapeDtypeStruct((devices, 2, C), jnp.float32)
    row = lax.axis_index(ROWS)
    flags = jnp.stack(
        [lax.axis_index(TM) == 0, row == 0, row == lax.axis_size(ROWS) - 1]
    ).astype(jnp.int32)
    scratch = [pltpu.VMEM((frames + 2, rows + 2, width, C), jnp.bfloat16)]
    specs = [SMEM] + [VMEM] * 9
    vectors = [v.reshape(1, C) for v in (gain_one, shift_one, bias_one, gain_two, shift_two, bias_two)]

    back = shifted(features[-2:], TM, 1)
    sums = pl.pallas_call(
        stats_kernel, out_shape=copies, in_specs=[VMEM], out_specs=VMEM, name="moments",
        compiler_params=pltpu.CompilerParams(vmem_limit_bytes=8 * MIB),
    )(features)
    above, below = edges(features, back)
    sums = everywhere(sums)
    hidden, sums_two = pl.pallas_call(
        first_conv_kernel,
        out_shape=(jax.ShapeDtypeStruct(features.shape, jnp.bfloat16), copies),
        in_specs=specs,
        out_specs=(VMEM, VMEM),
        scratch_shapes=scratch,
        compiler_params=pltpu.CompilerParams(vmem_limit_bytes=32 * MIB),
        name="first_conv",
    )(flags, features, back, above, below, sums, vectors[0], vectors[1], weight_one, vectors[2])

    back = shifted(hidden[-2:], TM, 1)
    above, below = edges(hidden, back)
    sums_two = everywhere(sums_two)
    return pl.pallas_call(
        second_conv_kernel,
        out_shape=jax.ShapeDtypeStruct(features.shape, jnp.bfloat16),
        in_specs=specs + [VMEM],
        out_specs=VMEM,
        scratch_shapes=scratch,
        compiler_params=pltpu.CompilerParams(vmem_limit_bytes=32 * MIB),
        name="second_conv",
    )(flags, hidden, back, above, below, sums_two, vectors[3], vectors[4], weight_two, vectors[5], features)


def solution(mesh):
    split = Mesh(mesh.devices.reshape(4, 2, 8, 4), EVERY)
    return jax.shard_map(
        body,
        mesh=split,
        in_specs=(P(TM, ROWS, None, None), P(), P(), P(), P(), P(), P(), P(), P()),
        out_specs=P(TM, ROWS, None, None),
        check_vma=False,
    )
```

time: 123 us -> 98.2 us (0.80)
  the two profiles are of different devices: /device:TPU:111 before, /device:TPU:102 now
where the time goes in v2:
time: 98.2 us; the launch traced here: 97.7 us
  starting transfers between devices  44.3 us (45%)
  waiting for transfers between devices  33 us (34%)
  Pallas kernels  16 us (16%)
  local copies, waits for them, and re-layouts  4.27 us (4%)
    all_to_all x2, starting transfers between devices, everywhere(): lax.all_to_all(copies, EVERY, split_axis=0, concat_axis=0, tiled=True)  27.7 us
    ppermute x6, waiting for transfers between devices, shifted(): lax.ppermute(block, axes, [(i, i + step) for i in range(count) if 0 <= i...  25.6 us
    ppermute x6, starting transfers between devices, shifted(): lax.ppermute(block, axes, [(i, i + step) for i in range(count) if 0 <= i...  16.6 us
    all_to_all x2, waiting for transfers between devices, everywhere(): lax.all_to_all(copies, EVERY, split_axis=0, concat_axis=0, tiled=True)  7.32 us
    pallas_call x1, Pallas kernels, body(): pl.pallas_call(second_conv_kernel, out_shape=jax.ShapeDtypeStruct(feature...  6.65 us
    pallas_call x1, Pallas kernels, body(): pl.pallas_call(first_conv_kernel, out_shape=(jax.ShapeDtypeStruct(feature...  6.25 us
    unnamed x22, local copies, waits for them, and re-layouts  3.18 us
    pallas_call x2, Pallas kernels, edges(): pl.pallas_call(edge_kernel, out_shape=(shape, shape), in_specs=[VMEM] * 2...  2.03 us
  transfers between devices with their start and end apart: 8, of which 6 were waited for; matrix products, arithmetic and copies ran while one was open for 0% of the time, Pallas kernels for 3%

profile of v2, /device:TPU:102, one launch (start us, length us, event | category | flops | bytes accessed | tf_op | source)
XLA Modules:
  0.0 97.7 jit_solution(9986183968600361526)
XLA Ops:
  0.0 0.0 copy-start
  0.0 1.1 %slice.6 = bf16[2,2,320,128]{3,2,1,0:T(8,128)(2,1)S(1)} slice(bf16[4,2,320,128]{3,2,1,0:T(8,128)(2,1)} %features_ref.1), slice={[2:4], [0:2], [0:320], [0:128]} | slice | bytes 655360 | tf_op jit(solution)/shard_map/slice | solution.py:209
  1.1 1.8 %collective-permute-start = (bf16[2,2,320,128]{3,2,1,0:T(8,128)(2,1)S(1)}, bf16[2,2,320,128]{3,2,1,0:T(8,128)(2,1)S(1)}, u32[]{:S(2)}, u32[]{:S(2)}) collective-permute-start(bf16[2,2,320,128]{3,2,1,0:T(8,128)(2,1)S(1)} %slice.6), channel_id=1, source_target_pairs={{0,32},{32,64},{64,96},{96,128},{128,160},{160,192},{192,224},{1,3... | collective-permute-start | bytes 983048 | tf_op jit(solution)/shard_map/ppermute | solution.py:178
  2.8 0.0 copy-done
  2.8 1.1 %moments.1 = f32[256,2,128]{2,1,0:T(2,128)} custom-call(bf16[4,2,320,128]{3,2,1,0:T(8,128)(2,1)S(1)} %copy-done), custom_call_target="tpu_custom_call" | custom-call | tf_op jit(solution)/shard_map/moments/pallas_call | solution.py:210
  3.9 0.0 copy-start.1
  3.9 15.1 %all-to-all-start = ((f32[256,2,128]{2,1,0:T(2,128)}), f32[256,2,128]{2,1,0:T(2,128)S(1)}, u32[]{:S(2)}, u32[]{:S(2)}) async-start(f32[256,2,128]{2,1,0:T(2,128)} %moments.1), calls=%async_computation | async-start | bytes 524288 | tf_op jit(solution)/shard_map/all_to_all | solution.py:194
  19.1 0.0 collective-permute-done.back_ref
  19.1 1.0 %edge_rows.2 = (bf16[6,1,320,128]{3,2,1,0:T(8,128)(2,1)}, bf16[6,1,320,128]{3,2,1,0:T(8,128)(2,1)}) custom-call(bf16[4,2,320,128]{3,2,1,0:T(8,128)(2,1)S(1)} %copy-done, bf16[2,2,320,128]{3,2,1,0:T(8,128)(2,1)S(1)} %collective-permute-done.back_ref), custom_call_target="tpu_custom_call" | custom-call | tf_op jit(solution)/shard_map/edge_rows/pallas_call | solution.py:184
  20.1 4.8 %collective-permute-start.1 = (bf16[6,1,320,128]{3,2,1,0:T(8,128)(2,1)}, bf16[6,1,320,128]{3,2,1,0:T(8,128)(2,1)S(1)}, u32[]{:S(2)}, u32[]{:S(2)}) collective-permute-start(bf16[6,1,320,128]{3,2,1,0:T(8,128)(2,1)} %get-tuple-element.11), channel_id=1, source_target_pairs={{0,1},{1,2},{2,3},{3,4},{4,5},{5,6},{6,7},{7,8},{8,9},{9,10},{10,1... | collective-permute-start | bytes 1474568 | tf_op jit(solution)/shard_map/ppermute | solution.py:178
  24.9 1.9 %collective-permute-start.2 = (bf16[6,1,320,128]{3,2,1,0:T(8,128)(2,1)}, bf16[6,1,320,128]{3,2,1,0:T(8,128)(2,1)S(1)}, u32[]{:S(2)}, u32[]{:S(2)}) collective-permute-start(bf16[6,1,320,128]{3,2,1,0:T(8,128)(2,1)} %get-tuple-element.12), channel_id=1, source_target_pairs={{1,0},{2,1},{3,2},{4,3},{5,4},{6,5},{7,6},{8,7},{9,8},{10,9},{11,1... | collective-permute-start | bytes 1474568 | tf_op jit(solution)/shard_map/ppermute | solution.py:178
  26.8 0.1 add_convert_fusion.flags_ref
  26.9 3.6 %all-to-all-done.sums_ref = f32[256,2,128]{2,1,0:T(2,128)S(1)} async-done(((f32[256,2,128]{2,1,0:T(2,128)}), f32[256,2,128]{2,1,0:T(2,128)S(1)}, u32[]{:S(2)}, u32[]{:S(2)}) %all-to-all-start) | async-done | bytes 262176 | tf_op jit(solution)/shard_map/all_to_all | solution.py:194
  30.5 5.5 %collective-permute-done.1.above_ref = bf16[6,1,320,128]{3,2,1,0:T(8,128)(2,1)S(1)} collective-permute-done((bf16[6,1,320,128]{3,2,1,0:T(8,128)(2,1)}, bf16[6,1,320,128]{3,2,1,0:T(8,128)(2,1)S(1)}, u32[]{:S(2)}, u32[]{:S(2)}) %collective-permute-start.1) | collective-permute-done | bytes 491552 | tf_op jit(solution)/shard_map/ppermute | solution.py:178
  36.1 7.2 %collective-permute-done.2.below_ref = bf16[6,1,320,128]{3,2,1,0:T(8,128)(2,1)S(1)} collective-permute-done((bf16[6,1,320,128]{3,2,1,0:T(8,128)(2,1)}, bf16[6,1,320,128]{3,2,1,0:T(8,128)(2,1)S(1)}, u32[]{:S(2)}, u32[]{:S(2)}) %collective-permute-start.2) | collective-permute-done | bytes 491552 | tf_op jit(solution)/shard_map/ppermute | solution.py:178
  43.3 0.0 copy-start.3
  43.3 0.8 copy-done.3
  44.0 0.0 copy-start.5
  44.1 0.0 copy-start.6
  44.1 0.0 copy-start.7
  44.1 0.0 copy-done.1
  44.1 0.6 copy-done.5
  44.7 0.0 copy-done.6
  44.7 0.0 copy-done.7
  44.7 0.0 copy-start.4
  44.7 1.0 %copy-done.4 = bf16[6,1,320,128]{3,2,1,0:T(8,128)(2,1)S(1)} copy-done((bf16[6,1,320,128]{3,2,1,0:T(8,128)(2,1)S(1)}, bf16[6,1,320,128]{3,2,1,0:T(8,128)(2,1)}, u32[]{:S(2)}) %copy-start.4) | copy-done | bytes 491544
  45.8 6.2 %first_conv.1 = (bf16[4,2,320,128]{3,2,1,0:T(8,128)(2,1)S(1)}, f32[256,2,128]{2,1,0:T(2,128)}) custom-call(s32[3]{0:T(128)S(1)} %add_convert_fusion.flags_ref, bf16[4,2,320,128]{3,2,1,0:T(8,128)(2,1)S(1)} %copy-done, bf16[2,2,320,128]{3,2,1,0:T(8,128)(2,1)S(1)} %collective-permute-done.back_ref, ...), custom_call_target="tpu_custom_call" | custom-call | tf_op jit(solution)/shard_map/first_conv/pallas_call | solution.py:216
  52.0 0.0 copy-start.2
  52.1 1.4 %collective-permute-start.3 = (bf16[2,2,320,128]{3,2,1,0:T(8,128)(2,1)S(1)}, bf16[2,2,320,128]{3,2,1,0:T(8,128)(2,1)S(1)}, u32[]{:S(2)}, u32[]{:S(2)}) collective-permute-start(bf16[2,2,320,128]{3,2,1,0:T(8,128)(2,1)S(1)} %slice.7), channel_id=1, source_target_pairs={{0,32},{32,64},{64,96},{96,128},{128,160},{160,192},{192,224},{1,3... | collective-permute-start | bytes 983048 | tf_op jit(solution)/shard_map/ppermute | solution.py:178
  53.5 12.5 %all-to-all-start.1 = ((f32[256,2,128]{2,1,0:T(2,128)}), f32[256,2,128]{2,1,0:T(2,128)S(1)}, u32[]{:S(2)}, u32[]{:S(2)}) async-start(f32[256,2,128]{2,1,0:T(2,128)} %get-tuple-element.16), calls=%async_computation.1 | async-start | bytes 524288 | tf_op jit(solution)/shard_map/all_to_all | solution.py:194
  66.0 0.0 collective-permute-done.3.back_ref
  66.1 1.0 %edge_rows.3 = (bf16[6,1,320,128]{3,2,1,0:T(8,128)(2,1)}, bf16[6,1,320,128]{3,2,1,0:T(8,128)(2,1)}) custom-call(bf16[4,2,320,128]{3,2,1,0:T(8,128)(2,1)S(1)} %get-tuple-element.13.own_ref, bf16[2,2,320,128]{3,2,1,0:T(8,128)(2,1)S(1)} %collective-permute-done.3.back_ref), custom_call_target="tpu_custom_call" | custom-call | tf_op jit(solution)/shard_map/edge_rows/pallas_call | solution.py:184
  67.1 4.8 %collective-permute-start.4 = (bf16[6,1,320,128]{3,2,1,0:T(8,128)(2,1)}, bf16[6,1,320,128]{3,2,1,0:T(8,128)(2,1)S(1)}, u32[]{:S(2)}, u32[]{:S(2)}) collective-permute-start(bf16[6,1,320,128]{3,2,1,0:T(8,128)(2,1)} %get-tuple-element.14), channel_id=1, source_target_pairs={{0,1},{1,2},{2,3},{3,4},{4,5},{5,6},{6,7},{7,8},{8,9},{9,10},{10,1... | collective-permute-start | bytes 1474568 | tf_op jit(solution)/shard_map/ppermute | solution.py:178
  71.9 1.9 %collective-permute-start.5 = (bf16[6,1,320,128]{3,2,1,0:T(8,128)(2,1)}, bf16[6,1,320,128]{3,2,1,0:T(8,128)(2,1)}, u32[]{:S(2)}, u32[]{:S(2)}) collective-permute-start(bf16[6,1,320,128]{3,2,1,0:T(8,128)(2,1)} %get-tuple-element.15), channel_id=1, source_target_pairs={{1,0},{2,1},{3,2},{4,3},{5,4},{6,5},{7,6},{8,7},{9,8},{10,9},{11,1... | collective-permute-start | bytes 1474568 | tf_op jit(solution)/shard_map/ppermute | solution.py:178
  73.8 3.7 %all-to-all-done.1.sums_ref = f32[256,2,128]{2,1,0:T(2,128)S(1)} async-done(((f32[256,2,128]{2,1,0:T(2,128)}), f32[256,2,128]{2,1,0:T(2,128)S(1)}, u32[]{:S(2)}, u32[]{:S(2)}) %all-to-all-start.1) | async-done | bytes 262176 | tf_op jit(solution)/shard_map/all_to_all | solution.py:194
  77.5 5.6 %collective-permute-done.4.above_ref = bf16[6,1,320,128]{3,2,1,0:T(8,128)(2,1)S(1)} collective-permute-done((bf16[6,1,320,128]{3,2,1,0:T(8,128)(2,1)}, bf16[6,1,320,128]{3,2,1,0:T(8,128)(2,1)S(1)}, u32[]{:S(2)}, u32[]{:S(2)}) %collective-permute-start.4) | collective-permute-done | bytes 491552 | tf_op jit(solution)/shard_map/ppermute | solution.py:178
  83.1 7.3 %collective-permute-done.5.below_ref = bf16[6,1,320,128]{3,2,1,0:T(8,128)(2,1)} collective-permute-done((bf16[6,1,320,128]{3,2,1,0:T(8,128)(2,1)}, bf16[6,1,320,128]{3,2,1,0:T(8,128)(2,1)}, u32[]{:S(2)}, u32[]{:S(2)}) %collective-permute-start.5) | collective-permute-done | bytes 491552 | tf_op jit(solution)/shard_map/ppermute | solution.py:178
  90.4 0.0 copy-start.8
  90.4 0.0 copy-start.9
  90.4 0.0 copy-start.10
  90.4 0.0 copy-done.2
  90.4 0.6 copy-done.8
  91.0 0.0 copy-done.9
  91.0 0.0 copy-done.10
  91.1 6.6 %second_conv.1 = bf16[4,2,320,128]{3,2,1,0:T(8,128)(2,1)} custom-call(s32[3]{0:T(128)S(1)} %add_convert_fusion.flags_ref, bf16[4,2,320,128]{3,2,1,0:T(8,128)(2,1)S(1)} %get-tuple-element.13.own_ref, bf16[2,2,320,128]{3,2,1,0:T(8,128)(2,1)S(1)} %collective-permute-done.3.back_ref, bf16[6,1,320,128]{3,2,1,0:T(8,128)(2,1)S(1)} %collective-permute-done.4.above_ref, ...), custom_call_target="tpu_custom_call" | custom-call | tf_op jit(solution)/shard_map/second_conv/pallas_call | solution.py:229
  (1 shorter events, 0.0 us)
Async XLA Ops:
  0.0 2.8 %copy-start = (bf16[4,2,320,128]{3,2,1,0:T(8,128)(2,1)S(1)}, bf16[4,2,320,128]{3,2,1,0:T(8,128)(2,1)}, u32[]{:S(2)}) copy-start(bf16[4,2,320,128]{3,2,1,0:T(8,128)(2,1)} %features_ref.1) | copy-start | bytes 1966084
  1.1 18.0 %collective-permute-start = (bf16[2,2,320,128]{3,2,1,0:T(8,128)(2,1)S(1)}, bf16[2,2,320,128]{3,2,1,0:T(8,128)(2,1)S(1)}, u32[]{:S(2)}, u32[]{:S(2)}) collective-permute-start(bf16[2,2,320,128]{3,2,1,0:T(8,128)(2,1)S(1)} %slice.6), channel_id=1, source_target_pairs={{0,32},{32,64},{64,96},{96,128},{128,160},{160,192},{192,224},{1,3... | collective-permute-start | bytes 983048 | tf_op jit(solution)/shard_map/ppermute | solution.py:178
  3.9 40.1 %copy-start.1 = (bf16[3456,128]{1,0:T(8,128)(2,1)S(1)}, bf16[3456,128]{1,0:T(8,128)(2,1)}, u32[]{:S(2)}) copy-start(bf16[3456,128]{1,0:T(8,128)(2,1)} %w_ref.2) | copy-start | bytes 2654212
  3.9 26.6 %all-to-all-start = ((f32[256,2,128]{2,1,0:T(2,128)}), f32[256,2,128]{2,1,0:T(2,128)S(1)}, u32[]{:S(2)}, u32[]{:S(2)}) async-start(f32[256,2,128]{2,1,0:T(2,128)} %moments.1), calls=%async_computation | async-start | bytes 524288 | tf_op jit(solution)/shard_map/all_to_all | solution.py:194
  20.1 16.0 %collective-permute-start.1 = (bf16[6,1,320,128]{3,2,1,0:T(8,128)(2,1)}, bf16[6,1,320,128]{3,2,1,0:T(8,128)(2,1)S(1)}, u32[]{:S(2)}, u32[]{:S(2)}) collective-permute-start(bf16[6,1,320,128]{3,2,1,0:T(8,128)(2,1)} %get-tuple-element.11), channel_id=1, source_target_pairs={{0,1},{1,2},{2,3},{3,4},{4,5},{5,6},{6,7},{7,8},{8,9},{9,10},{10,1... | collective-permute-start | bytes 1474568 | tf_op jit(solution)/shard_map/ppermute | solution.py:178
  24.9 18.4 %collective-permute-start.2 = (bf16[6,1,320,128]{3,2,1,0:T(8,128)(2,1)}, bf16[6,1,320,128]{3,2,1,0:T(8,128)(2,1)S(1)}, u32[]{:S(2)}, u32[]{:S(2)}) collective-permute-start(bf16[6,1,320,128]{3,2,1,0:T(8,128)(2,1)} %get-tuple-element.12), channel_id=1, source_target_pairs={{1,0},{2,1},{3,2},{4,3},{5,4},{6,5},{7,6},{8,7},{9,8},{10,9},{11,1... | collective-permute-start | bytes 1474568 | tf_op jit(solution)/shard_map/ppermute | solution.py:178
  43.3 0.8 copy-start.3
  44.0 0.7 copy-start.5
  44.1 0.7 copy-start.6
  44.1 0.7 copy-start.7
  44.7 1.0 %copy-start.4 = (bf16[6,1,320,128]{3,2,1,0:T(8,128)(2,1)S(1)}, bf16[6,1,320,128]{3,2,1,0:T(8,128)(2,1)}, u32[]{:S(2)}) copy-start(bf16[6,1,320,128]{3,2,1,0:T(8,128)(2,1)} %copy-done.3) | copy-start | bytes 1474564
  52.0 38.3 %copy-start.2 = (bf16[3456,128]{1,0:T(8,128)(2,1)S(1)}, bf16[3456,128]{1,0:T(8,128)(2,1)}, u32[]{:S(2)}) copy-start(bf16[3456,128]{1,0:T(8,128)(2,1)} %w_ref.3) | copy-start | bytes 2654212
  52.1 14.0 %collective-permute-start.3 = (bf16[2,2,320,128]{3,2,1,0:T(8,128)(2,1)S(1)}, bf16[2,2,320,128]{3,2,1,0:T(8,128)(2,1)S(1)}, u32[]{:S(2)}, u32[]{:S(2)}) collective-permute-start(bf16[2,2,320,128]{3,2,1,0:T(8,128)(2,1)S(1)} %slice.7), channel_id=1, source_target_pairs={{0,32},{32,64},{64,96},{96,128},{128,160},{160,192},{192,224},{1,3... | collective-permute-start | bytes 983048 | tf_op jit(solution)/shard_map/ppermute | solution.py:178
  53.5 24.0 %all-to-all-start.1 = ((f32[256,2,128]{2,1,0:T(2,128)}), f32[256,2,128]{2,1,0:T(2,128)S(1)}, u32[]{:S(2)}, u32[]{:S(2)}) async-start(f32[256,2,128]{2,1,0:T(2,128)} %get-tuple-element.16), calls=%async_computation.1 | async-start | bytes 524288 | tf_op jit(solution)/shard_map/all_to_all | solution.py:194
  67.1 16.0 %collective-permute-start.4 = (bf16[6,1,320,128]{3,2,1,0:T(8,128)(2,1)}, bf16[6,1,320,128]{3,2,1,0:T(8,128)(2,1)S(1)}, u32[]{:S(2)}, u32[]{:S(2)}) collective-permute-start(bf16[6,1,320,128]{3,2,1,0:T(8,128)(2,1)} %get-tuple-element.14), channel_id=1, source_target_pairs={{0,1},{1,2},{2,3},{3,4},{4,5},{5,6},{6,7},{7,8},{8,9},{9,10},{10,1... | collective-permute-start | bytes 1474568 | tf_op jit(solution)/shard_map/ppermute | solution.py:178
  71.9 18.5 %collective-permute-start.5 = (bf16[6,1,320,128]{3,2,1,0:T(8,128)(2,1)}, bf16[6,1,320,128]{3,2,1,0:T(8,128)(2,1)}, u32[]{:S(2)}, u32[]{:S(2)}) collective-permute-start(bf16[6,1,320,128]{3,2,1,0:T(8,128)(2,1)} %get-tuple-element.15), channel_id=1, source_target_pairs={{1,0},{2,1},{3,2},{4,3},{5,4},{6,5},{7,6},{8,7},{9,8},{10,9},{11,1... | collective-permute-start | bytes 1474568 | tf_op jit(solution)/shard_map/ppermute | solution.py:178
  90.4 0.7 copy-start.8
  90.4 0.7 copy-start.9
  90.4 0.7 copy-start.10

commit v3 on v2

v3 whole, which is shorter than its diff:
```python
import jax
import jax.numpy as jnp
from jax import lax
from jax.experimental import pallas as pl
from jax.experimental.pallas import tpu as pltpu
from jax.sharding import Mesh
from jax.sharding import PartitionSpec as P

C = 128
GROUP = 4
TM = ("y", "c")
ROWS = ("z", "x")
EVERY = TM + ROWS
EPS = 1e-06
MIB = 1 << 20
VMEM = pl.BlockSpec(memory_space=pltpu.VMEM)
SMEM = pl.BlockSpec(memory_space=pltpu.SMEM)


def group_total(v):
    lane = lax.broadcasted_iota(jnp.int32, v.shape, v.ndim - 1)
    for step in (1, 2):
        ahead = pltpu.roll(v, C - step, v.ndim - 1)
        behind = pltpu.roll(v, step, v.ndim - 1)
        v = v + jnp.where((lane & step) == 0, ahead, behind)
    return v


def packed_sums(ref):
    frames, rows, width, _ = ref.shape
    cells = frames * rows * width * GROUP

    def over(step):
        total = jnp.zeros((8, C), jnp.float32)
        for f in range(frames):
            for r in range(rows):
                part = step(ref[f, r].astype(jnp.float32))
                total = total + part.reshape(width // 8, 8, C).sum(axis=0)
        return group_total(jnp.broadcast_to(jnp.sum(total, axis=0, keepdims=True), (8, C)))

    first = over(lambda v: v)
    mean = first[:1] / cells
    centered = over(lambda v: (v - mean) * (v - mean))
    place = lax.broadcasted_iota(jnp.int32, (8, C), 1) % GROUP
    return jnp.where(place == 0, first, jnp.where(place == 1, centered, 0.0))


def scale_and_offset(sums_ref, gain_ref, shift_ref, cells):
    devices = sums_ref.shape[0]
    cells = cells * GROUP
    place = lax.broadcasted_iota(jnp.int32, (8, C), 1) % GROUP

    def whole(rows):
        total = jnp.sum(rows.reshape(devices // 8, 8, C), axis=0)
        total = jnp.broadcast_to(jnp.sum(total, axis=0, keepdims=True), (8, C))
        return total

    every = sums_ref[...]
    total = whole(every)
    average = group_total(jnp.where(place == 0, total, 0.0)) / (cells * devices)
    apart = every / cells - average[:1]
    between = whole(apart * apart) * cells
    squares = jnp.where(place == 0, between, jnp.where(place == 1, total, 0.0))
    spread = group_total(squares) / (cells * devices)
    scale = lax.rsqrt(spread[:1] + EPS) * gain_ref[...]
    offset = shift_ref[...] - average[:1] * scale
    return 0.5 * scale, 0.5 * offset


def activated(values, scale, offset):
    half = values.astype(jnp.float32) * scale + offset
    return (half + half * jnp.tanh(half)).astype(jnp.bfloat16)


def fill(act_ref, own_ref, back_ref, above_ref, below_ref, flags_ref, scale, offset):
    earlier = back_ref.shape[0]
    frames, rows, width = act_ref.shape[0], act_ref.shape[1], act_ref.shape[2]
    for f in range(frames):
        for r in range(rows):
            if f < earlier:
                source = back_ref[f, r]
            elif r == 0:
                source = above_ref[f - earlier, 0]
            elif r == rows - 1:
                source = below_ref[f - earlier, 0]
            else:
                source = own_ref[f - earlier, r - 1]
            act_ref[f, r] = activated(source, scale, offset)

    @pl.when(flags_ref[1] == 1)
    def _():
        act_ref[:, 0] = jnp.zeros((frames, width, C), jnp.bfloat16)

    @pl.when(flags_ref[2] == 1)
    def _():
        act_ref[:, rows - 1] = jnp.zeros((frames, width, C), jnp.bfloat16)

    @pl.when(flags_ref[0] == 1)
    def _():
        for f in range(earlier):
            act_ref[f] = act_ref[earlier]


def taps(act_ref, w_ref, start, count):
    width = act_ref.shape[2]
    cells = count * width
    pieces = [
        act_ref[start + i : start + i + count, r].reshape(cells, C) for i in range(3) for r in range(4)
    ]
    left = jnp.concatenate(pieces, axis=1)
    column = lax.broadcasted_iota(jnp.int32, (cells, 2 * C), 0) % width

    def block(i, j, k):
        if not 0 <= j < 3:
            return jnp.zeros((C, C), jnp.bfloat16)
        first = ((i * 3 + j) * 3 + k) * C
        return w_ref[first : first + C, :]

    total = None
    for k in (1, 0, 2):
        right = jnp.concatenate(
            [
                jnp.concatenate([block(i, r, k), block(i, r - 1, k)], axis=1)
                for i in range(3)
                for r in range(4)
            ],
            axis=0,
        )
        part = jnp.dot(left, right, preferred_element_type=jnp.float32)
        if k == 0:
            part = jnp.where(column == 0, 0.0, pltpu.roll(part, 1, 0))
        if k == 2:
            part = jnp.where(column == width - 1, 0.0, pltpu.roll(part, cells - 1, 0))
        total = part if total is None else total + part
    return total


def hand_out(ref, top_ref, bottom_ref, sums_ref):
    rows = ref.shape[1]
    top_ref[:, 0] = ref[:, 0]
    bottom_ref[:, 0] = ref[:, rows - 1]
    sums_ref[...] = jnp.broadcast_to(packed_sums(ref)[:1], sums_ref.shape)


def moments_kernel(x_ref, top_ref, bottom_ref, sums_ref):
    hand_out(x_ref, top_ref, bottom_ref, sums_ref)


def first_conv_kernel(
    flags_ref, own_ref, back_ref, above_ref, below_ref, sums_ref, gain_ref, shift_ref, w_ref, bias_ref,
    hidden_ref, top_ref, bottom_ref, next_ref, act_ref,
):
    frames, rows, width, _ = own_ref.shape
    scale, offset = scale_and_offset(sums_ref, gain_ref, shift_ref, frames * rows * width)
    fill(act_ref, own_ref, back_ref, above_ref, below_ref, flags_ref, scale, offset)
    for f in range(frames):
        total = taps(act_ref, w_ref, f, 1)
        for r in range(rows):
            value = total[:, r * C : (r + 1) * C] + bias_ref[...]
            hidden_ref[f, r] = value.astype(jnp.bfloat16)
    hand_out(hidden_ref, top_ref, bottom_ref, next_ref)


def second_conv_kernel(
    flags_ref, own_ref, back_ref, above_ref, below_ref, sums_ref, gain_ref, shift_ref, w_ref, bias_ref,
    features_ref, out_ref, act_ref,
):
    frames, rows, width, _ = own_ref.shape
    scale, offset = scale_and_offset(sums_ref, gain_ref, shift_ref, frames * rows * width)
    fill(act_ref, own_ref, back_ref, above_ref, below_ref, flags_ref, scale, offset)
    for f in range(frames):
        total = taps(act_ref, w_ref, f, 1)
        for r in range(rows):
            value = total[:, r * C : (r + 1) * C] + bias_ref[...]
            value = value + features_ref[f, r].astype(jnp.float32)
            out_ref[f, r] = value.astype(jnp.bfloat16)


def last_kernel(own_ref, above_ref, below_ref, last_ref):
    earlier, rows = last_ref.shape[0], last_ref.shape[1]
    for f in range(earlier):
        source = own_ref.shape[0] - earlier + f
        last_ref[f, 0] = above_ref[source, 0]
        last_ref[f, 1 : rows - 1] = own_ref[source]
        last_ref[f, rows - 1] = below_ref[source, 0]


def shifted(block, axes, step):
    count = lax.axis_size(axes)
    return lax.ppermute(block, axes, [(i, i + step) for i in range(count) if 0 <= i + step < count])


def neighbours(own, top, bottom):
    _, rows, width, _ = own.shape
    above = shifted(bottom, ROWS, 1)
    below = shifted(top, ROWS, -1)
    last = pl.pallas_call(
        last_kernel,
        out_shape=jax.ShapeDtypeStruct((2, rows + 2, width, C), own.dtype),
        in_specs=[VMEM] * 3,
        out_specs=VMEM,
        name="last_frames",
        compiler_params=pltpu.CompilerParams(vmem_limit_bytes=8 * MIB),
    )(own, above, below)
    back = shifted(last, TM, 1)
    return back, above, below


def everywhere(copies):
    devices = copies.shape[0]
    received = lax.all_to_all(
        copies.reshape(devices, 1, C), EVERY, split_axis=0, concat_axis=0, tiled=True
    )
    return received.reshape(devices, C)


def body(features, gain_one, shift_one, weight_one, bias_one, gain_two, shift_two, weight_two, bias_two):
    frames, rows, width, _ = features.shape
    copies = jax.ShapeDtypeStruct((lax.axis_size(EVERY), C), jnp.float32)
    tile = jax.ShapeDtypeStruct(features.shape, jnp.bfloat16)
    edge = jax.ShapeDtypeStruct((frames, 1, width, C), jnp.bfloat16)
    row = lax.axis_index(ROWS)
    flags = jnp.stack(
        [lax.axis_index(TM) == 0, row == 0, row == lax.axis_size(ROWS) - 1]
    ).astype(jnp.int32)
    common = dict(
        scratch_shapes=[pltpu.VMEM((frames + 2, rows + 2, width, C), jnp.bfloat16)],
        compiler_params=pltpu.CompilerParams(vmem_limit_bytes=32 * MIB),
    )
    specs = [SMEM] + [VMEM] * 9
    vectors = [v.reshape(1, C) for v in (gain_one, shift_one, bias_one, gain_two, shift_two, bias_two)]

    top, bottom, sums = pl.pallas_call(
        moments_kernel,
        out_shape=(edge, edge, copies),
        in_specs=[VMEM],
        out_specs=(VMEM,) * 3,
        name="moments",
        compiler_params=pltpu.CompilerParams(vmem_limit_bytes=8 * MIB),
    )(features)
    back, above, below = neighbours(features, top, bottom)
    sums = everywhere(sums)
    hidden, top, bottom, sums_two = pl.pallas_call(
        first_conv_kernel,
        out_shape=(tile, edge, edge, copies),
        in_specs=specs,
        out_specs=(VMEM,) * 4,
        name="first_conv",
        **common,
    )(flags, features, back, above, below, sums, vectors[0], vectors[1], weight_one, vectors[2])

    back, above, below = neighbours(hidden, top, bottom)
    sums_two = everywhere(sums_two)
    return pl.pallas_call(
        second_conv_kernel,
        out_shape=tile,
        in_specs=specs + [VMEM],
        out_specs=VMEM,
        name="second_conv",
        **common,
    )(flags, hidden, back, above, below, sums_two, vectors[3], vectors[4], weight_two, vectors[5], features)


def solution(mesh):
    split = Mesh(mesh.devices.reshape(4, 2, 8, 4), EVERY)
    return jax.shard_map(
        body,
        mesh=split,
        in_specs=(P(TM, ROWS, None, None), P(), P(), P(), P(), P(), P(), P(), P()),
        out_specs=P(TM, ROWS, None, None),
        check_vma=False,
    )
```

time: 98.2 us -> 104 us (1.059)
  the two profiles are of different devices: /device:TPU:102 before, /device:TPU:1 now
where the time goes in v3:
time: 104 us; the launch traced here: 103 us
  starting transfers between devices  34.8 us (33%)
  waiting for transfers between devices  29.2 us (28%)
  blocking collectives  23.2 us (22%)
  Pallas kernels  12.7 us (12%)
  local copies, waits for them, and re-layouts  3.08 us (3%)
    all_to_all x1, blocking collectives, everywhere(): lax.all_to_all(copies.reshape(devices, 1, C), EVERY, split_axis=0, concat...  23.2 us
    ppermute x6, starting transfers between devices, shifted(): lax.ppermute(block, axes, [(i, i + step) for i in range(count) if 0 <= i...  17.8 us
    ppermute x6, waiting for transfers between devices, shifted(): lax.ppermute(block, axes, [(i, i + step) for i in range(count) if 0 <= i...  17.7 us
    all_to_all x1, starting transfers between devices, everywhere(): lax.all_to_all(copies.reshape(devices, 1, C), EVERY, split_axis=0, concat...  17 us
    all_to_all x1, waiting for transfers between devices, everywhere(): lax.all_to_all(copies.reshape(devices, 1, C), EVERY, split_axis=0, concat...  11.5 us
    pallas_call x1, Pallas kernels, body(): pl.pallas_call(first_conv_kernel, out_shape=(tile, edge, edge, copies), i...  6.08 us
    pallas_call x1, Pallas kernels, body(): pl.pallas_call(second_conv_kernel, out_shape=tile, in_specs=specs + [VMEM...  5.93 us
    unnamed x22, local copies, waits for them, and re-layouts  3.08 us
  transfers between devices with their start and end apart: 7, of which 5 were waited for; matrix products, arithmetic and copies ran while one was open for 0% of the time, Pallas kernels for 0%

profile of v3, /device:TPU:1, one launch (start us, length us, event | category | flops | bytes accessed | tf_op | source)
XLA Modules:
  0.0 103.2 jit_solution(1260714019246923137)
XLA Ops:
  0.0 0.0 copy-start
  0.0 1.1 %copy-done = bf16[4,2,320,128]{3,2,1,0:T(8,128)(2,1)S(1)} copy-done((bf16[4,2,320,128]{3,2,1,0:T(8,128)(2,1)S(1)}, bf16[4,2,320,128]{3,2,1,0:T(8,128)(2,1)}, u32[]{:S(2)}) %copy-start) | copy-done | bytes 655384
  1.1 0.6 moments.1
  1.7 0.0 copy-start.4
  1.7 0.6 copy-done.4
  2.3 3.9 %collective-permute-start = (bf16[4,1,320,128]{3,2,1,0:T(8,128)(2,1)S(1)}, bf16[4,1,320,128]{3,2,1,0:T(8,128)(2,1)S(1)}, u32[]{:S(2)}, u32[]{:S(2)}) collective-permute-start(bf16[4,1,320,128]{3,2,1,0:T(8,128)(2,1)S(1)} %get-tuple-element.12), channel_id=1, source_target_pairs={{0,1},{1,2},{2,3},{3,4},{4,5},{5,6},{6,7},{7,8},{8,9},{9,10},{10,1... | collective-permute-start | bytes 983048 | tf_op jit(solution)/shard_map/ppermute | solution.py:190
  6.3 0.0 copy-start.1
  6.3 0.0 copy-start.2
  6.3 1.4 %collective-permute-start.1 = (bf16[4,1,320,128]{3,2,1,0:T(8,128)(2,1)S(1)}, bf16[4,1,320,128]{3,2,1,0:T(8,128)(2,1)S(1)}, u32[]{:S(2)}, u32[]{:S(2)}) collective-permute-start(bf16[4,1,320,128]{3,2,1,0:T(8,128)(2,1)S(1)} %get-tuple-element.13), channel_id=1, source_target_pairs={{1,0},{2,1},{3,2},{4,3},{5,4},{6,5},{7,6},{8,7},{9,8},{10,9},{11,1... | collective-permute-start | bytes 983048 | tf_op jit(solution)/shard_map/ppermute | solution.py:190
  7.7 4.9 %collective-permute-done.above_ref = bf16[4,1,320,128]{3,2,1,0:T(8,128)(2,1)S(1)} collective-permute-done((bf16[4,1,320,128]{3,2,1,0:T(8,128)(2,1)S(1)}, bf16[4,1,320,128]{3,2,1,0:T(8,128)(2,1)S(1)}, u32[]{:S(2)}, u32[]{:S(2)}) %collective-permute-start) | collective-permute-done | bytes 327712 | tf_op jit(solution)/shard_map/ppermute | solution.py:190
  12.6 4.0 %collective-permute-done.1.below_ref = bf16[4,1,320,128]{3,2,1,0:T(8,128)(2,1)S(1)} collective-permute-done((bf16[4,1,320,128]{3,2,1,0:T(8,128)(2,1)S(1)}, bf16[4,1,320,128]{3,2,1,0:T(8,128)(2,1)S(1)}, u32[]{:S(2)}, u32[]{:S(2)}) %collective-permute-start.1) | collective-permute-done | bytes 327712 | tf_op jit(solution)/shard_map/ppermute | solution.py:190
  16.7 4.9 %collective-permute-start.2 = (bf16[2,4,320,128]{3,2,1,0:T(8,128)(2,1)S(1)}, bf16[2,4,320,128]{3,2,1,0:T(8,128)(2,1)S(1)}, u32[]{:S(2)}, u32[]{:S(2)}) collective-permute-start(bf16[2,4,320,128]{3,2,1,0:T(8,128)(2,1)S(1)} %last_frames.2), channel_id=1, source_target_pairs={{0,32},{32,64},{64,96},{96,128},{128,160},{160,192},{192,224},{1,3... | collective-permute-start | bytes 1966088 | tf_op jit(solution)/shard_map/ppermute | solution.py:190
  21.6 17.0 %all-to-all-start = ((f32[256,1,128]{2,1,0:T(1,128)}), f32[256,1,128]{2,1,0:T(1,128)}, u32[]{:S(2)}, u32[]{:S(2)}) async-start(f32[256,1,128]{2,1,0:T(1,128)} %bitcast.18), calls=%async_computation | async-start | bytes 262144 | tf_op jit(solution)/shard_map/all_to_all | solution.py:211
  38.6 0.1 add_convert_fusion.flags_ref
  38.7 11.5 %all-to-all-done = f32[256,1,128]{2,1,0:T(1,128)} async-done(((f32[256,1,128]{2,1,0:T(1,128)}), f32[256,1,128]{2,1,0:T(1,128)}, u32[]{:S(2)}, u32[]{:S(2)}) %all-to-all-start) | async-done | bytes 131104 | tf_op jit(solution)/shard_map/all_to_all | solution.py:211
  50.2 0.0 collective-permute-done.2.back_ref
  50.2 0.0 copy-start.5
  50.2 0.0 copy-start.6
  50.2 0.0 copy-start.7
  50.3 0.0 copy-done.1
  50.3 0.0 copy-done.2
  50.3 0.6 copy-done.5
  50.9 0.0 copy-done.6
  50.9 0.0 copy-done.7
  50.9 6.1 %first_conv.1 = (bf16[4,2,320,128]{3,2,1,0:T(8,128)(2,1)S(1)}, bf16[4,1,320,128]{3,2,1,0:T(8,128)(2,1)S(1)}, bf16[4,1,320,128]{3,2,1,0:T(8,128)(2,1)S(1)}, f32[256,128]{1,0:T(8,128)S(1)}) custom-call(s32[3]{0:T(128)S(1)} %add_convert_fusion.flags_ref, bf16[4,2,320,128]{3,2,1,0:T(8,128)(2,1)S(1)} %copy-done.1, ...), custom_call_target="tpu_custom_call" | custom-call | tf_op jit(solution)/shard_map/first_conv/pallas_call | solution.py:243
  57.0 2.3 %collective-permute-start.3 = (bf16[4,1,320,128]{3,2,1,0:T(8,128)(2,1)S(1)}, bf16[4,1,320,128]{3,2,1,0:T(8,128)(2,1)S(1)}, u32[]{:S(2)}, u32[]{:S(2)}) collective-permute-start(bf16[4,1,320,128]{3,2,1,0:T(8,128)(2,1)S(1)} %get-tuple-element.16), channel_id=1, source_target_pairs={{0,1},{1,2},{2,3},{3,4},{4,5},{5,6},{6,7},{7,8},{8,9},{9,10},{10,1... | collective-permute-start | bytes 983048 | tf_op jit(solution)/shard_map/ppermute | solution.py:190
  59.3 1.3 %collective-permute-start.4 = (bf16[4,1,320,128]{3,2,1,0:T(8,128)(2,1)S(1)}, bf16[4,1,320,128]{3,2,1,0:T(8,128)(2,1)S(1)}, u32[]{:S(2)}, u32[]{:S(2)}) collective-permute-start(bf16[4,1,320,128]{3,2,1,0:T(8,128)(2,1)S(1)} %get-tuple-element.17), channel_id=1, source_target_pairs={{1,0},{2,1},{3,2},{4,3},{5,4},{6,5},{7,6},{8,7},{9,8},{10,9},{11,1... | collective-permute-start | bytes 983048 | tf_op jit(solution)/shard_map/ppermute | solution.py:190
  60.6 4.9 %collective-permute-done.3.above_ref = bf16[4,1,320,128]{3,2,1,0:T(8,128)(2,1)S(1)} collective-permute-done((bf16[4,1,320,128]{3,2,1,0:T(8,128)(2,1)S(1)}, bf16[4,1,320,128]{3,2,1,0:T(8,128)(2,1)S(1)}, u32[]{:S(2)}, u32[]{:S(2)}) %collective-permute-start.3) | collective-permute-done | bytes 327712 | tf_op jit(solution)/shard_map/ppermute | solution.py:190
  65.6 3.9 %collective-permute-done.4.below_ref = bf16[4,1,320,128]{3,2,1,0:T(8,128)(2,1)S(1)} collective-permute-done((bf16[4,1,320,128]{3,2,1,0:T(8,128)(2,1)S(1)}, bf16[4,1,320,128]{3,2,1,0:T(8,128)(2,1)S(1)}, u32[]{:S(2)}, u32[]{:S(2)}) %collective-permute-start.4) | collective-permute-done | bytes 327712 | tf_op jit(solution)/shard_map/ppermute | solution.py:190
  69.4 0.0 copy-start.3
  69.5 3.9 %collective-permute-start.5 = (bf16[2,4,320,128]{3,2,1,0:T(8,128)(2,1)S(1)}, bf16[2,4,320,128]{3,2,1,0:T(8,128)(2,1)S(1)}, u32[]{:S(2)}, u32[]{:S(2)}) collective-permute-start(bf16[2,4,320,128]{3,2,1,0:T(8,128)(2,1)S(1)} %last_frames.3), channel_id=1, source_target_pairs={{0,32},{32,64},{64,96},{96,128},{128,160},{160,192},{192,224},{1,3... | collective-permute-start | bytes 1966088 | tf_op jit(solution)/shard_map/ppermute | solution.py:190
  73.4 23.2 %all_to_all.10 = f32[256,1,128]{2,1,0:T(1,128)S(1)} all-to-all(f32[256,1,128]{2,1,0:T(1,128)S(1)} %bitcast.19), channel_id=1, replica_groups=mesh['y'=4,'c'=2,'z'=8,'x'=4] {'y','c','z','x'}, dimensions={0} | all-to-all | bytes 262144 | tf_op jit(solution)/shard_map/all_to_all | solution.py:211
  96.6 0.0 collective-permute-done.5.back_ref
  96.6 0.0 copy-start.8
  96.6 0.0 copy-start.9
  96.6 0.0 copy-start.10
  96.6 0.0 copy-done.3
  96.6 0.6 copy-done.8
  97.2 0.0 copy-done.9
  97.2 0.0 copy-done.10
  97.2 5.9 %second_conv.1 = bf16[4,2,320,128]{3,2,1,0:T(8,128)(2,1)} custom-call(s32[3]{0:T(128)S(1)} %add_convert_fusion.flags_ref, bf16[4,2,320,128]{3,2,1,0:T(8,128)(2,1)S(1)} %get-tuple-element.15.own_ref, bf16[2,4,320,128]{3,2,1,0:T(8,128)(2,1)S(1)} %collective-permute-done.5.back_ref, bf16[4,1,320,128]{3,2,1,0:T(8,128)(2,1)S(1)} %collective-permute-done.3.above_ref, ...), custom_call_target="tpu_custom_call" | custom-call | tf_op jit(solution)/shard_map/second_conv/pallas_call | solution.py:254
  (2 shorter events, 0.1 us)
Async XLA Ops:
  0.0 1.1 %copy-start = (bf16[4,2,320,128]{3,2,1,0:T(8,128)(2,1)S(1)}, bf16[4,2,320,128]{3,2,1,0:T(8,128)(2,1)}, u32[]{:S(2)}) copy-start(bf16[4,2,320,128]{3,2,1,0:T(8,128)(2,1)} %features_ref.1) | copy-start | bytes 1966084
  1.7 0.7 copy-start.4
  2.3 10.3 %collective-permute-start = (bf16[4,1,320,128]{3,2,1,0:T(8,128)(2,1)S(1)}, bf16[4,1,320,128]{3,2,1,0:T(8,128)(2,1)S(1)}, u32[]{:S(2)}, u32[]{:S(2)}) collective-permute-start(bf16[4,1,320,128]{3,2,1,0:T(8,128)(2,1)S(1)} %get-tuple-element.12), channel_id=1, source_target_pairs={{0,1},{1,2},{2,3},{3,4},{4,5},{5,6},{6,7},{7,8},{8,9},{9,10},{10,1... | collective-permute-start | bytes 983048 | tf_op jit(solution)/shard_map/ppermute | solution.py:190
  6.3 44.0 %copy-start.1 = (bf16[4,2,320,128]{3,2,1,0:T(8,128)(2,1)S(1)}, bf16[4,2,320,128]{3,2,1,0:T(8,128)(2,1)}, u32[]{:S(2)}) copy-start(bf16[4,2,320,128]{3,2,1,0:T(8,128)(2,1)} %features_ref.1) | copy-start | bytes 1966084
  6.3 44.0 %copy-start.2 = (bf16[3456,128]{1,0:T(8,128)(2,1)S(1)}, bf16[3456,128]{1,0:T(8,128)(2,1)}, u32[]{:S(2)}) copy-start(bf16[3456,128]{1,0:T(8,128)(2,1)} %w_ref.2) | copy-start | bytes 2654212
  6.3 10.3 %collective-permute-start.1 = (bf16[4,1,320,128]{3,2,1,0:T(8,128)(2,1)S(1)}, bf16[4,1,320,128]{3,2,1,0:T(8,128)(2,1)S(1)}, u32[]{:S(2)}, u32[]{:S(2)}) collective-permute-start(bf16[4,1,320,128]{3,2,1,0:T(8,128)(2,1)S(1)} %get-tuple-element.13), channel_id=1, source_target_pairs={{1,0},{2,1},{3,2},{4,3},{5,4},{6,5},{7,6},{8,7},{9,8},{10,9},{11,1... | collective-permute-start | bytes 983048 | tf_op jit(solution)/shard_map/ppermute | solution.py:190
  16.7 33.5 %collective-permute-start.2 = (bf16[2,4,320,128]{3,2,1,0:T(8,128)(2,1)S(1)}, bf16[2,4,320,128]{3,2,1,0:T(8,128)(2,1)S(1)}, u32[]{:S(2)}, u32[]{:S(2)}) collective-permute-start(bf16[2,4,320,128]{3,2,1,0:T(8,128)(2,1)S(1)} %last_frames.2), channel_id=1, source_target_pairs={{0,32},{32,64},{64,96},{96,128},{128,160},{160,192},{192,224},{1,3... | collective-permute-start | bytes 1966088 | tf_op jit(solution)/shard_map/ppermute | solution.py:190
  21.6 28.6 %all-to-all-start = ((f32[256,1,128]{2,1,0:T(1,128)}), f32[256,1,128]{2,1,0:T(1,128)}, u32[]{:S(2)}, u32[]{:S(2)}) async-start(f32[256,1,128]{2,1,0:T(1,128)} %bitcast.18), calls=%async_computation | async-start | bytes 262144 | tf_op jit(solution)/shard_map/all_to_all | solution.py:211
  50.2 0.7 copy-start.5
  50.2 0.7 copy-start.6
  50.2 0.7 copy-start.7
  57.0 8.6 %collective-permute-start.3 = (bf16[4,1,320,128]{3,2,1,0:T(8,128)(2,1)S(1)}, bf16[4,1,320,128]{3,2,1,0:T(8,128)(2,1)S(1)}, u32[]{:S(2)}, u32[]{:S(2)}) collective-permute-start(bf16[4,1,320,128]{3,2,1,0:T(8,128)(2,1)S(1)} %get-tuple-element.16), channel_id=1, source_target_pairs={{0,1},{1,2},{2,3},{3,4},{4,5},{5,6},{6,7},{7,8},{8,9},{9,10},{10,1... | collective-permute-start | bytes 983048 | tf_op jit(solution)/shard_map/ppermute | solution.py:190
  59.3 10.1 %collective-permute-start.4 = (bf16[4,1,320,128]{3,2,1,0:T(8,128)(2,1)S(1)}, bf16[4,1,320,128]{3,2,1,0:T(8,128)(2,1)S(1)}, u32[]{:S(2)}, u32[]{:S(2)}) collective-permute-start(bf16[4,1,320,128]{3,2,1,0:T(8,128)(2,1)S(1)} %get-tuple-element.17), channel_id=1, source_target_pairs={{1,0},{2,1},{3,2},{4,3},{5,4},{6,5},{7,6},{8,7},{9,8},{10,9},{11,1... | collective-permute-start | bytes 983048 | tf_op jit(solution)/shard_map/ppermute | solution.py:190
  69.4 27.2 %copy-start.3 = (bf16[3456,128]{1,0:T(8,128)(2,1)S(1)}, bf16[3456,128]{1,0:T(8,128)(2,1)}, u32[]{:S(2)}) copy-start(bf16[3456,128]{1,0:T(8,128)(2,1)} %w_ref.3) | copy-start | bytes 2654212
  69.5 27.1 %collective-permute-start.5 = (bf16[2,4,320,128]{3,2,1,0:T(8,128)(2,1)S(1)}, bf16[2,4,320,128]{3,2,1,0:T(8,128)(2,1)S(1)}, u32[]{:S(2)}, u32[]{:S(2)}) collective-permute-start(bf16[2,4,320,128]{3,2,1,0:T(8,128)(2,1)S(1)} %last_frames.3), channel_id=1, source_target_pairs={{0,32},{32,64},{64,96},{96,128},{128,160},{160,192},{192,224},{1,3... | collective-permute-start | bytes 1966088 | tf_op jit(solution)/shard_map/ppermute | solution.py:190
  96.6 0.7 copy-start.8
  96.6 0.7 copy-start.9
  96.6 0.7 copy-start.10

commit v4 on v3

--- a/solution.py
+++ b/solution.py
@@ -1,3 +1,5 @@
+import functools
+
 import jax
 import jax.numpy as jnp
 from jax import lax
@@ -11,6 +13,8 @@
 TM = ("y", "c")
 ROWS = ("z", "x")
 EVERY = TM + ROWS
+FAR = ("y", "z")
+NEAR = ("c", "x")
 EPS = 1e-06
 MIB = 1 << 20
 VMEM = pl.BlockSpec(memory_space=pltpu.VMEM)
@@ -26,6 +30,20 @@
     return v
 
 
+def lane_place(shape):
+    return lax.broadcasted_iota(jnp.int32, shape, len(shape) - 1) % GROUP
+
+
+def packed(first, centered):
+    place = lane_place(first.shape)
+    return jnp.where(place == 0, first, jnp.where(place == 1, centered, 0.0))
+
+
+def column_total(rows):
+    total = jnp.sum(rows.reshape(rows.shape[0] // 8, 8, C), axis=0)
+    return jnp.broadcast_to(jnp.sum(total, axis=0, keepdims=True), (8, C))
+
+
 def packed_sums(ref):
     frames, rows, width, _ = ref.shape
     cells = frames * rows * width * GROUP
@@ -36,34 +54,31 @@
             for r in range(rows):
                 part = step(ref[f, r].astype(jnp.float32))
                 total = total + part.reshape(width // 8, 8, C).sum(axis=0)
-        return group_total(jnp.broadcast_to(jnp.sum(total, axis=0, keepdims=True), (8, C)))
+        return group_total(column_total(total))
 
     first = over(lambda v: v)
     mean = first[:1] / cells
-    centered = over(lambda v: (v - mean) * (v - mean))
-    place = lax.broadcasted_iota(jnp.int32, (8, C), 1) % GROUP
-    return jnp.where(place == 0, first, jnp.where(place == 1, centered, 0.0))
-
-
-def scale_and_offset(sums_ref, gain_ref, shift_ref, cells):
-    devices = sums_ref.shape[0]
-    cells = cells * GROUP
-    place = lax.broadcasted_iota(jnp.int32, (8, C), 1) % GROUP
-
-    def whole(rows):
-        total = jnp.sum(rows.reshape(devices // 8, 8, C), axis=0)
-        total = jnp.broadcast_to(jnp.sum(total, axis=0, keepdims=True), (8, C))
-        return total
-
-    every = sums_ref[...]
-    total = whole(every)
-    average = group_total(jnp.where(place == 0, total, 0.0)) / (cells * devices)
-    apart = every / cells - average[:1]
-    between = whole(apart * apart) * cells
-    squares = jnp.where(place == 0, between, jnp.where(place == 1, total, 0.0))
-    spread = group_total(squares) / (cells * devices)
-    scale = lax.rsqrt(spread[:1] + EPS) * gain_ref[...]
-    offset = shift_ref[...] - average[:1] * scale
+    return packed(first, over(lambda v: (v - mean) * (v - mean)))
+
+
+def merged(every, cells):
+    count = every.shape[0]
+    total = column_total(every)
+    place = lane_place(total.shape)
+    first = group_total(jnp.where(place == 0, total, 0.0))
+    apart = every / cells - first[:1] / (cells * count)
+    between = column_total(apart * apart) * cells
+    centered = group_total(jnp.where(place == 0, between, jnp.where(place == 1, total, 0.0)))
+    return first, centered
+
+
+def scale_and_offset(sums_ref, vectors_ref, which, tile_cells, devices):
+    count = sums_ref.shape[0]
+    cells = tile_cells * GROUP * devices
+    first, centered = merged(sums_ref[...], cells // count)
+    average, spread = first[:1] / cells, centered[:1] / cells
+    scale = lax.rsqrt(spread + EPS) * vectors_ref[which : which + 1]
+    offset = vectors_ref[which + 1 : which + 2] - average * scale
     return 0.5 * scale, 0.5 * offset
 
 
@@ -142,36 +157,44 @@
     sums_ref[...] = jnp.broadcast_to(packed_sums(ref)[:1], sums_ref.shape)
 
 
-def moments_kernel(x_ref, top_ref, bottom_ref, sums_ref):
+def moments_kernel(x_ref, *refs):
+    vectors, (top_ref, bottom_ref, sums_ref, vectors_ref) = refs[:-4], refs[-4:]
     hand_out(x_ref, top_ref, bottom_ref, sums_ref)
+    for i, vector in enumerate(vectors):
+        vectors_ref[i : i + 1] = vector[...]
+
+
+def relay_kernel(cells, sums_ref, next_ref):
+    both = packed(*merged(sums_ref[...], cells))
+    next_ref[...] = jnp.broadcast_to(both[:1], next_ref.shape)
 
 
 def first_conv_kernel(
-    flags_ref, own_ref, back_ref, above_ref, below_ref, sums_ref, gain_ref, shift_ref, w_ref, bias_ref,
+    devices, flags_ref, own_ref, back_ref, above_ref, below_ref, sums_ref, vectors_ref, w_ref,
     hidden_ref, top_ref, bottom_ref, next_ref, act_ref,
 ):
     frames, rows, width, _ = own_ref.shape
-    scale, offset = scale_and_offset(sums_ref, gain_ref, shift_ref, frames * rows * width)
+    scale, offset = scale_and_offset(sums_ref, vectors_ref, 0, frames * rows * width, devices)
     fill(act_ref, own_ref, back_ref, above_ref, below_ref, flags_ref, scale, offset)
     for f in range(frames):
         total = taps(act_ref, w_ref, f, 1)
         for r in range(rows):
-            value = total[:, r * C : (r + 1) * C] + bias_ref[...]
+            value = total[:, r * C : (r + 1) * C] + vectors_ref[2:3]
             hidden_ref[f, r] = value.astype(jnp.bfloat16)
     hand_out(hidden_ref, top_ref, bottom_ref, next_ref)
 
 
 def second_conv_kernel(
-    flags_ref, own_ref, back_ref, above_ref, below_ref, sums_ref, gain_ref, shift_ref, w_ref, bias_ref,
+    devices, flags_ref, own_ref, back_ref, above_ref, below_ref, sums_ref, vectors_ref, w_ref,
     features_ref, out_ref, act_ref,
 ):
     frames, rows, width, _ = own_ref.shape
-    scale, offset = scale_and_offset(sums_ref, gain_ref, shift_ref, frames * rows * width)
+    scale, offset = scale_and_offset(sums_ref, vectors_ref, 3, frames * rows * width, devices)
     fill(act_ref, own_ref, back_ref, above_ref, below_ref, flags_ref, scale, offset)
     for f in range(frames):
         total = taps(act_ref, w_ref, f, 1)
         for r in range(rows):
-            value = total[:, r * C : (r + 1) * C] + bias_ref[...]
+            value = total[:, r * C : (r + 1) * C] + vectors_ref[5:6]
             value = value + features_ref[f, r].astype(jnp.float32)
             out_ref[f, r] = value.astype(jnp.bfloat16)
 
@@ -206,17 +229,30 @@
     return back, above, below
 
 
-def everywhere(copies):
-    devices = copies.shape[0]
-    received = lax.all_to_all(
-        copies.reshape(devices, 1, C), EVERY, split_axis=0, concat_axis=0, tiled=True
-    )
-    return received.reshape(devices, C)
+def exchanged(copies, axes):
+    count = copies.shape[0]
+    received = lax.all_to_all(copies.reshape(count, 1, C), axes, split_axis=0, concat_axis=0, tiled=True)
+    return received.reshape(count, C)
+
+
+def everywhere(copies, tile_cells):
+    sums = exchanged(copies, FAR)
+    copies = pl.pallas_call(
+        functools.partial(relay_kernel, tile_cells * GROUP),
+        out_shape=jax.ShapeDtypeStruct((lax.axis_size(NEAR), C), jnp.float32),
+        in_specs=[VMEM],
+        out_specs=VMEM,
+        name="relay",
+        compiler_params=pltpu.CompilerParams(vmem_limit_bytes=4 * MIB),
+    )(sums)
+    return exchanged(copies, NEAR)
 
 
 def body(features, gain_one, shift_one, weight_one, bias_one, gain_two, shift_two, weight_two, bias_two):
     frames, rows, width, _ = features.shape
-    copies = jax.ShapeDtypeStruct((lax.axis_size(EVERY), C), jnp.float32)
+    copies = jax.ShapeDtypeStruct((lax.axis_size(FAR), C), jnp.float32)
+    devices = lax.axis_size(EVERY)
+    tile_cells = frames * rows * width
     tile = jax.ShapeDtypeStruct(features.shape, jnp.bfloat16)
     edge = jax.ShapeDtypeStruct((frames, 1, width, C), jnp.bfloat16)
     row = lax.axis_index(ROWS)
@@ -227,38 +263,38 @@
         scratch_shapes=[pltpu.VMEM((frames + 2, rows + 2, width, C), jnp.bfloat16)],
         compiler_params=pltpu.CompilerParams(vmem_limit_bytes=32 * MIB),
     )
-    specs = [SMEM] + [VMEM] * 9
+    specs = [SMEM] + [VMEM] * 7
     vectors = [v.reshape(1, C) for v in (gain_one, shift_one, bias_one, gain_two, shift_two, bias_two)]
 
-    top, bottom, sums = pl.pallas_call(
+    top, bottom, sums, vectors = pl.pallas_call(
         moments_kernel,
-        out_shape=(edge, edge, copies),
-        in_specs=[VMEM],
-        out_specs=(VMEM,) * 3,
+        out_shape=(edge, edge, copies, jax.ShapeDtypeStruct((8, C), jnp.float32)),
+        in_specs=[VMEM] * 7,
+        out_specs=(VMEM,) * 4,
         name="moments",
         compiler_params=pltpu.CompilerParams(vmem_limit_bytes=8 * MIB),
-    )(features)
+    )(features, *vectors)
     back, above, below = neighbours(features, top, bottom)
-    sums = everywhere(sums)
+    sums = everywhere(sums, tile_cells)
     hidden, top, bottom, sums_two = pl.pallas_call(
-        first_conv_kernel,
+        functools.partial(first_conv_kernel, devices),
         out_shape=(tile, edge, edge, copies),
         in_specs=specs,
         out_specs=(VMEM,) * 4,
         name="first_conv",
         **common,
-    )(flags, features, back, above, below, sums, vectors[0], vectors[1], weight_one, vectors[2])
+    )(flags, features, back, above, below, sums, vectors, weight_one)
 
     back, above, below = neighbours(hidden, top, bottom)
-    sums_two = everywhere(sums_two)
+    sums_two = everywhere(sums_two, tile_cells)
     return pl.pallas_call(
-        second_conv_kernel,
+        functools.partial(second_conv_kernel, devices),
         out_shape=tile,
         in_specs=specs + [VMEM],
         out_specs=VMEM,
         name="second_conv",
         **common,
-    )(flags, hidden, back, above, below, sums_two, vectors[3], vectors[4], weight_two, vectors[5], features)
+    )(flags, hidden, back, above, below, sums_two, vectors, weight_two, features)
 
 
 def solution(mesh):

time: 104 us -> 107 us (1.029)
  waiting for transfers between devices: 29.2 us -> 30.8 us
  Pallas kernels: 12.7 us -> 14 us
  local copies, waits for them, and re-layouts: 3.08 us -> 1.81 us
    all_to_all x1 -> x2, waiting for transfers between devices: 11.5 us -> 13.1 us  [exchanged(): lax.all_to_all(copies.reshape(count, 1, C), axes, split_axis=0, concat_ax...]
    pallas_call x3 -> x5, Pallas kernels: 12.6 us -> 13.9 us  [the longest x1 5.91 us: body(): pl.pallas_call(functools.partial(second_conv_kernel, devices), out_shape=...]
    unnamed x22 -> x20, local copies, waits for them, and re-layouts: 3.08 us -> 1.81 us
    all_to_all x1 -> x2, blocking collectives: 23.2 us -> 24.1 us  [exchanged(): lax.all_to_all(copies.reshape(count, 1, C), axes, split_axis=0, concat_ax...]
    all_to_all x1 -> x2, starting transfers between devices: 17 us -> 17.8 us  [exchanged(): lax.all_to_all(copies.reshape(count, 1, C), axes, split_axis=0, concat_ax...]
  transfers between devices with their start and end apart: 7 -> 8, of which waited for: 5 -> 6; matrix products, arithmetic and copies ran while one was open for 0% -> 0% of each run, Pallas kernels for 0% -> 1%
where the time goes in v4:
time: 107 us
  starting transfers between devices  35.6 us (33%)
  waiting for transfers between devices  30.8 us (29%)
  blocking collectives  24.1 us (23%)
  Pallas kernels  14 us (13%)
  local copies, waits for them, and re-layouts  1.81 us (2%)
    all_to_all x2, blocking collectives, exchanged(): lax.all_to_all(copies.reshape(count, 1, C), axes, split_axis=0, concat_ax...  24.1 us
    ppermute x6, starting transfers between devices, shifted(): lax.ppermute(block, axes, [(i, i + step) for i in range(count) if 0 <= i...  17.9 us
    all_to_all x2, starting transfers between devices, exchanged(): lax.all_to_all(copies.reshape(count, 1, C), axes, split_axis=0, concat_ax...  17.8 us
    ppermute x6, waiting for transfers between devices, shifted(): lax.ppermute(block, axes, [(i, i + step) for i in range(count) if 0 <= i...  17.7 us
    all_to_all x2, waiting for transfers between devices, exchanged(): lax.all_to_all(copies.reshape(count, 1, C), axes, split_axis=0, concat_ax...  13.1 us
    pallas_call x1, Pallas kernels, body(): pl.pallas_call(functools.partial(second_conv_kernel, devices), out_shape=...  5.91 us
    pallas_call x1, Pallas kernels, body(): pl.pallas_call(functools.partial(first_conv_kernel, devices), out_shape=(...  5.63 us
  transfers between devices with their start and end apart: 8, of which 6 were waited for; matrix products, arithmetic and copies ran while one was open for 0% of the time, Pallas kernels for 1%

profile of v4, /device:TPU:1, one launch (start us, length us, event | category | flops | bytes accessed | tf_op | source)
XLA Modules:
  0.0 106.6 jit_solution(7532260858525381056)
XLA Ops:
  0.0 0.0 copy-start.7
  0.0 0.0 copy-start.8
  0.0 0.0 copy-start.9
  0.0 0.0 copy-start.4
  0.0 0.0 copy-start.5
  0.0 0.0 copy-start.6
  0.0 0.6 copy-done.7
  0.7 0.0 copy-done.8
  0.7 0.0 copy-done.9
  0.7 0.0 copy-done.4
  0.7 0.0 copy-done.5
  0.7 0.0 copy-done.6
  0.7 0.0 copy-start
  0.7 1.1 %copy-done = bf16[4,2,320,128]{3,2,1,0:T(8,128)(2,1)S(1)} copy-done((bf16[4,2,320,128]{3,2,1,0:T(8,128)(2,1)S(1)}, bf16[4,2,320,128]{3,2,1,0:T(8,128)(2,1)}, u32[]{:S(2)}) %copy-start) | copy-done | bytes 655384
  1.8 1.2 %moments.1 = (bf16[4,1,320,128]{3,2,1,0:T(8,128)(2,1)S(1)}, bf16[4,1,320,128]{3,2,1,0:T(8,128)(2,1)S(1)}, f32[32,128]{1,0:T(8,128)}, f32[8,128]{1,0:T(8,128)S(1)}) custom-call(bf16[4,2,320,128]{3,2,1,0:T(8,128)(2,1)S(1)} %copy-done, f32[1,128]{1,0:T(1,128)S(1)} %bitcast.31, f32[1,128]{1,0:T(1,128)S(1)} %bitcast.32, f32[1,128]{1,0:T(1,128)S(1)} %bitcast.33, ...), custom_call_target="tpu_custom_call" | custom-call | tf_op jit(solution)/shard_map/moments/pallas_call | solution.py:269
  3.0 3.9 %collective-permute-start = (bf16[4,1,320,128]{3,2,1,0:T(8,128)(2,1)S(1)}, bf16[4,1,320,128]{3,2,1,0:T(8,128)(2,1)S(1)}, u32[]{:S(2)}, u32[]{:S(2)}) collective-permute-start(bf16[4,1,320,128]{3,2,1,0:T(8,128)(2,1)S(1)} %get-tuple-element.13), channel_id=1, source_target_pairs={{0,1},{1,2},{2,3},{3,4},{4,5},{5,6},{6,7},{7,8},{8,9},{9,10},{10,1... | collective-permute-start | bytes 983048 | tf_op jit(solution)/shard_map/ppermute | solution.py:213
  7.0 0.0 copy-start.1
  7.0 0.0 copy-start.2
  7.0 1.4 %collective-permute-start.1 = (bf16[4,1,320,128]{3,2,1,0:T(8,128)(2,1)S(1)}, bf16[4,1,320,128]{3,2,1,0:T(8,128)(2,1)S(1)}, u32[]{:S(2)}, u32[]{:S(2)}) collective-permute-start(bf16[4,1,320,128]{3,2,1,0:T(8,128)(2,1)S(1)} %get-tuple-element.14), channel_id=1, source_target_pairs={{1,0},{2,1},{3,2},{4,3},{5,4},{6,5},{7,6},{8,7},{9,8},{10,9},{11,1... | collective-permute-start | bytes 983048 | tf_op jit(solution)/shard_map/ppermute | solution.py:213
  8.4 4.9 %collective-permute-done.above_ref = bf16[4,1,320,128]{3,2,1,0:T(8,128)(2,1)S(1)} collective-permute-done((bf16[4,1,320,128]{3,2,1,0:T(8,128)(2,1)S(1)}, bf16[4,1,320,128]{3,2,1,0:T(8,128)(2,1)S(1)}, u32[]{:S(2)}, u32[]{:S(2)}) %collective-permute-start) | collective-permute-done | bytes 327712 | tf_op jit(solution)/shard_map/ppermute | solution.py:213
  13.3 4.0 %collective-permute-done.1.below_ref = bf16[4,1,320,128]{3,2,1,0:T(8,128)(2,1)S(1)} collective-permute-done((bf16[4,1,320,128]{3,2,1,0:T(8,128)(2,1)S(1)}, bf16[4,1,320,128]{3,2,1,0:T(8,128)(2,1)S(1)}, u32[]{:S(2)}, u32[]{:S(2)}) %collective-permute-start.1) | collective-permute-done | bytes 327712 | tf_op jit(solution)/shard_map/ppermute | solution.py:213
  17.4 4.9 %collective-permute-start.2 = (bf16[2,4,320,128]{3,2,1,0:T(8,128)(2,1)S(1)}, bf16[2,4,320,128]{3,2,1,0:T(8,128)(2,1)S(1)}, u32[]{:S(2)}, u32[]{:S(2)}) collective-permute-start(bf16[2,4,320,128]{3,2,1,0:T(8,128)(2,1)S(1)} %last_frames.2), channel_id=1, source_target_pairs={{0,32},{32,64},{64,96},{96,128},{128,160},{160,192},{192,224},{1,3... | collective-permute-start | bytes 1966088 | tf_op jit(solution)/shard_map/ppermute | solution.py:213
  22.3 12.3 %all-to-all-start = ((f32[32,1,128]{2,1,0:T(1,128)}), f32[32,1,128]{2,1,0:T(1,128)S(1)}, u32[]{:S(2)}, u32[]{:S(2)}) async-start(f32[32,1,128]{2,1,0:T(1,128)} %bitcast.10), calls=%async_computation | async-start | bytes 32768 | tf_op jit(solution)/shard_map/all_to_all | solution.py:234
  34.6 8.6 %all-to-all-done = f32[32,1,128]{2,1,0:T(1,128)S(1)} async-done(((f32[32,1,128]{2,1,0:T(1,128)}), f32[32,1,128]{2,1,0:T(1,128)S(1)}, u32[]{:S(2)}, u32[]{:S(2)}) %all-to-all-start) | async-done | bytes 16416 | tf_op jit(solution)/shard_map/all_to_all | solution.py:234
  43.2 0.9 relay.2
  44.1 5.5 %all-to-all-start.1 = ((f32[8,1,128]{2,1,0:T(1,128)}), f32[8,1,128]{2,1,0:T(1,128)S(1)}, u32[]{:S(2)}, u32[]{:S(2)}) async-start(f32[8,1,128]{2,1,0:T(1,128)} %bitcast.13), calls=%async_computation.1 | async-start | bytes 8192 | tf_op jit(solution)/shard_map/all_to_all | solution.py:234
  49.6 0.1 add_convert_fusion.flags_ref
  49.6 4.4 %all-to-all-done.1 = f32[8,1,128]{2,1,0:T(1,128)S(1)} async-done(((f32[8,1,128]{2,1,0:T(1,128)}), f32[8,1,128]{2,1,0:T(1,128)S(1)}, u32[]{:S(2)}, u32[]{:S(2)}) %all-to-all-start.1) | async-done | bytes 4128 | tf_op jit(solution)/shard_map/all_to_all | solution.py:234
  54.1 0.0 collective-permute-done.2.back_ref
  54.1 0.0 copy-done.1
  54.1 0.0 copy-done.2
  54.1 5.6 %first_conv.1 = (bf16[4,2,320,128]{3,2,1,0:T(8,128)(2,1)S(1)}, bf16[4,1,320,128]{3,2,1,0:T(8,128)(2,1)S(1)}, bf16[4,1,320,128]{3,2,1,0:T(8,128)(2,1)S(1)}, f32[32,128]{1,0:T(8,128)S(1)}) custom-call(s32[3]{0:T(128)S(1)} %add_convert_fusion.flags_ref, bf16[4,2,320,128]{3,2,1,0:T(8,128)(2,1)S(1)} %copy-done.1, ...), custom_call_target="tpu_custom_call" | custom-call | tf_op jit(solution)/shard_map/first_conv/pallas_call | solution.py:279
  59.7 2.2 %collective-permute-start.3 = (bf16[4,1,320,128]{3,2,1,0:T(8,128)(2,1)S(1)}, bf16[4,1,320,128]{3,2,1,0:T(8,128)(2,1)S(1)}, u32[]{:S(2)}, u32[]{:S(2)}) collective-permute-start(bf16[4,1,320,128]{3,2,1,0:T(8,128)(2,1)S(1)} %get-tuple-element.18), channel_id=1, source_target_pairs={{0,1},{1,2},{2,3},{3,4},{4,5},{5,6},{6,7},{7,8},{8,9},{9,10},{10,1... | collective-permute-start | bytes 983048 | tf_op jit(solution)/shard_map/ppermute | solution.py:213
  61.9 1.3 %collective-permute-start.4 = (bf16[4,1,320,128]{3,2,1,0:T(8,128)(2,1)S(1)}, bf16[4,1,320,128]{3,2,1,0:T(8,128)(2,1)S(1)}, u32[]{:S(2)}, u32[]{:S(2)}) collective-permute-start(bf16[4,1,320,128]{3,2,1,0:T(8,128)(2,1)S(1)} %get-tuple-element.19), channel_id=1, source_target_pairs={{1,0},{2,1},{3,2},{4,3},{5,4},{6,5},{7,6},{8,7},{9,8},{10,9},{11,1... | collective-permute-start | bytes 983048 | tf_op jit(solution)/shard_map/ppermute | solution.py:213
  63.2 5.0 %collective-permute-done.3.above_ref = bf16[4,1,320,128]{3,2,1,0:T(8,128)(2,1)S(1)} collective-permute-done((bf16[4,1,320,128]{3,2,1,0:T(8,128)(2,1)S(1)}, bf16[4,1,320,128]{3,2,1,0:T(8,128)(2,1)S(1)}, u32[]{:S(2)}, u32[]{:S(2)}) %collective-permute-start.3) | collective-permute-done | bytes 327712 | tf_op jit(solution)/shard_map/ppermute | solution.py:213
  68.2 3.9 %collective-permute-done.4.below_ref = bf16[4,1,320,128]{3,2,1,0:T(8,128)(2,1)S(1)} collective-permute-done((bf16[4,1,320,128]{3,2,1,0:T(8,128)(2,1)S(1)}, bf16[4,1,320,128]{3,2,1,0:T(8,128)(2,1)S(1)}, u32[]{:S(2)}, u32[]{:S(2)}) %collective-permute-start.4) | collective-permute-done | bytes 327712 | tf_op jit(solution)/shard_map/ppermute | solution.py:213
  72.0 0.0 copy-start.3
  72.1 4.2 %collective-permute-start.5 = (bf16[2,4,320,128]{3,2,1,0:T(8,128)(2,1)S(1)}, bf16[2,4,320,128]{3,2,1,0:T(8,128)(2,1)S(1)}, u32[]{:S(2)}, u32[]{:S(2)}) collective-permute-start(bf16[2,4,320,128]{3,2,1,0:T(8,128)(2,1)S(1)} %last_frames.3), channel_id=1, source_target_pairs={{0,32},{32,64},{64,96},{96,128},{128,160},{160,192},{192,224},{1,3... | collective-permute-start | bytes 1966088 | tf_op jit(solution)/shard_map/ppermute | solution.py:213
  76.2 14.3 %all_to_all.20 = f32[32,1,128]{2,1,0:T(1,128)S(1)} all-to-all(f32[32,1,128]{2,1,0:T(1,128)S(1)} %bitcast.29), channel_id=1, replica_groups=mesh['y'=4,'c'=2,'z'=8,'x'=4] {'y','z'}, dimensions={0} | all-to-all | bytes 32768 | tf_op jit(solution)/shard_map/all_to_all | solution.py:234
  90.6 0.3 relay.3
  90.9 9.8 %all_to_all.21 = f32[8,1,128]{2,1,0:T(1,128)S(1)} all-to-all(f32[8,1,128]{2,1,0:T(1,128)S(1)} %bitcast.28), channel_id=1, replica_groups=mesh['y'=4,'c'=2,'z'=8,'x'=4] {'c','x'}, dimensions={0} | all-to-all | bytes 8192 | tf_op jit(solution)/shard_map/all_to_all | solution.py:234
  100.7 0.0 collective-permute-done.5.back_ref
  100.7 0.0 copy-done.3
  100.7 5.9 %second_conv.1 = bf16[4,2,320,128]{3,2,1,0:T(8,128)(2,1)} custom-call(s32[3]{0:T(128)S(1)} %add_convert_fusion.flags_ref, bf16[4,2,320,128]{3,2,1,0:T(8,128)(2,1)S(1)} %get-tuple-element.17.own_ref, bf16[2,4,320,128]{3,2,1,0:T(8,128)(2,1)S(1)} %collective-permute-done.5.back_ref, bf16[4,1,320,128]{3,2,1,0:T(8,128)(2,1)S(1)} %collective-permute-done.3.above_ref, ...), custom_call_target="tpu_custom_call" | custom-call | tf_op jit(solution)/shard_map/second_conv/pallas_call | solution.py:290
  (2 shorter events, 0.1 us)
Async XLA Ops:
  0.0 0.7 copy-start.7
  0.0 0.7 copy-start.8
  0.0 0.7 copy-start.9
  0.0 0.7 copy-start.4
  0.0 0.7 copy-start.5
  0.0 0.7 copy-start.6
  0.7 1.1 %copy-start = (bf16[4,2,320,128]{3,2,1,0:T(8,128)(2,1)S(1)}, bf16[4,2,320,128]{3,2,1,0:T(8,128)(2,1)}, u32[]{:S(2)}) copy-start(bf16[4,2,320,128]{3,2,1,0:T(8,128)(2,1)} %features_ref.1) | copy-start | bytes 1966084
  3.0 10.3 %collective-permute-start = (bf16[4,1,320,128]{3,2,1,0:T(8,128)(2,1)S(1)}, bf16[4,1,320,128]{3,2,1,0:T(8,128)(2,1)S(1)}, u32[]{:S(2)}, u32[]{:S(2)}) collective-permute-start(bf16[4,1,320,128]{3,2,1,0:T(8,128)(2,1)S(1)} %get-tuple-element.13), channel_id=1, source_target_pairs={{0,1},{1,2},{2,3},{3,4},{4,5},{5,6},{6,7},{7,8},{8,9},{9,10},{10,1... | collective-permute-start | bytes 983048 | tf_op jit(solution)/shard_map/ppermute | solution.py:213
  7.0 47.1 %copy-start.1 = (bf16[4,2,320,128]{3,2,1,0:T(8,128)(2,1)S(1)}, bf16[4,2,320,128]{3,2,1,0:T(8,128)(2,1)}, u32[]{:S(2)}) copy-start(bf16[4,2,320,128]{3,2,1,0:T(8,128)(2,1)} %features_ref.1) | copy-start | bytes 1966084
  7.0 47.1 %copy-start.2 = (bf16[3456,128]{1,0:T(8,128)(2,1)S(1)}, bf16[3456,128]{1,0:T(8,128)(2,1)}, u32[]{:S(2)}) copy-start(bf16[3456,128]{1,0:T(8,128)(2,1)} %w_ref.2) | copy-start | bytes 2654212
  7.0 10.3 %collective-permute-start.1 = (bf16[4,1,320,128]{3,2,1,0:T(8,128)(2,1)S(1)}, bf16[4,1,320,128]{3,2,1,0:T(8,128)(2,1)S(1)}, u32[]{:S(2)}, u32[]{:S(2)}) collective-permute-start(bf16[4,1,320,128]{3,2,1,0:T(8,128)(2,1)S(1)} %get-tuple-element.14), channel_id=1, source_target_pairs={{1,0},{2,1},{3,2},{4,3},{5,4},{6,5},{7,6},{8,7},{9,8},{10,9},{11,1... | collective-permute-start | bytes 983048 | tf_op jit(solution)/shard_map/ppermute | solution.py:213
  17.4 36.7 %collective-permute-start.2 = (bf16[2,4,320,128]{3,2,1,0:T(8,128)(2,1)S(1)}, bf16[2,4,320,128]{3,2,1,0:T(8,128)(2,1)S(1)}, u32[]{:S(2)}, u32[]{:S(2)}) collective-permute-start(bf16[2,4,320,128]{3,2,1,0:T(8,128)(2,1)S(1)} %last_frames.2), channel_id=1, source_target_pairs={{0,32},{32,64},{64,96},{96,128},{128,160},{160,192},{192,224},{1,3... | collective-permute-start | bytes 1966088 | tf_op jit(solution)/shard_map/ppermute | solution.py:213
  22.3 20.9 %all-to-all-start = ((f32[32,1,128]{2,1,0:T(1,128)}), f32[32,1,128]{2,1,0:T(1,128)S(1)}, u32[]{:S(2)}, u32[]{:S(2)}) async-start(f32[32,1,128]{2,1,0:T(1,128)} %bitcast.10), calls=%async_computation | async-start | bytes 32768 | tf_op jit(solution)/shard_map/all_to_all | solution.py:234
  44.1 10.0 %all-to-all-start.1 = ((f32[8,1,128]{2,1,0:T(1,128)}), f32[8,1,128]{2,1,0:T(1,128)S(1)}, u32[]{:S(2)}, u32[]{:S(2)}) async-start(f32[8,1,128]{2,1,0:T(1,128)} %bitcast.13), calls=%async_computation.1 | async-start | bytes 8192 | tf_op jit(solution)/shard_map/all_to_all | solution.py:234
  59.7 8.4 %collective-permute-start.3 = (bf16[4,1,320,128]{3,2,1,0:T(8,128)(2,1)S(1)}, bf16[4,1,320,128]{3,2,1,0:T(8,128)(2,1)S(1)}, u32[]{:S(2)}, u32[]{:S(2)}) collective-permute-start(bf16[4,1,320,128]{3,2,1,0:T(8,128)(2,1)S(1)} %get-tuple-element.18), channel_id=1, source_target_pairs={{0,1},{1,2},{2,3},{3,4},{4,5},{5,6},{6,7},{7,8},{8,9},{9,10},{10,1... | collective-permute-start | bytes 983048 | tf_op jit(solution)/shard_map/ppermute | solution.py:213
  61.9 10.1 %collective-permute-start.4 = (bf16[4,1,320,128]{3,2,1,0:T(8,128)(2,1)S(1)}, bf16[4,1,320,128]{3,2,1,0:T(8,128)(2,1)S(1)}, u32[]{:S(2)}, u32[]{:S(2)}) collective-permute-start(bf16[4,1,320,128]{3,2,1,0:T(8,128)(2,1)S(1)} %get-tuple-element.19), channel_id=1, source_target_pairs={{1,0},{2,1},{3,2},{4,3},{5,4},{6,5},{7,6},{8,7},{9,8},{10,9},{11,1... | collective-permute-start | bytes 983048 | tf_op jit(solution)/shard_map/ppermute | solution.py:213
  72.0 28.7 %copy-start.3 = (bf16[3456,128]{1,0:T(8,128)(2,1)S(1)}, bf16[3456,128]{1,0:T(8,128)(2,1)}, u32[]{:S(2)}) copy-start(bf16[3456,128]{1,0:T(8,128)(2,1)} %w_ref.3) | copy-start | bytes 2654212
  72.1 28.6 %collective-permute-start.5 = (bf16[2,4,320,128]{3,2,1,0:T(8,128)(2,1)S(1)}, bf16[2,4,320,128]{3,2,1,0:T(8,128)(2,1)S(1)}, u32[]{:S(2)}, u32[]{:S(2)}) collective-permute-start(bf16[2,4,320,128]{3,2,1,0:T(8,128)(2,1)S(1)} %last_frames.3), channel_id=1, source_target_pairs={{0,32},{32,64},{64,96},{96,128},{128,160},{160,192},{192,224},{1,3... | collective-permute-start | bytes 1966088 | tf_op jit(solution)/shard_map/ppermute | solution.py:213

commit v5 on v4

--- a/solution.py
+++ b/solution.py
@@ -87,36 +87,23 @@
     return (half + half * jnp.tanh(half)).astype(jnp.bfloat16)
 
 
-def fill(act_ref, own_ref, back_ref, above_ref, below_ref, flags_ref, scale, offset):
-    earlier = back_ref.shape[0]
-    frames, rows, width = act_ref.shape[0], act_ref.shape[1], act_ref.shape[2]
-    for f in range(frames):
-        for r in range(rows):
-            if f < earlier:
-                source = back_ref[f, r]
-            elif r == 0:
-                source = above_ref[f - earlier, 0]
-            elif r == rows - 1:
-                source = below_ref[f - earlier, 0]
-            else:
-                source = own_ref[f - earlier, r - 1]
-            act_ref[f, r] = activated(source, scale, offset)
-
-    @pl.when(flags_ref[1] == 1)
-    def _():
-        act_ref[:, 0] = jnp.zeros((frames, width, C), jnp.bfloat16)
-
-    @pl.when(flags_ref[2] == 1)
-    def _():
-        act_ref[:, rows - 1] = jnp.zeros((frames, width, C), jnp.bfloat16)
-
-    @pl.when(flags_ref[0] == 1)
-    def _():
+def fill(act_ref, own_ref, rows_ref, back_ref, diagonal_ref, own_at, back_at, scale, offset):
+    earlier, frames, rows = back_ref.shape[0], own_ref.shape[0], own_ref.shape[1]
+    for r in range(rows):
         for f in range(earlier):
-            act_ref[f] = act_ref[earlier]
-
-
-def taps(act_ref, w_ref, start, count):
+            act_ref[f, back_at + r] = activated(back_ref[f, r], scale, offset)
+            act_ref[f, rows - back_at + r] = activated(diagonal_ref[f, r], scale, offset)
+        for f in range(frames):
+            act_ref[f + earlier, own_at + r] = activated(own_ref[f, r], scale, offset)
+            act_ref[f + earlier, rows - own_at + r] = activated(rows_ref[f, r], scale, offset)
+
+
+def repeat_first(act_ref, earlier):
+    for f in range(earlier):
+        act_ref[f] = act_ref[earlier]
+
+
+def taps(act_ref, w_ref, start, count, wraps=None):
     width = act_ref.shape[2]
     cells = count * width
     pieces = [
@@ -125,17 +112,21 @@
     left = jnp.concatenate(pieces, axis=1)
     column = lax.broadcasted_iota(jnp.int32, (cells, 2 * C), 0) % width
 
-    def block(i, j, k):
+    def block(i, r, out, k):
+        j = r - out
         if not 0 <= j < 3:
             return jnp.zeros((C, C), jnp.bfloat16)
         first = ((i * 3 + j) * 3 + k) * C
-        return w_ref[first : first + C, :]
+        found = w_ref[first : first + C, :]
+        if wraps is not None and r // 2 != out:
+            return jnp.where(wraps, jnp.zeros_like(found), found)
+        return found
 
     total = None
     for k in (1, 0, 2):
         right = jnp.concatenate(
             [
-                jnp.concatenate([block(i, r, k), block(i, r - 1, k)], axis=1)
+                jnp.concatenate([block(i, r, 0, k), block(i, r, 1, k)], axis=1)
                 for i in range(3)
                 for r in range(4)
             ],
@@ -150,16 +141,15 @@
     return total
 
 
-def hand_out(ref, top_ref, bottom_ref, sums_ref):
-    rows = ref.shape[1]
-    top_ref[:, 0] = ref[:, 0]
-    bottom_ref[:, 0] = ref[:, rows - 1]
+def hand_out(ref, last_ref, sums_ref):
+    earlier = last_ref.shape[0]
+    last_ref[...] = ref[ref.shape[0] - earlier :]
     sums_ref[...] = jnp.broadcast_to(packed_sums(ref)[:1], sums_ref.shape)
 
 
 def moments_kernel(x_ref, *refs):
-    vectors, (top_ref, bottom_ref, sums_ref, vectors_ref) = refs[:-4], refs[-4:]
-    hand_out(x_ref, top_ref, bottom_ref, sums_ref)
+    vectors, (last_ref, sums_ref, vectors_ref) = refs[:-3], refs[-3:]
+    hand_out(x_ref, last_ref, sums_ref)
     for i, vector in enumerate(vectors):
         vectors_ref[i : i + 1] = vector[...]
 
@@ -170,27 +160,52 @@
 
 
 def first_conv_kernel(
-    devices, flags_ref, own_ref, back_ref, above_ref, below_ref, sums_ref, vectors_ref, w_ref,
-    hidden_ref, top_ref, bottom_ref, next_ref, act_ref,
+    devices, place_ref, own_ref, rows_ref, back_ref, diagonal_ref, sums_ref, vectors_ref, w_ref,
+    hidden_ref, last_ref, next_ref, act_ref,
 ):
     frames, rows, width, _ = own_ref.shape
+    core, tm, row, last_row = place_ref[0], place_ref[1], place_ref[2], place_ref[3]
+    side = rows * (1 - core)
     scale, offset = scale_and_offset(sums_ref, vectors_ref, 0, frames * rows * width, devices)
-    fill(act_ref, own_ref, back_ref, above_ref, below_ref, flags_ref, scale, offset)
+    fill(act_ref, own_ref, rows_ref, back_ref, diagonal_ref, side, side, scale, offset)
+
+    @pl.when(tm == 0)
+    def _():
+        repeat_first(act_ref, back_ref.shape[0])
+
+    wraps = row == core * last_row
     for f in range(frames):
-        total = taps(act_ref, w_ref, f, 1)
+        total = taps(act_ref, w_ref, f, 1, wraps)
         for r in range(rows):
             value = total[:, r * C : (r + 1) * C] + vectors_ref[2:3]
             hidden_ref[f, r] = value.astype(jnp.bfloat16)
-    hand_out(hidden_ref, top_ref, bottom_ref, next_ref)
+    hand_out(hidden_ref, last_ref, next_ref)
 
 
 def second_conv_kernel(
-    devices, flags_ref, own_ref, back_ref, above_ref, below_ref, sums_ref, vectors_ref, w_ref,
+    devices, place_ref, own_ref, rows_ref, back_ref, diagonal_ref, sums_ref, vectors_ref, w_ref,
     features_ref, out_ref, act_ref,
 ):
     frames, rows, width, _ = own_ref.shape
+    core, tm, row, last_row = place_ref[0], place_ref[1], place_ref[2], place_ref[3]
     scale, offset = scale_and_offset(sums_ref, vectors_ref, 3, frames * rows * width, devices)
-    fill(act_ref, own_ref, back_ref, above_ref, below_ref, flags_ref, scale, offset)
+    fill(
+        act_ref, own_ref, rows_ref, back_ref, diagonal_ref, rows * core, rows * (1 - core), scale, offset
+    )
+    outside = jnp.zeros((act_ref.shape[0], width, C), jnp.bfloat16)
+
+    @pl.when(row == 0)
+    def _():
+        act_ref[:, 0] = outside
+
+    @pl.when(row == last_row)
+    def _():
+        act_ref[:, act_ref.shape[1] - 1] = outside
+
+    @pl.when(tm == 0)
+    def _():
+        repeat_first(act_ref, back_ref.shape[0])
+
     for f in range(frames):
         total = taps(act_ref, w_ref, f, 1)
         for r in range(rows):
@@ -199,34 +214,22 @@
             out_ref[f, r] = value.astype(jnp.bfloat16)
 
 
-def last_kernel(own_ref, above_ref, below_ref, last_ref):
-    earlier, rows = last_ref.shape[0], last_ref.shape[1]
-    for f in range(earlier):
-        source = own_ref.shape[0] - earlier + f
-        last_ref[f, 0] = above_ref[source, 0]
-        last_ref[f, 1 : rows - 1] = own_ref[source]
-        last_ref[f, rows - 1] = below_ref[source, 0]
-
-
-def shifted(block, axes, step):
-    count = lax.axis_size(axes)
-    return lax.ppermute(block, axes, [(i, i + step) for i in range(count) if 0 <= i + step < count])
-
-
-def neighbours(own, top, bottom):
-    _, rows, width, _ = own.shape
-    above = shifted(bottom, ROWS, 1)
-    below = shifted(top, ROWS, -1)
-    last = pl.pallas_call(
-        last_kernel,
-        out_shape=jax.ShapeDtypeStruct((2, rows + 2, width, C), own.dtype),
-        in_specs=[VMEM] * 3,
-        out_specs=VMEM,
-        name="last_frames",
-        compiler_params=pltpu.CompilerParams(vmem_limit_bytes=8 * MIB),
-    )(own, above, below)
-    back = shifted(last, TM, 1)
-    return back, above, below
+def sent(block, tm_step, row_steps):
+    tms, rows = lax.axis_size(TM), lax.axis_size(ROWS)
+    route = []
+    for t in range(tms):
+        for r in range(rows):
+            source = (t - tm_step, (r + row_steps[t % 2]) % rows)
+            if source[0] >= 0:
+                route.append((source[0] * rows + source[1], t * rows + r))
+    return lax.ppermute(block, EVERY, route)
+
+
+def neighbours(own, last, row_steps):
+    beside = sent(own, 0, row_steps)
+    back = sent(last, 1, (0, 0))
+    diagonal = sent(last, 1, (-1, 1))
+    return beside, back, diagonal
 
 
 def exchanged(copies, axes):
@@ -250,42 +253,41 @@
 
 def body(features, gain_one, shift_one, weight_one, bias_one, gain_two, shift_two, weight_two, bias_two):
     frames, rows, width, _ = features.shape
-    copies = jax.ShapeDtypeStruct((lax.axis_size(FAR), C), jnp.float32)
     devices = lax.axis_size(EVERY)
     tile_cells = frames * rows * width
+    copies = jax.ShapeDtypeStruct((lax.axis_size(FAR), C), jnp.float32)
     tile = jax.ShapeDtypeStruct(features.shape, jnp.bfloat16)
-    edge = jax.ShapeDtypeStruct((frames, 1, width, C), jnp.bfloat16)
-    row = lax.axis_index(ROWS)
-    flags = jnp.stack(
-        [lax.axis_index(TM) == 0, row == 0, row == lax.axis_size(ROWS) - 1]
+    two = jax.ShapeDtypeStruct((2, rows, width, C), jnp.bfloat16)
+    place = jnp.stack(
+        [lax.axis_index("c"), lax.axis_index(TM), lax.axis_index(ROWS), lax.axis_size(ROWS) - 1]
     ).astype(jnp.int32)
     common = dict(
         scratch_shapes=[pltpu.VMEM((frames + 2, rows + 2, width, C), jnp.bfloat16)],
-        compiler_params=pltpu.CompilerParams(vmem_limit_bytes=32 * MIB),
+        compiler_params=pltpu.CompilerParams(vmem_limit_bytes=20 * MIB),
     )
     specs = [SMEM] + [VMEM] * 7
     vectors = [v.reshape(1, C) for v in (gain_one, shift_one, bias_one, gain_two, shift_two, bias_two)]
 
-    top, bottom, sums, vectors = pl.pallas_call(
+    last, sums, vectors = pl.pallas_call(
         moments_kernel,
-        out_shape=(edge, edge, copies, jax.ShapeDtypeStruct((8, C), jnp.float32)),
+        out_shape=(two, copies, jax.ShapeDtypeStruct((8, C), jnp.float32)),
         in_specs=[VMEM] * 7,
-        out_specs=(VMEM,) * 4,
+        out_specs=(VMEM,) * 3,
         name="moments",
         compiler_params=pltpu.CompilerParams(vmem_limit_bytes=8 * MIB),
     )(features, *vectors)
-    back, above, below = neighbours(features, top, bottom)
+    around = neighbours(features, last, (-1, 1))
     sums = everywhere(sums, tile_cells)
-    hidden, top, bottom, sums_two = pl.pallas_call(
+    hidden, last, sums_two = pl.pallas_call(
         functools.partial(first_conv_kernel, devices),
-        out_shape=(tile, edge, edge, copies),
+        out_shape=(tile, two, copies),
         in_specs=specs,
-        out_specs=(VMEM,) * 4,
+        out_specs=(VMEM,) * 3,
         name="first_conv",
         **common,
-    )(flags, features, back, above, below, sums, vectors, weight_one)
-
-    back, above, below = neighbours(hidden, top, bottom)
+    )(place, features, *around, sums, vectors, weight_one)
+
+    around = neighbours(hidden, last, (1, -1))
     sums_two = everywhere(sums_two, tile_cells)
     return pl.pallas_call(
         functools.partial(second_conv_kernel, devices),
@@ -294,7 +296,7 @@
         out_specs=VMEM,
         name="second_conv",
         **common,
-    )(flags, hidden, back, above, below, sums_two, vectors, weight_two, features)
+    )(place, hidden, *around, sums_two, vectors, weight_two, features)
 
 
 def solution(mesh):

time: 107 us -> 86 us (0.80)
  waiting for transfers between devices: 30.8 us -> 13 us
  blocking collectives: 24.1 us -> 21 us
  starting transfers between devices: 35.6 us -> 34.4 us
  local copies, waits for them, and re-layouts: 1.81 us -> 2.97 us
    ppermute x6, waiting for transfers between devices: 17.7 us -> 0.02 us  [sent(): return lax.ppermute(block, EVERY, route)]
    all_to_all x2, starting transfers between devices: 17.8 us -> 10.7 us  [exchanged(): lax.all_to_all(copies.reshape(count, 1, C), axes, split_axis=0, concat_ax...]
    ppermute x6, starting transfers between devices: 17.9 us -> 23.7 us  [sent(): return lax.ppermute(block, EVERY, route)]
    all_to_all x2, blocking collectives: 24.1 us -> 21 us  [exchanged(): lax.all_to_all(copies.reshape(count, 1, C), axes, split_axis=0, concat_ax...]
    unnamed x20, local copies, waits for them, and re-layouts: 1.81 us -> 2.97 us
  transfers between devices with their start and end apart: 8 -> 8, of which waited for: 6 -> 2; matrix products, arithmetic and copies ran while one was open for 0% -> 0% of each run, Pallas kernels for 1% -> 3%
where the time goes in v5:
time: 86 us; the launch traced here: 85.5 us
  starting transfers between devices  34.4 us (40%)
  blocking collectives  21 us (24%)
  Pallas kernels  13.9 us (16%)
  waiting for transfers between devices  13 us (15%)
  local copies, waits for them, and re-layouts  2.97 us (3%)
    ppermute x6, starting transfers between devices, sent(): return lax.ppermute(block, EVERY, route)  23.7 us
    all_to_all x2, blocking collectives, exchanged(): lax.all_to_all(copies.reshape(count, 1, C), axes, split_axis=0, concat_ax...  21 us
    all_to_all x2, waiting for transfers between devices, exchanged(): lax.all_to_all(copies.reshape(count, 1, C), axes, split_axis=0, concat_ax...  13 us
    all_to_all x2, starting transfers between devices, exchanged(): lax.all_to_all(copies.reshape(count, 1, C), axes, split_axis=0, concat_ax...  10.7 us
    pallas_call x1, Pallas kernels, body(): pl.pallas_call(functools.partial(second_conv_kernel, devices), out_shape=...  5.91 us
    pallas_call x1, Pallas kernels, body(): pl.pallas_call(functools.partial(first_conv_kernel, devices), out_shape=(...  5.58 us
    unnamed x20, local copies, waits for them, and re-layouts  2.97 us
  transfers between devices with their start and end apart: 8, of which 2 were waited for; matrix products, arithmetic and copies ran while one was open for 0% of the time, Pallas kernels for 3%

profile of v5, /device:TPU:1, one launch (start us, length us, event | category | flops | bytes accessed | tf_op | source)
XLA Modules:
  0.0 85.5 jit_solution(2641049431339047641)
XLA Ops:
  0.0 8.6 %collective-permute-start = (bf16[4,2,320,128]{3,2,1,0:T(8,128)(2,1)}, bf16[4,2,320,128]{3,2,1,0:T(8,128)(2,1)S(1)}, u32[]{:S(2)}, u32[]{:S(2)}) collective-permute-start(bf16[4,2,320,128]{3,2,1,0:T(8,128)(2,1)} %features_ref.1), channel_id=1, source_target_pairs={{31,0},{0,1},{1,2},{2,3},{3,4},{4,5},{5,6},{6,7},{7,8},{8,9},{9,10... | collective-permute-start | bytes 1966088 | tf_op jit(solution)/shard_map/ppermute | solution.py:225
  8.6 0.0 copy-start.7
  8.6 0.0 copy-start.8
  8.6 0.0 copy-start.9
  8.6 0.0 copy-start.4
  8.6 0.0 copy-start.5
  8.6 0.0 copy-start.6
  8.6 0.6 copy-done.7
  9.2 0.0 copy-done.8
  9.3 0.0 copy-done.9
  9.3 0.0 copy-done.4
  9.3 0.0 copy-done.5
  9.3 0.0 copy-done.6
  9.3 0.0 copy-start
  9.3 1.1 %copy-done = bf16[4,2,320,128]{3,2,1,0:T(8,128)(2,1)S(1)} copy-done((bf16[4,2,320,128]{3,2,1,0:T(8,128)(2,1)S(1)}, bf16[4,2,320,128]{3,2,1,0:T(8,128)(2,1)}, u32[]{:S(2)}) %copy-start) | copy-done | bytes 655384
  10.4 0.0 copy-start.1
  10.4 1.2 %moments.1 = (bf16[2,2,320,128]{3,2,1,0:T(8,128)(2,1)S(1)}, f32[32,128]{1,0:T(8,128)}, f32[8,128]{1,0:T(8,128)S(1)}) custom-call(bf16[4,2,320,128]{3,2,1,0:T(8,128)(2,1)S(1)} %copy-done, f32[1,128]{1,0:T(1,128)S(1)} %bitcast.31, f32[1,128]{1,0:T(1,128)S(1)} %bitcast.32, f32[1,128]{1,0:T(1,128)S(1)} %bitcast.33, f32[1,128]{1,0:T(1,128)S(1)} %bitcast.34, ...), custom_call_target="tpu_custom_call" | custom-call | tf_op jit(solution)/shard_map/moments/pallas_call | solution.py:271
  11.6 1.9 %collective-permute-start.2 = (bf16[2,2,320,128]{3,2,1,0:T(8,128)(2,1)S(1)}, bf16[2,2,320,128]{3,2,1,0:T(8,128)(2,1)S(1)}, u32[]{:S(2)}, u32[]{:S(2)}) collective-permute-start(bf16[2,2,320,128]{3,2,1,0:T(8,128)(2,1)S(1)} %get-tuple-element.11), channel_id=1, source_target_pairs={{1,32},{2,33},{3,34},{4,35},{5,36},{6,37},{7,38},{8,39},{9,40},{10... | collective-permute-start | bytes 983048 | tf_op jit(solution)/shard_map/ppermute | solution.py:225
  13.5 4.0 %collective-permute-start.1 = (bf16[2,2,320,128]{3,2,1,0:T(8,128)(2,1)S(1)}, bf16[2,2,320,128]{3,2,1,0:T(8,128)(2,1)S(1)}, u32[]{:S(2)}, u32[]{:S(2)}) collective-permute-start(bf16[2,2,320,128]{3,2,1,0:T(8,128)(2,1)S(1)} %get-tuple-element.11), channel_id=1, source_target_pairs={{0,32},{1,33},{2,34},{3,35},{4,36},{5,37},{6,38},{7,39},{8,40},{9,... | collective-permute-start | bytes 983048 | tf_op jit(solution)/shard_map/ppermute | solution.py:225
  17.5 5.6 %all-to-all-start = ((f32[32,1,128]{2,1,0:T(1,128)}), f32[32,1,128]{2,1,0:T(1,128)S(1)}, u32[]{:S(2)}, u32[]{:S(2)}) async-start(f32[32,1,128]{2,1,0:T(1,128)} %bitcast.10), calls=%async_computation | async-start | bytes 32768 | tf_op jit(solution)/shard_map/all_to_all | solution.py:237
  23.2 8.6 %all-to-all-done = f32[32,1,128]{2,1,0:T(1,128)S(1)} async-done(((f32[32,1,128]{2,1,0:T(1,128)}), f32[32,1,128]{2,1,0:T(1,128)S(1)}, u32[]{:S(2)}, u32[]{:S(2)}) %all-to-all-start) | async-done | bytes 16416 | tf_op jit(solution)/shard_map/all_to_all | solution.py:237
  31.8 0.9 %relay.2 = f32[8,128]{1,0:T(8,128)} custom-call(f32[32,128]{1,0:T(8,128)S(1)} %bitcast.25), custom_call_target="tpu_custom_call" | custom-call | tf_op jit(solution)/shard_map/relay/pallas_call | solution.py:243
  32.7 5.1 %all-to-all-start.1 = ((f32[8,1,128]{2,1,0:T(1,128)}), f32[8,1,128]{2,1,0:T(1,128)S(1)}, u32[]{:S(2)}, u32[]{:S(2)}) async-start(f32[8,1,128]{2,1,0:T(1,128)} %bitcast.13), calls=%async_computation.1 | async-start | bytes 8192 | tf_op jit(solution)/shard_map/all_to_all | solution.py:237
  37.8 0.1 pad_add_fusion.place_ref
  37.8 4.4 %all-to-all-done.1 = f32[8,1,128]{2,1,0:T(1,128)S(1)} async-done(((f32[8,1,128]{2,1,0:T(1,128)}), f32[8,1,128]{2,1,0:T(1,128)S(1)}, u32[]{:S(2)}, u32[]{:S(2)}) %all-to-all-start.1) | async-done | bytes 4128 | tf_op jit(solution)/shard_map/all_to_all | solution.py:237
  42.3 0.0 collective-permute-done.2.diagonal_ref
  42.3 0.0 collective-permute-done.1.back_ref
  42.3 0.0 collective-permute-done.rows_ref
  42.3 0.0 copy-done.1
  42.3 0.0 copy-start.2
  42.3 1.2 %copy-done.2 = bf16[3456,128]{1,0:T(8,128)(2,1)S(1)} copy-done((bf16[3456,128]{1,0:T(8,128)(2,1)S(1)}, bf16[3456,128]{1,0:T(8,128)(2,1)}, u32[]{:S(2)}) %copy-start.2) | copy-done | bytes 884760
  43.5 0.0 copy-start.3
  43.5 5.6 %first_conv.1 = (bf16[4,2,320,128]{3,2,1,0:T(8,128)(2,1)S(1)}, bf16[2,2,320,128]{3,2,1,0:T(8,128)(2,1)S(1)}, f32[32,128]{1,0:T(8,128)S(1)}) custom-call(s32[4]{0:T(128)S(1)} %pad_add_fusion.place_ref, bf16[4,2,320,128]{3,2,1,0:T(8,128)(2,1)S(1)} %copy-done.1, bf16[4,2,320,128]{3,2,1,0:T(8,128)(2,1)S(1)} %collective-permute-done.rows_ref, ...), custom_call_target="tpu_custom_call" | custom-call | tf_op jit(solution)/shard_map/first_conv/pallas_call | solution.py:281
  49.1 0.3 collective-permute-start.3
  49.4 4.0 %collective-permute-start.5 = (bf16[2,2,320,128]{3,2,1,0:T(8,128)(2,1)S(1)}, bf16[2,2,320,128]{3,2,1,0:T(8,128)(2,1)S(1)}, u32[]{:S(2)}, u32[]{:S(2)}) collective-permute-start(bf16[2,2,320,128]{3,2,1,0:T(8,128)(2,1)S(1)} %get-tuple-element.15), channel_id=1, source_target_pairs={{1,32},{2,33},{3,34},{4,35},{5,36},{6,37},{7,38},{8,39},{9,40},{10... | collective-permute-start | bytes 983048 | tf_op jit(solution)/shard_map/ppermute | solution.py:225
  53.3 4.9 %collective-permute-start.4 = (bf16[2,2,320,128]{3,2,1,0:T(8,128)(2,1)S(1)}, bf16[2,2,320,128]{3,2,1,0:T(8,128)(2,1)S(1)}, u32[]{:S(2)}, u32[]{:S(2)}) collective-permute-start(bf16[2,2,320,128]{3,2,1,0:T(8,128)(2,1)S(1)} %get-tuple-element.15), channel_id=1, source_target_pairs={{0,32},{1,33},{2,34},{3,35},{4,36},{5,37},{6,38},{7,39},{8,40},{9,... | collective-permute-start | bytes 983048 | tf_op jit(solution)/shard_map/ppermute | solution.py:225
  58.3 12.0 %all_to_all.20 = f32[32,1,128]{2,1,0:T(1,128)S(1)} all-to-all(f32[32,1,128]{2,1,0:T(1,128)S(1)} %bitcast.29), channel_id=1, replica_groups=mesh['y'=4,'c'=2,'z'=8,'x'=4] {'y','z'}, dimensions={0} | all-to-all | bytes 32768 | tf_op jit(solution)/shard_map/all_to_all | solution.py:237
  70.2 0.3 relay.3
  70.5 9.1 %all_to_all.21 = f32[8,1,128]{2,1,0:T(1,128)S(1)} all-to-all(f32[8,1,128]{2,1,0:T(1,128)S(1)} %bitcast.28), channel_id=1, replica_groups=mesh['y'=4,'c'=2,'z'=8,'x'=4] {'c','x'}, dimensions={0} | all-to-all | bytes 8192 | tf_op jit(solution)/shard_map/all_to_all | solution.py:237
  79.6 0.0 collective-permute-done.5.diagonal_ref
  79.6 0.0 collective-permute-done.4.back_ref
  79.6 0.0 collective-permute-done.3.rows_ref
  79.6 0.0 copy-done.3
  79.6 5.9 %second_conv.1 = bf16[4,2,320,128]{3,2,1,0:T(8,128)(2,1)} custom-call(s32[4]{0:T(128)S(1)} %pad_add_fusion.place_ref, bf16[4,2,320,128]{3,2,1,0:T(8,128)(2,1)S(1)} %get-tuple-element.14.own_ref, bf16[4,2,320,128]{3,2,1,0:T(8,128)(2,1)S(1)} %collective-permute-done.3.rows_ref, bf16[2,2,320,128]{3,2,1,0:T(8,128)(2,1)S(1)} %collective-permute-done.4.back_ref, ...), custom_call_target="tpu_custom_call" | custom-call | tf_op jit(solution)/shard_map/second_conv/pallas_call | solution.py:292
Async XLA Ops:
  0.0 42.3 %collective-permute-start = (bf16[4,2,320,128]{3,2,1,0:T(8,128)(2,1)}, bf16[4,2,320,128]{3,2,1,0:T(8,128)(2,1)S(1)}, u32[]{:S(2)}, u32[]{:S(2)}) collective-permute-start(bf16[4,2,320,128]{3,2,1,0:T(8,128)(2,1)} %features_ref.1), channel_id=1, source_target_pairs={{31,0},{0,1},{1,2},{2,3},{3,4},{4,5},{5,6},{6,7},{7,8},{8,9},{9,10... | collective-permute-start | bytes 1966088 | tf_op jit(solution)/shard_map/ppermute | solution.py:225
  8.6 0.7 copy-start.7
  8.6 0.7 copy-start.8
  8.6 0.7 copy-start.9
  8.6 0.7 copy-start.4
  8.6 0.7 copy-start.5
  8.6 0.7 copy-start.6
  9.3 1.1 %copy-start = (bf16[4,2,320,128]{3,2,1,0:T(8,128)(2,1)S(1)}, bf16[4,2,320,128]{3,2,1,0:T(8,128)(2,1)}, u32[]{:S(2)}) copy-start(bf16[4,2,320,128]{3,2,1,0:T(8,128)(2,1)} %features_ref.1) | copy-start | bytes 1966084
  10.4 31.9 %copy-start.1 = (bf16[4,2,320,128]{3,2,1,0:T(8,128)(2,1)S(1)}, bf16[4,2,320,128]{3,2,1,0:T(8,128)(2,1)}, u32[]{:S(2)}) copy-start(bf16[4,2,320,128]{3,2,1,0:T(8,128)(2,1)} %features_ref.1) | copy-start | bytes 1966084
  11.6 30.7 %collective-permute-start.2 = (bf16[2,2,320,128]{3,2,1,0:T(8,128)(2,1)S(1)}, bf16[2,2,320,128]{3,2,1,0:T(8,128)(2,1)S(1)}, u32[]{:S(2)}, u32[]{:S(2)}) collective-permute-start(bf16[2,2,320,128]{3,2,1,0:T(8,128)(2,1)S(1)} %get-tuple-element.11), channel_id=1, source_target_pairs={{1,32},{2,33},{3,34},{4,35},{5,36},{6,37},{7,38},{8,39},{9,40},{10... | collective-permute-start | bytes 983048 | tf_op jit(solution)/shard_map/ppermute | solution.py:225
  13.5 28.8 %collective-permute-start.1 = (bf16[2,2,320,128]{3,2,1,0:T(8,128)(2,1)S(1)}, bf16[2,2,320,128]{3,2,1,0:T(8,128)(2,1)S(1)}, u32[]{:S(2)}, u32[]{:S(2)}) collective-permute-start(bf16[2,2,320,128]{3,2,1,0:T(8,128)(2,1)S(1)} %get-tuple-element.11), channel_id=1, source_target_pairs={{0,32},{1,33},{2,34},{3,35},{4,36},{5,37},{6,38},{7,39},{8,40},{9,... | collective-permute-start | bytes 983048 | tf_op jit(solution)/shard_map/ppermute | solution.py:225
  17.5 14.2 %all-to-all-start = ((f32[32,1,128]{2,1,0:T(1,128)}), f32[32,1,128]{2,1,0:T(1,128)S(1)}, u32[]{:S(2)}, u32[]{:S(2)}) async-start(f32[32,1,128]{2,1,0:T(1,128)} %bitcast.10), calls=%async_computation | async-start | bytes 32768 | tf_op jit(solution)/shard_map/all_to_all | solution.py:237
  32.7 9.6 %all-to-all-start.1 = ((f32[8,1,128]{2,1,0:T(1,128)}), f32[8,1,128]{2,1,0:T(1,128)S(1)}, u32[]{:S(2)}, u32[]{:S(2)}) async-start(f32[8,1,128]{2,1,0:T(1,128)} %bitcast.13), calls=%async_computation.1 | async-start | bytes 8192 | tf_op jit(solution)/shard_map/all_to_all | solution.py:237
  42.3 1.2 %copy-start.2 = (bf16[3456,128]{1,0:T(8,128)(2,1)S(1)}, bf16[3456,128]{1,0:T(8,128)(2,1)}, u32[]{:S(2)}) copy-start(bf16[3456,128]{1,0:T(8,128)(2,1)} %w_ref.2) | copy-start | bytes 2654212
  43.5 36.1 %copy-start.3 = (bf16[3456,128]{1,0:T(8,128)(2,1)S(1)}, bf16[3456,128]{1,0:T(8,128)(2,1)}, u32[]{:S(2)}) copy-start(bf16[3456,128]{1,0:T(8,128)(2,1)} %w_ref.3) | copy-start | bytes 2654212
  49.1 30.6 %collective-permute-start.3 = (bf16[4,2,320,128]{3,2,1,0:T(8,128)(2,1)S(1)}, bf16[4,2,320,128]{3,2,1,0:T(8,128)(2,1)S(1)}, u32[]{:S(2)}, u32[]{:S(2)}) collective-permute-start(bf16[4,2,320,128]{3,2,1,0:T(8,128)(2,1)S(1)} %get-tuple-element.14.own_ref), channel_id=1, source_target_pairs={{1,0},{2,1},{3,2},{4,3},{5,4},{6,5},{7,6},{8,7},{9,8},{10,9},{11,1... | collective-permute-start | bytes 1966088 | tf_op jit(solution)/shard_map/ppermute | solution.py:225
  49.4 30.2 %collective-permute-start.5 = (bf16[2,2,320,128]{3,2,1,0:T(8,128)(2,1)S(1)}, bf16[2,2,320,128]{3,2,1,0:T(8,128)(2,1)S(1)}, u32[]{:S(2)}, u32[]{:S(2)}) collective-permute-start(bf16[2,2,320,128]{3,2,1,0:T(8,128)(2,1)S(1)} %get-tuple-element.15), channel_id=1, source_target_pairs={{1,32},{2,33},{3,34},{4,35},{5,36},{6,37},{7,38},{8,39},{9,40},{10... | collective-permute-start | bytes 983048 | tf_op jit(solution)/shard_map/ppermute | solution.py:225
  53.3 26.3 %collective-permute-start.4 = (bf16[2,2,320,128]{3,2,1,0:T(8,128)(2,1)S(1)}, bf16[2,2,320,128]{3,2,1,0:T(8,128)(2,1)S(1)}, u32[]{:S(2)}, u32[]{:S(2)}) collective-permute-start(bf16[2,2,320,128]{3,2,1,0:T(8,128)(2,1)S(1)} %get-tuple-element.15), channel_id=1, source_target_pairs={{0,32},{1,33},{2,34},{3,35},{4,36},{5,37},{6,38},{7,39},{8,40},{9,... | collective-permute-start | bytes 983048 | tf_op jit(solution)/shard_map/ppermute | solution.py:225

commit v6 on v5

v6 whole, which is shorter than its diff:
```python
import functools

import jax
import jax.numpy as jnp
from jax import lax
from jax.experimental import pallas as pl
from jax.experimental.pallas import tpu as pltpu
from jax.sharding import Mesh
from jax.sharding import PartitionSpec as P

C = 128
GROUP = 4
TM = ("y", "c")
ROWS = ("z", "x")
EVERY = TM + ROWS
FAR = ("y", "z")
NEAR = ("c", "x")
EPS = 1e-06
MIB = 1 << 20
VMEM = pl.BlockSpec(memory_space=pltpu.VMEM)
HBM = pl.BlockSpec(memory_space=pltpu.HBM)


def group_total(v):
    lane = lax.broadcasted_iota(jnp.int32, v.shape, v.ndim - 1)
    for step in (1, 2):
        ahead = pltpu.roll(v, C - step, v.ndim - 1)
        behind = pltpu.roll(v, step, v.ndim - 1)
        v = v + jnp.where((lane & step) == 0, ahead, behind)
    return v


def lane_place(shape):
    return lax.broadcasted_iota(jnp.int32, shape, len(shape) - 1) % GROUP


def packed(first, centered):
    place = lane_place(first.shape)
    return jnp.where(place == 0, first, jnp.where(place == 1, centered, 0.0))


def column_total(rows):
    total = jnp.sum(rows.reshape(rows.shape[0] // 8, 8, C), axis=0)
    return jnp.broadcast_to(jnp.sum(total, axis=0, keepdims=True), (8, C))


def merged(every, cells):
    count = every.shape[0]
    total = column_total(every)
    place = lane_place(total.shape)
    first = group_total(jnp.where(place == 0, total, 0.0))
    apart = every / cells - first[:1] / (cells * count)
    between = column_total(apart * apart) * cells
    centered = group_total(jnp.where(place == 0, between, jnp.where(place == 1, total, 0.0)))
    return first, centered


def scale_and_offset(sums_ref, vectors_ref, which, tile_cells, devices):
    count = sums_ref.shape[0]
    cells = tile_cells * GROUP * devices
    first, centered = merged(sums_ref[...], cells // count)
    average, spread = first[:1] / cells, centered[:1] / cells
    scale = lax.rsqrt(spread + EPS) * vectors_ref[which : which + 1]
    offset = vectors_ref[which + 1 : which + 2] - average * scale
    return 0.5 * scale, 0.5 * offset


def activated(values, scale, offset):
    half = values.astype(jnp.float32) * scale + offset
    return (half + half * jnp.tanh(half)).astype(jnp.bfloat16)


def taps(act_ref, w_ref, f, wraps):
    width = act_ref.shape[2]
    column = lax.broadcasted_iota(jnp.int32, (width, C), 0)

    def left(rows, unused):
        pieces = []
        for i in range(3):
            for r in rows:
                piece = act_ref[f + i, r]
                if wraps is not None and r == unused:
                    piece = jnp.where(wraps, jnp.zeros_like(piece), piece)
                pieces.append(piece)
        return jnp.concatenate(pieces, axis=1)

    def block(i, j, k):
        if not 0 <= j < 3:
            return jnp.zeros((C, C), jnp.bfloat16)
        first = ((i * 3 + j) * 3 + k) * C
        return w_ref[first : first + C, :]

    def pair(i, r, out, k):
        found = block(i, r - out, k)
        if wraps is not None and 0 <= r - out < 3 and r // 2 != out:
            found = jnp.where(wraps, jnp.zeros_like(found), found)
        return found

    early = jnp.concatenate(
        [jnp.concatenate([block(i, j, 0), block(i, j, 1)], axis=1) for i in range(3) for j in range(3)],
        axis=0,
    )
    late = jnp.concatenate(
        [jnp.concatenate([pair(i, r, 0, 2), pair(i, r, 1, 2)], axis=1) for i in range(3) for r in range(4)],
        axis=0,
    )
    ends = jnp.dot(left(range(4), None), late, preferred_element_type=jnp.float32)
    totals = []
    for out in range(2):
        part = jnp.dot(left(range(out, out + 3), 2 - out), early, preferred_element_type=jnp.float32)
        before = jnp.where(column == 0, 0.0, pltpu.roll(part[:, :C], 1, 0))
        after = ends[:, out * C : (out + 1) * C]
        after = jnp.where(column == width - 1, 0.0, pltpu.roll(after, width - 1, 0))
        totals.append(before + part[:, C:] + after)
    return totals


def conv(sources, act_ref, w_ref, wraps, emit):
    earlier = 2
    frames, rows = act_ref.shape[0], act_ref.shape[1]

    def fill(f):
        for r in range(rows):
            act_ref[f, r] = sources(f, r)

    for f in range(earlier):
        fill(f)
    for f in range(frames - earlier):
        fill(f + earlier)
        emit(f, taps(act_ref, w_ref, f, wraps))


def source_of(own_ref, rows_ref, back_ref, diagonal_ref, own_low, back_low, tm, scale, offset, hides):
    earlier = back_ref.shape[0]

    def pick(low, one, other, r):
        return jnp.where(low if r < 2 else jnp.logical_not(low), one, other)

    def sources(f, r):
        here = max(f - earlier, 0)
        value = pick(own_low, own_ref[here, r % 2], rows_ref[here, r % 2], r)
        if f < earlier:
            past = pick(back_low, back_ref[f, r % 2], diagonal_ref[f, r % 2], r)
            value = jnp.where(tm == 0, value, past)
        value = activated(value, scale, offset)
        if r in hides:
            value = jnp.where(hides[r], jnp.zeros_like(value), value)
        return value

    return sources


def moments_kernel(x_hbm, *refs):
    vectors_hbm, (last_ref, sums_ref, vectors_ref, x_ref, x_sems, vector_sems) = refs[:-6], refs[-6:]
    frames, rows, width, _ = x_ref.shape
    earlier = last_ref.shape[0]
    copies = [pltpu.make_async_copy(x_hbm.at[f], x_ref.at[f], x_sems.at[f]) for f in range(frames)]
    small = [
        pltpu.make_async_copy(v, vectors_ref.at[i : i + 1], vector_sems.at[i])
        for i, v in enumerate(vectors_hbm)
    ]
    for copy in copies + small:
        copy.start()
    cells = frames * rows * width * GROUP

    def folded(f, step):
        total = jnp.zeros((8, C), jnp.float32)
        for r in range(rows):
            total = total + step(x_ref[f, r].astype(jnp.float32)).reshape(width // 8, 8, C).sum(axis=0)
        return total

    first = jnp.zeros((8, C), jnp.float32)
    for f in range(frames):
        copies[f].wait()
        first = first + folded(f, lambda v: v)
    first = group_total(column_total(first))
    mean = first[:1] / cells
    centered = jnp.zeros((8, C), jnp.float32)
    for f in range(frames):
        centered = centered + folded(f, lambda v: (v - mean) * (v - mean))
    last_ref[...] = x_ref[frames - earlier :]
    both = packed(first, group_total(column_total(centered)))
    sums_ref[...] = jnp.broadcast_to(both[:1], sums_ref.shape)
    for copy in small:
        copy.wait()


def relay_kernel(cells, sums_ref, next_ref):
    both = packed(*merged(sums_ref[...], cells))
    next_ref[...] = jnp.broadcast_to(both[:1], next_ref.shape)


def first_conv_kernel(
    devices, last_row, own_ref, rows_ref, back_ref, diagonal_ref, sums_ref, vectors_ref, w_ref,
    hidden_ref, last_ref, next_ref, act_ref,
):
    frames, rows, width, _ = own_ref.shape
    earlier = back_ref.shape[0]
    core, tm, row = lax.axis_index("c"), lax.axis_index(TM), lax.axis_index(ROWS)
    scale, offset = scale_and_offset(sums_ref, vectors_ref, 0, frames * rows * width, devices)
    low = core == 1
    sources = source_of(own_ref, rows_ref, back_ref, diagonal_ref, low, low, tm, scale, offset, {})
    held = []

    def folded(values):
        return sum(v.reshape(width // 8, 8, C).sum(axis=0) for v in values)

    def emit(f, totals):
        rounded = [(v + vectors_ref[2:3]).astype(jnp.bfloat16) for v in totals]
        for r, v in enumerate(rounded):
            hidden_ref[f, r] = v
            if f >= frames - earlier:
                last_ref[f - frames + earlier, r] = v
        wide = [v.astype(jnp.float32) for v in rounded]
        if not held:
            held.append(jnp.sum(folded(wide), axis=0, keepdims=True) / (rows * width))
        apart = [v - held[0] for v in wide]
        held.append((folded(apart), folded([v * v for v in apart])))

    conv(sources, act_ref, w_ref, row == core * last_row, emit)
    cells = frames * rows * width
    first = jnp.sum(sum(a for a, _ in held[1:]), axis=0, keepdims=True)
    square = jnp.sum(sum(b for _, b in held[1:]), axis=0, keepdims=True)
    mean = held[0] + first / cells
    shape = (8, C)
    whole = group_total(jnp.broadcast_to(mean * cells, shape))
    apart = mean - whole[:1] / (cells * GROUP)
    centered = square - first * first / cells + cells * apart * apart
    both = packed(whole, group_total(jnp.broadcast_to(centered, shape)))
    next_ref[...] = jnp.broadcast_to(both[:1], next_ref.shape)


def second_conv_kernel(
    devices, last_row, own_ref, rows_ref, back_ref, diagonal_ref, sums_ref, vectors_ref, w_ref,
    features_ref, out_ref, act_ref,
):
    frames, rows, width, _ = own_ref.shape
    core, tm, row = lax.axis_index("c"), lax.axis_index(TM), lax.axis_index(ROWS)
    scale, offset = scale_and_offset(sums_ref, vectors_ref, 3, frames * rows * width, devices)
    hides = {0: row == 0, act_ref.shape[1] - 1: row == last_row}
    sources = source_of(
        own_ref, rows_ref, back_ref, diagonal_ref, core == 0, core == 1, tm, scale, offset, hides
    )

    def emit(f, totals):
        for r, v in enumerate(totals):
            value = v + vectors_ref[5:6] + features_ref[f, r].astype(jnp.float32)
            out_ref[f, r] = value.astype(jnp.bfloat16)

    conv(sources, act_ref, w_ref, None, emit)


def sent(block, tm_step, row_steps):
    tms, rows = lax.axis_size(TM), lax.axis_size(ROWS)
    route = []
    for t in range(tms):
        for r in range(rows):
            source = (t - tm_step, (r + row_steps[t % 2]) % rows)
            if source[0] >= 0:
                route.append((source[0] * rows + source[1], t * rows + r))
    return lax.ppermute(block, EVERY, route)


def neighbours(own, last, row_steps):
    beside = sent(own, 0, row_steps)
    back = sent(last, 1, (0, 0))
    diagonal = sent(last, 1, (-1, 1))
    return beside, back, diagonal


def exchanged(copies, axes):
    count = copies.shape[0]
    received = lax.all_to_all(copies.reshape(count, 1, C), axes, split_axis=0, concat_axis=0, tiled=True)
    return received.reshape(count, C)


def everywhere(copies, tile_cells):
    sums = exchanged(copies, FAR)
    copies = pl.pallas_call(
        functools.partial(relay_kernel, tile_cells * GROUP),
        out_shape=jax.ShapeDtypeStruct((lax.axis_size(NEAR), C), jnp.float32),
        in_specs=[VMEM],
        out_specs=VMEM,
        name="relay",
        cost_estimate=pl.CostEstimate(flops=0, bytes_accessed=1 << 24, transcendentals=0),
        compiler_params=pltpu.CompilerParams(vmem_limit_bytes=4 * MIB),
    )(sums)
    return exchanged(copies, NEAR)


def body(features, gain_one, shift_one, weight_one, bias_one, gain_two, shift_two, weight_two, bias_two):
    frames, rows, width, _ = features.shape
    devices = lax.axis_size(EVERY)
    tile_cells = frames * rows * width
    copies = jax.ShapeDtypeStruct((lax.axis_size(FAR), C), jnp.float32)
    tile = jax.ShapeDtypeStruct(features.shape, jnp.bfloat16)
    two = jax.ShapeDtypeStruct((2, rows, width, C), jnp.bfloat16)
    last_row = lax.axis_size(ROWS) - 1
    common = dict(
        scratch_shapes=[pltpu.VMEM((frames + 2, rows + 2, width, C), jnp.bfloat16)],
        compiler_params=pltpu.CompilerParams(vmem_limit_bytes=10 * MIB),
    )
    specs = [VMEM] * 7
    vectors = [v.reshape(1, C) for v in (gain_one, shift_one, bias_one, gain_two, shift_two, bias_two)]

    last, sums, vectors = pl.pallas_call(
        moments_kernel,
        out_shape=(two, copies, jax.ShapeDtypeStruct((8, C), jnp.float32)),
        in_specs=[HBM] * 7,
        out_specs=(VMEM,) * 3,
        scratch_shapes=[
            pltpu.VMEM(features.shape, jnp.bfloat16),
            pltpu.SemaphoreType.DMA((frames,)),
            pltpu.SemaphoreType.DMA((len(vectors),)),
        ],
        name="moments",
        compiler_params=pltpu.CompilerParams(vmem_limit_bytes=4 * MIB),
    )(features, *vectors)
    around = neighbours(features, last, (-1, 1))
    sums = everywhere(sums, tile_cells)
    hidden, last, sums_two = pl.pallas_call(
        functools.partial(first_conv_kernel, devices, last_row),
        out_shape=(tile, two, copies),
        in_specs=specs,
        out_specs=(VMEM,) * 3,
        name="first_conv",
        **common,
    )(features, *around, sums, vectors, weight_one)

    around = neighbours(hidden, last, (1, -1))
    sums_two = everywhere(sums_two, tile_cells)
    return pl.pallas_call(
        functools.partial(second_conv_kernel, devices, last_row),
        out_shape=tile,
        in_specs=specs + [VMEM],
        out_specs=VMEM,
        name="second_conv",
        **common,
    )(hidden, *around, sums_two, vectors, weight_two, features)


def solution(mesh):
    split = Mesh(mesh.devices.reshape(4, 2, 8, 4), EVERY)
    return jax.shard_map(
        body,
        mesh=split,
        in_specs=(P(TM, ROWS, None, None), P(), P(), P(), P(), P(), P(), P(), P()),
        out_specs=P(TM, ROWS, None, None),
        check_vma=False,
    )
```

time: 86 us -> 82.7 us (0.962)
  blocking collectives: 21 us -> 44.6 us
  waiting for transfers between devices: 13 us -> 0.02 us
  starting transfers between devices: 34.4 us -> 23.7 us
  Pallas kernels: 13.9 us -> 10.8 us
    all_to_all x2 -> x4, blocking collectives: 21 us -> 44.6 us  [exchanged(): lax.all_to_all(copies.reshape(count, 1, C), axes, split_axis=0, concat_ax...]
    all_to_all x2 -> x0, waiting for transfers between devices: 13 us -> none  [exchanged(): lax.all_to_all(copies.reshape(count, 1, C), axes, split_axis=0, concat_ax...]
    all_to_all x2 -> x0, starting transfers between devices: 10.7 us -> none  [exchanged(): lax.all_to_all(copies.reshape(count, 1, C), axes, split_axis=0, concat_ax...]
    pallas_call x2, Pallas kernels: 11.5 us -> 8.66 us  [the longest x1 4.52 us: body(): pl.pallas_call(functools.partial(second_conv_kernel, devices, last_row),...]
  transfers between devices with their start and end apart: 8 -> 6, of which waited for: 2 -> 0; matrix products, arithmetic and copies ran while one was open for 0% -> 0% of each run, Pallas kernels for 3% -> 3%
where the time goes in v6:
time: 82.7 us; the launch traced here: 82.3 us
  blocking collectives  44.6 us (54%)
  starting transfers between devices  23.7 us (29%)
  Pallas kernels  10.8 us (13%)
  local copies, waits for them, and re-layouts  2.97 us (4%)
    all_to_all x4, blocking collectives, exchanged(): lax.all_to_all(copies.reshape(count, 1, C), axes, split_axis=0, concat_ax...  44.6 us
    ppermute x6, starting transfers between devices, sent(): return lax.ppermute(block, EVERY, route)  23.7 us
    pallas_call x1, Pallas kernels, body(): pl.pallas_call(functools.partial(second_conv_kernel, devices, last_row),...  4.52 us
    pallas_call x1, Pallas kernels, body(): pl.pallas_call(functools.partial(first_conv_kernel, devices, last_row), o...  4.14 us
    unnamed x20, local copies, waits for them, and re-layouts  2.97 us
  transfers between devices with their start and end apart: 6, of which 0 were waited for; matrix products, arithmetic and copies ran while one was open for 0% of the time, Pallas kernels for 3%

profile of v6, /device:TPU:1, one launch (start us, length us, event | category | flops | bytes accessed | tf_op | source)
XLA Modules:
  0.0 82.3 jit_solution(1343249440584250113)
XLA Ops:
  0.0 8.6 %collective-permute-start = (bf16[4,2,320,128]{3,2,1,0:T(8,128)(2,1)}, bf16[4,2,320,128]{3,2,1,0:T(8,128)(2,1)S(1)}, u32[]{:S(2)}, u32[]{:S(2)}) collective-permute-start(bf16[4,2,320,128]{3,2,1,0:T(8,128)(2,1)} %features_ref.1), channel_id=1, source_target_pairs={{31,0},{0,1},{1,2},{2,3},{3,4},{4,5},{5,6},{6,7},{7,8},{8,9},{9,10... | collective-permute-start | bytes 1966088 | tf_op jit(solution)/shard_map/ppermute | solution.py:261
  8.6 0.0 copy-start.7
  8.6 0.0 copy-start.8
  8.6 0.0 copy-start.9
  8.6 0.0 copy-start.4
  8.6 0.0 copy-start.5
  8.6 0.0 copy-start.6
  8.6 0.6 copy-done.7
  9.2 0.0 copy-done.8
  9.3 0.0 copy-done.9
  9.3 0.0 copy-done.4
  9.3 0.0 copy-done.5
  9.3 0.0 copy-done.6
  9.3 0.0 copy-start
  9.3 1.1 %copy-done = bf16[4,2,320,128]{3,2,1,0:T(8,128)(2,1)S(1)} copy-done((bf16[4,2,320,128]{3,2,1,0:T(8,128)(2,1)S(1)}, bf16[4,2,320,128]{3,2,1,0:T(8,128)(2,1)}, u32[]{:S(2)}) %copy-start) | copy-done | bytes 655384
  10.4 0.0 copy-start.1
  10.4 1.6 %moments.1 = (bf16[2,2,320,128]{3,2,1,0:T(8,128)(2,1)S(1)}, f32[32,128]{1,0:T(8,128)S(1)}, f32[8,128]{1,0:T(8,128)S(1)}) custom-call(bf16[4,2,320,128]{3,2,1,0:T(8,128)(2,1)S(1)} %copy-done, f32[1,128]{1,0:T(1,128)S(1)} %bitcast.30, f32[1,128]{1,0:T(1,128)S(1)} %bitcast.31, f32[1,128]{1,0:T(1,128)S(1)} %bitcast.32, f32[1,128]{1,0:T(1,128)S(1)} %bitcast.33, ...), custom_call_target="tpu_custom_call" | custom-call | tf_op jit(solution)/shard_map/moments/pallas_call | solution.py:306
  12.0 1.9 %collective-permute-start.2 = (bf16[2,2,320,128]{3,2,1,0:T(8,128)(2,1)S(1)}, bf16[2,2,320,128]{3,2,1,0:T(8,128)(2,1)S(1)}, u32[]{:S(2)}, u32[]{:S(2)}) collective-permute-start(bf16[2,2,320,128]{3,2,1,0:T(8,128)(2,1)S(1)} %get-tuple-element.11), channel_id=1, source_target_pairs={{1,32},{2,33},{3,34},{4,35},{5,36},{6,37},{7,38},{8,39},{9,40},{10... | collective-permute-start | bytes 983048 | tf_op jit(solution)/shard_map/ppermute | solution.py:261
  13.9 4.0 %collective-permute-start.1 = (bf16[2,2,320,128]{3,2,1,0:T(8,128)(2,1)S(1)}, bf16[2,2,320,128]{3,2,1,0:T(8,128)(2,1)S(1)}, u32[]{:S(2)}, u32[]{:S(2)}) collective-permute-start(bf16[2,2,320,128]{3,2,1,0:T(8,128)(2,1)S(1)} %get-tuple-element.11), channel_id=1, source_target_pairs={{0,32},{1,33},{2,34},{3,35},{4,36},{5,37},{6,38},{7,39},{8,40},{9,... | collective-permute-start | bytes 983048 | tf_op jit(solution)/shard_map/ppermute | solution.py:261
  18.0 14.1 %all_to_all.20 = f32[32,1,128]{2,1,0:T(1,128)S(1)} all-to-all(f32[32,1,128]{2,1,0:T(1,128)S(1)} %bitcast.28), channel_id=1, replica_groups=mesh['y'=4,'c'=2,'z'=8,'x'=4] {'y','z'}, dimensions={0} | all-to-all | bytes 32768 | tf_op jit(solution)/shard_map/all_to_all | solution.py:273
  32.0 0.3 relay.2
  32.4 9.5 %all_to_all.21 = f32[8,1,128]{2,1,0:T(1,128)S(1)} all-to-all(f32[8,1,128]{2,1,0:T(1,128)S(1)} %bitcast.25), channel_id=1, replica_groups=mesh['y'=4,'c'=2,'z'=8,'x'=4] {'c','x'}, dimensions={0} | all-to-all | bytes 8192 | tf_op jit(solution)/shard_map/all_to_all | solution.py:273
  41.8 0.0 collective-permute-done.2.diagonal_ref
  41.8 0.0 collective-permute-done.1.back_ref
  41.8 0.0 collective-permute-done.rows_ref
  41.8 0.0 copy-done.1
  41.8 0.0 copy-start.2
  41.9 1.2 %copy-done.2 = bf16[3456,128]{1,0:T(8,128)(2,1)S(1)} copy-done((bf16[3456,128]{1,0:T(8,128)(2,1)S(1)}, bf16[3456,128]{1,0:T(8,128)(2,1)}, u32[]{:S(2)}) %copy-start.2) | copy-done | bytes 884760
  43.0 0.0 copy-start.3
  43.0 4.1 %first_conv.1 = (bf16[4,2,320,128]{3,2,1,0:T(8,128)(2,1)S(1)}, bf16[2,2,320,128]{3,2,1,0:T(8,128)(2,1)S(1)}, f32[32,128]{1,0:T(8,128)S(1)}) custom-call(bf16[4,2,320,128]{3,2,1,0:T(8,128)(2,1)S(1)} %copy-done.1, bf16[4,2,320,128]{3,2,1,0:T(8,128)(2,1)S(1)} %collective-permute-done.rows_ref, bf16[2,2,320,128]{3,2,1,0:T(8,128)(2,1)S(1)} %collective-permute-done.1.back_ref, ...), custom_call_target="tpu_custom_call" | custom-call | tf_op jit(solution)/shard_map/first_conv/pallas_call | solution.py:321
  47.2 0.3 collective-permute-start.3
  47.5 4.0 %collective-permute-start.5 = (bf16[2,2,320,128]{3,2,1,0:T(8,128)(2,1)S(1)}, bf16[2,2,320,128]{3,2,1,0:T(8,128)(2,1)S(1)}, u32[]{:S(2)}, u32[]{:S(2)}) collective-permute-start(bf16[2,2,320,128]{3,2,1,0:T(8,128)(2,1)S(1)} %get-tuple-element.15), channel_id=1, source_target_pairs={{1,32},{2,33},{3,34},{4,35},{5,36},{6,37},{7,38},{8,39},{9,40},{10... | collective-permute-start | bytes 983048 | tf_op jit(solution)/shard_map/ppermute | solution.py:261
  51.4 4.9 %collective-permute-start.4 = (bf16[2,2,320,128]{3,2,1,0:T(8,128)(2,1)S(1)}, bf16[2,2,320,128]{3,2,1,0:T(8,128)(2,1)S(1)}, u32[]{:S(2)}, u32[]{:S(2)}) collective-permute-start(bf16[2,2,320,128]{3,2,1,0:T(8,128)(2,1)S(1)} %get-tuple-element.15), channel_id=1, source_target_pairs={{0,32},{1,33},{2,34},{3,35},{4,36},{5,37},{6,38},{7,39},{8,40},{9,... | collective-permute-start | bytes 983048 | tf_op jit(solution)/shard_map/ppermute | solution.py:261
  56.4 12.0 %all_to_all.22 = f32[32,1,128]{2,1,0:T(1,128)S(1)} all-to-all(f32[32,1,128]{2,1,0:T(1,128)S(1)} %bitcast.27), channel_id=1, replica_groups=mesh['y'=4,'c'=2,'z'=8,'x'=4] {'y','z'}, dimensions={0} | all-to-all | bytes 32768 | tf_op jit(solution)/shard_map/all_to_all | solution.py:273
  68.3 0.3 relay.3
  68.6 9.1 %all_to_all.23 = f32[8,1,128]{2,1,0:T(1,128)S(1)} all-to-all(f32[8,1,128]{2,1,0:T(1,128)S(1)} %bitcast.26), channel_id=1, replica_groups=mesh['y'=4,'c'=2,'z'=8,'x'=4] {'c','x'}, dimensions={0} | all-to-all | bytes 8192 | tf_op jit(solution)/shard_map/all_to_all | solution.py:273
  77.7 0.0 collective-permute-done.5.diagonal_ref
  77.7 0.0 collective-permute-done.4.back_ref
  77.7 0.0 collective-permute-done.3.rows_ref
  77.7 0.0 copy-done.3
  77.7 4.5 %second_conv.1 = bf16[4,2,320,128]{3,2,1,0:T(8,128)(2,1)} custom-call(bf16[4,2,320,128]{3,2,1,0:T(8,128)(2,1)S(1)} %get-tuple-element.14.own_ref, bf16[4,2,320,128]{3,2,1,0:T(8,128)(2,1)S(1)} %collective-permute-done.3.rows_ref, bf16[2,2,320,128]{3,2,1,0:T(8,128)(2,1)S(1)} %collective-permute-done.4.back_ref, ...), custom_call_target="tpu_custom_call" | custom-call | tf_op jit(solution)/shard_map/second_conv/pallas_call | solution.py:332
Async XLA Ops:
  0.0 41.8 %collective-permute-start = (bf16[4,2,320,128]{3,2,1,0:T(8,128)(2,1)}, bf16[4,2,320,128]{3,2,1,0:T(8,128)(2,1)S(1)}, u32[]{:S(2)}, u32[]{:S(2)}) collective-permute-start(bf16[4,2,320,128]{3,2,1,0:T(8,128)(2,1)} %features_ref.1), channel_id=1, source_target_pairs={{31,0},{0,1},{1,2},{2,3},{3,4},{4,5},{5,6},{6,7},{7,8},{8,9},{9,10... | collective-permute-start | bytes 1966088 | tf_op jit(solution)/shard_map/ppermute | solution.py:261
  8.6 0.7 copy-start.7
  8.6 0.7 copy-start.8
  8.6 0.7 copy-start.9
  8.6 0.7 copy-start.4
  8.6 0.7 copy-start.5
  8.6 0.7 copy-start.6
  9.3 1.1 %copy-start = (bf16[4,2,320,128]{3,2,1,0:T(8,128)(2,1)S(1)}, bf16[4,2,320,128]{3,2,1,0:T(8,128)(2,1)}, u32[]{:S(2)}) copy-start(bf16[4,2,320,128]{3,2,1,0:T(8,128)(2,1)} %features_ref.1) | copy-start | bytes 1966084
  10.4 31.4 %copy-start.1 = (bf16[4,2,320,128]{3,2,1,0:T(8,128)(2,1)S(1)}, bf16[4,2,320,128]{3,2,1,0:T(8,128)(2,1)}, u32[]{:S(2)}) copy-start(bf16[4,2,320,128]{3,2,1,0:T(8,128)(2,1)} %features_ref.1) | copy-start | bytes 1966084
  12.0 29.8 %collective-permute-start.2 = (bf16[2,2,320,128]{3,2,1,0:T(8,128)(2,1)S(1)}, bf16[2,2,320,128]{3,2,1,0:T(8,128)(2,1)S(1)}, u32[]{:S(2)}, u32[]{:S(2)}) collective-permute-start(bf16[2,2,320,128]{3,2,1,0:T(8,128)(2,1)S(1)} %get-tuple-element.11), channel_id=1, source_target_pairs={{1,32},{2,33},{3,34},{4,35},{5,36},{6,37},{7,38},{8,39},{9,40},{10... | collective-permute-start | bytes 983048 | tf_op jit(solution)/shard_map/ppermute | solution.py:261
  13.9 27.9 %collective-permute-start.1 = (bf16[2,2,320,128]{3,2,1,0:T(8,128)(2,1)S(1)}, bf16[2,2,320,128]{3,2,1,0:T(8,128)(2,1)S(1)}, u32[]{:S(2)}, u32[]{:S(2)}) collective-permute-start(bf16[2,2,320,128]{3,2,1,0:T(8,128)(2,1)S(1)} %get-tuple-element.11), channel_id=1, source_target_pairs={{0,32},{1,33},{2,34},{3,35},{4,36},{5,37},{6,38},{7,39},{8,40},{9,... | collective-permute-start | bytes 983048 | tf_op jit(solution)/shard_map/ppermute | solution.py:261
  41.8 1.2 %copy-start.2 = (bf16[3456,128]{1,0:T(8,128)(2,1)S(1)}, bf16[3456,128]{1,0:T(8,128)(2,1)}, u32[]{:S(2)}) copy-start(bf16[3456,128]{1,0:T(8,128)(2,1)} %w_ref.2) | copy-start | bytes 2654212
  43.0 34.7 %copy-start.3 = (bf16[3456,128]{1,0:T(8,128)(2,1)S(1)}, bf16[3456,128]{1,0:T(8,128)(2,1)}, u32[]{:S(2)}) copy-start(bf16[3456,128]{1,0:T(8,128)(2,1)} %w_ref.3) | copy-start | bytes 2654212
  47.2 30.6 %collective-permute-start.3 = (bf16[4,2,320,128]{3,2,1,0:T(8,128)(2,1)S(1)}, bf16[4,2,320,128]{3,2,1,0:T(8,128)(2,1)S(1)}, u32[]{:S(2)}, u32[]{:S(2)}) collective-permute-start(bf16[4,2,320,128]{3,2,1,0:T(8,128)(2,1)S(1)} %get-tuple-element.14.own_ref), channel_id=1, source_target_pairs={{1,0},{2,1},{3,2},{4,3},{5,4},{6,5},{7,6},{8,7},{9,8},{10,9},{11,1... | collective-permute-start | bytes 1966088 | tf_op jit(solution)/shard_map/ppermute | solution.py:261
  47.5 30.2 %collective-permute-start.5 = (bf16[2,2,320,128]{3,2,1,0:T(8,128)(2,1)S(1)}, bf16[2,2,320,128]{3,2,1,0:T(8,128)(2,1)S(1)}, u32[]{:S(2)}, u32[]{:S(2)}) collective-permute-start(bf16[2,2,320,128]{3,2,1,0:T(8,128)(2,1)S(1)} %get-tuple-element.15), channel_id=1, source_target_pairs={{1,32},{2,33},{3,34},{4,35},{5,36},{6,37},{7,38},{8,39},{9,40},{10... | collective-permute-start | bytes 983048 | tf_op jit(solution)/shard_map/ppermute | solution.py:261
  51.4 26.3 %collective-permute-start.4 = (bf16[2,2,320,128]{3,2,1,0:T(8,128)(2,1)S(1)}, bf16[2,2,320,128]{3,2,1,0:T(8,128)(2,1)S(1)}, u32[]{:S(2)}, u32[]{:S(2)}) collective-permute-start(bf16[2,2,320,128]{3,2,1,0:T(8,128)(2,1)S(1)} %get-tuple-element.15), channel_id=1, source_target_pairs={{0,32},{1,33},{2,34},{3,35},{4,36},{5,37},{6,38},{7,39},{8,40},{9,... | collective-permute-start | bytes 983048 | tf_op jit(solution)/shard_map/ppermute | solution.py:261
